TPU v7x, 512 devices: a whole 4x4x16 slice. The times are simulated.
512 devices in a mesh: segment: 16 (over z_lo, x), dp: 8 (over y, core), mp: 4 (over z_hi).
Axes of the slice: x: 4, y: 4, z: 16 (z_hi: 4, z_lo: 4; z = z_hi * 4 + z_lo), core: 2. Of those that a mesh axis runs over, the one named last changes fastest.
Arguments:
- encoder_image_states: bfloat16 [8, 128, 8192], P('dp', 'segment'), may hold values from -6 to 6
- frozen_key_value: bfloat16 [16, 8192, 2, 1024], P('segment', 'dp', None, 'mp'), may hold values from -0.0625 to 0.0625
- adapter_down_weight: bfloat16 [16, 8192, 128], P('segment', 'mp'), may hold values from -0.0625 to 0.0625
- adapter_up_weight: bfloat16 [16, 2, 64, 1024], P('segment', None, None, 'mp'), may hold values from -0.75 to 0.75
- queries: bfloat16 [16, 8, 128, 8192], P('segment', 'dp', None, 'mp'), may hold values from -9 to 9
- cotangent: bfloat16 [16, 8, 128, 8192], P('segment', 'dp', None, 'mp'), may hold values from -1.5 to 1.5
- text_token_length: int32 [8], P('dp'), may hold values from 32 to 128
- image_tile_count: int32 [8], P('dp'), may hold values from 1 to 4
Outputs:
- grad_down: bfloat16 [16, 8192, 128], P('segment', 'mp')
- up_gradient: bfloat16 [16, 2, 64, 1024], P('segment', None, None, 'mp')
- grad_image: float32 [8, 128, 8192], P('dp', 'segment')
All inputs are finite; a program needn't handle non-finite values.
Results may differ from a plain program's by a relative error of at most 0.017.
The roundings to bfloat16 on the way count: a program that leaves them out, or rounds other values in their place, can miss the bound.
Values may be sent and summed in bfloat16 or wider, within the bound.
No kernel may reach another device: no remote copies, remote signals or barrier semaphores. Data moves between devices by JAX's collectives and lax.ppermute only.
A program may use at most 64 MiB of HBM per device.

v0:
```python
import jax
import jax.numpy as jnp
from jax import lax
from jax.sharding import PartitionSpec as P

HD = 128
TILES = 4


adapter_scale = 2.0
contract_rows = (((0,), (0,)), ((), ()))
contracted_columns = (((1,), (1,)), ((), ()))


def body(
    encoder_image_states,
    frozen_key_value,
    adapter_down_weight,
    adapter_up_weight,
    queries,
    cotangent,
    text_token_length,
    image_tile_count,
):
    samples = encoder_image_states.shape[0]
    model_width = encoder_image_states.shape[2]
    whole_img = lax.all_gather(encoder_image_states, "segment", axis=1, tiled=True)
    image_rows = whole_img.shape[1]
    flat_rows = samples * image_rows
    flat_img = whole_img.reshape(flat_rows, model_width)
    fourth_part = adapter_down_weight.shape[1]
    parallel_index = lax.axis_index("mp")
    image_fourth = lax.dynamic_slice_in_dim(flat_img, parallel_index * fourth_part, fourth_part, 1)
    lowrank_state = adapter_up_weight.shape[2]
    key_value_columns = adapter_up_weight.shape[3]
    lowrank_projection = lax.psum(
        jnp.dot(image_fourth, adapter_down_weight[0], preferred_element_type=jnp.float32), "mp"
    ).astype(jnp.bfloat16)
    adapted_weight = jnp.concatenate(
        [
            jnp.dot(
                lowrank_projection[:, :lowrank_state],
                adapter_up_weight[0, 0],
                preferred_element_type=jnp.float32,
            ),
            jnp.dot(
                lowrank_projection[:, lowrank_state:],
                adapter_up_weight[0, 1],
                preferred_element_type=jnp.float32,
            ),
        ],
        axis=1,
    )
    local_weight = frozen_key_value[0]
    full_weight = lax.all_gather(local_weight, "dp", axis=0, tiled=True).reshape(
        model_width, 2 * key_value_columns
    )
    frozen_output = jnp.dot(flat_img, full_weight, preferred_element_type=jnp.float32)
    key_value_pair = (frozen_output + adapter_scale * adapted_weight).astype(jnp.bfloat16)
    local_heads = queries.shape[3] // HD
    local_kv = key_value_columns // HD
    group_size = local_heads // local_kv
    text_rows = queries.shape[2]
    query_rows = queries[0].reshape(samples, text_rows, local_kv, group_size, HD)
    cot_rows = cotangent[0].reshape(samples, text_rows, local_kv, group_size, HD)
    key_rows = key_value_pair[:, :key_value_columns].reshape(samples, image_rows, local_kv, HD)
    value_rows = key_value_pair[:, key_value_columns:].reshape(samples, image_rows, local_kv, HD)
    key_mask = jnp.arange(image_rows, dtype=jnp.int32)[None, :] < image_tile_count[:, None] * (
        image_rows // TILES
    )
    row_mask = (
        jnp.arange(text_rows, dtype=jnp.int32)[None, :] < text_token_length[:, None]
    ).astype(jnp.float32)
    scores = jnp.einsum(
        "btgrd,bjgd->bgrtj", query_rows, key_rows, preferred_element_type=jnp.float32
    ) * HD ** (-0.5)
    masked = jnp.where(key_mask[:, None, None, None, :], scores, -1e30)
    row_top = jnp.max(masked, axis=-1, keepdims=True)
    shifted = jnp.exp(masked - row_top)
    attention = shifted / jnp.sum(shifted, axis=-1, keepdims=True)
    row_gate = row_mask[:, None, None, :, None]
    kept = attention.astype(jnp.bfloat16) * row_gate.astype(jnp.bfloat16)
    dweights = jnp.einsum(
        "btgrd,bjgd->bgrtj", cot_rows, value_rows, preferred_element_type=jnp.float32
    )
    row_delta = jnp.sum(attention * dweights, axis=-1, keepdims=True)
    dscore = (attention * (dweights - row_delta) * row_gate * HD ** (-0.5)).astype(jnp.bfloat16)
    key_grad = jnp.einsum(
        "bgrtj,btgrd->bjgd", dscore, query_rows, preferred_element_type=jnp.float32
    )
    value_grad = jnp.einsum("bgrtj,btgrd->bjgd", kept, cot_rows, preferred_element_type=jnp.float32)
    kv_grad = jnp.concatenate(
        [
            key_grad.reshape(flat_rows, key_value_columns),
            value_grad.reshape(flat_rows, key_value_columns),
        ],
        axis=1,
    ).astype(jnp.bfloat16)
    backward_piece = adapter_scale * jnp.concatenate(
        [
            lax.dot_general(
                kv_grad[:, :key_value_columns],
                adapter_up_weight[0, 0],
                contracted_columns,
                preferred_element_type=jnp.float32,
            ),
            lax.dot_general(
                kv_grad[:, key_value_columns:],
                adapter_up_weight[0, 1],
                contracted_columns,
                preferred_element_type=jnp.float32,
            ),
        ],
        axis=1,
    )
    backward_lowrank = lax.psum(backward_piece, "mp").astype(jnp.bfloat16)
    up_gradient = adapter_scale * jnp.stack(
        [
            lax.dot_general(
                lowrank_projection[:, :lowrank_state],
                kv_grad[:, :key_value_columns],
                contract_rows,
                preferred_element_type=jnp.float32,
            ),
            lax.dot_general(
                lowrank_projection[:, lowrank_state:],
                kv_grad[:, key_value_columns:],
                contract_rows,
                preferred_element_type=jnp.float32,
            ),
        ]
    )
    grad_down = lax.dot_general(
        image_fourth, backward_lowrank, contract_rows, preferred_element_type=jnp.float32
    )
    down_sum, up_sum = lax.psum((grad_down, up_gradient), "dp")
    image_gradient_total = lax.dot_general(
        kv_grad, full_weight, contracted_columns, preferred_element_type=jnp.float32
    )
    adapter_portion = lax.dot_general(
        backward_lowrank,
        adapter_down_weight[0],
        contracted_columns,
        preferred_element_type=jnp.float32,
    )
    current_layer = lax.dynamic_slice_in_dim(
        image_gradient_total, parallel_index * fourth_part, fourth_part, 1
    )
    image_gradient_total = lax.dynamic_update_slice_in_dim(
        image_gradient_total, current_layer + adapter_portion, parallel_index * fourth_part, 1
    )
    image_gradient_total = image_gradient_total.reshape(samples, image_rows, model_width)
    shared_sum = lax.psum_scatter(image_gradient_total, "segment", scatter_dimension=1, tiled=True)
    result = lax.psum(shared_sum, "mp")
    return (down_sum.astype(jnp.bfloat16)[None], up_sum.astype(jnp.bfloat16)[None], result)


def solution(mesh):
    in_specs = (
        P("dp", "segment", None),
        P("segment", "dp", None, "mp"),
        P("segment", "mp", None),
        P("segment", None, None, "mp"),
        P("segment", "dp", None, "mp"),
        P("segment", "dp", None, "mp"),
        P("dp"),
        P("dp"),
    )
    out_specs = (P("segment", "mp", None), P("segment", None, None, "mp"), P("dp", "segment", None))
    return jax.shard_map(body, mesh=mesh, in_specs=in_specs, out_specs=out_specs, check_vma=False)
```

profile of v0, /device:TPU:1, one launch (start us, length us, event | category | flops | bytes accessed | tf_op | source)
XLA Modules:
  0.0 389.8 jit_solution(4577795114373816345)
XLA Ops:
  7.2 0.7 all-gather.4.cloned.1.call-update
  8.0 0.7 all-gather.6.cloned.1.call-update
  10.0 1.3 copy.38
  11.3 2.0 copy.39
  13.4 79.7 %all-gather.4.cloned.1.call-done = bf16[1,128,8192]{2,1,0:T(8,128)(2,1)} async-done(((bf16[1,8,8192]{2,1,0:T(8,128)(2,1)}), bf16[1,128,8192]{2,1,0:T(8,128)(2,1)}) %all-gather.4.cloned.1.call-update) | async-done | bytes 2097168 | tf_op jit(solution)/shard_map/all_gather | solution.py:27
  93.1 1.3 fusion.21
  94.5 22.6 %psum.35 = bf16[128,128]{1,0:T(8,128)(2,1)S(1)} all-reduce(f32[128,128]{1,0:T(8,128)S(1)} %fusion.21), channel_id=1, replica_groups=mesh['segment'=16,'dp'=8,'mp'=4] {'mp'}, use_global_device_ids=true, to_apply=%region_0.0 | all-reduce | flops 16384 | bytes 98304 | tf_op jit(solution)/shard_map/psum | solution.py:36
  117.1 0.2 fusion.42
  117.3 0.1 fusion.46
  117.4 44.3 %all-gather.6.cloned.1.call-done = bf16[1,8192,2,256]{3,2,0,1:T(2,128)(2,1)} async-done(((bf16[1,1024,2,256]{3,2,0,1:T(2,128)(2,1)}), bf16[1,8192,2,256]{3,2,0,1:T(2,128)(2,1)}) %all-gather.6.cloned.1.call-update) | async-done | bytes 8388624 | tf_op jit(solution)/shard_map/all_gather | solution.py:55
  161.7 8.2 %copy.40 = bf16[1024,8,2,256]{3,1,2,0:T(8,128)(2,1)} copy(bf16[1024,8,2,256]{3,2,1,0:T(2,128)(2,1)} %bitcast.113) | data formatting | bytes 16777216
  169.9 4.6 %fusion.10 = bf16[128,512]{1,0:T(8,128)(2,1)S(1)} fusion(bf16[8192,512]{1,0:T(8,128)(2,1)} %bitcast.108, bf16[1,128,8192]{2,1,0:T(8,128)(2,1)S(1)} %copy-done.1, f32[128,256]{1,0:T(8,128)S(1)} %fusion.42, f32[128,256]{1,0:T(8,128)S(1)} %fusion.46), kind=kOutput, calls=%fused_computation.11 | convolution fusion | flops 1074003968 | bytes 10878976 | tf_op jit(solution)/shard_map/dot_general | solution.py:58
  174.6 0.3 fusion.66
  174.9 0.2 fusion.16
  175.1 1.6 fusion.14
  176.7 0.1 fusion.40
  176.8 0.3 multiply_reduce_fusion
  177.2 0.5 fusion.13
  177.7 1.5 slice-done.1
  179.2 4.8 %fusion.34 = f32[128,8192]{1,0:T(8,128)} fusion(bf16[8192,512]{1,0:T(8,128)(2,1)S(1)} %bitcast.111, bf16[128,256]{0,1:T(8,128)(2,1)S(1)} %bitcast.118, bf16[128,256]{0,1:T(8,128)(2,1)S(1)} %bitcast.120), kind=kOutput, calls=%fused_computation.42 | convolution fusion | flops 1074003968 | bytes 12713984 | tf_op jit(solution)/shard_map/dot_general | solution.py:137
  183.9 0.1 fusion.44
  184.1 23.9 %psum.36 = bf16[128,128]{0,1:T(8,128)(2,1)S(1)} all-reduce(f32[128,128]{0,1:T(8,128)S(1)} %maximum_multiply_fusion.2), channel_id=1, replica_groups=mesh['segment'=16,'dp'=8,'mp'=4] {'mp'}, use_global_device_ids=true, to_apply=%region_4.5 | all-reduce | flops 16384 | bytes 98304 | tf_op jit(solution)/shard_map/psum | solution.py:116
  208.0 4.6 %copy.51 = f32[1,128,8192]{2,1,0:T(8,128)} copy(f32[1,128,8192]{2,1,0:T(8,128)} %bitcast.112) | data formatting | bytes 8388608
  212.6 2.5 fusion.1
  215.1 0.0 all-reduce.4.cloned.1.call-start
  215.1 1.3 fusion.23
  216.5 0.2 convolution_bitcast_fusion.3
  216.7 0.2 convolution_bitcast_fusion.4
  216.9 85.8 %reduce-scatter.2.cloned.1.call-done = f32[1,8,8192]{2,1,0:T(8,128)} async-done(((f32[1,128,8192]{2,1,0:T(8,128)}), f32[1,8,8192]{2,1,0:T(8,128)}) %reduce-scatter.2.cloned.1.call-update) | async-done | bytes 262160 | tf_op jit(solution)/shard_map/reduce_scatter | solution.py:153
  302.7 61.6 %all-reduce.5 = (bf16[2048,128]{1,0:T(8,128)(2,1)}, bf16[2,64,256]{2,1,0:T(8,128)(2,1)}) all-reduce(f32[2048,128]{1,0:T(8,128)} %fusion.23, f32[2,64,256]{2,1,0:T(8,128)S(1)} %maximum_multiply_fusion.1), channel_id=1, replica_groups=mesh['segment'=16,'dp'=8,'mp'=4] {'dp'}, use_global_device_ids=true, to_apply=%region_5.6 | all-reduce | flops 294912 | bytes 1769472 | tf_op jit(solution)/shard_map/psum | solution.py:136
  364.3 17.3 %all-reduce.4.cloned.1.call-done = f32[1,8,8192]{2,1,0:T(8,128)} async-done(((f32[1,8,8192]{2,1,0:T(8,128)}), f32[1,8,8192]{2,1,0:T(8,128)}) %all-reduce.4.cloned.1.call-update) | async-done | bytes 262160 | tf_op jit(solution)/shard_map/psum | solution.py:154
  381.6 1.7 copy.57
  (24 shorter events, 0.3 us)
Async XLA Ops:
  7.2 86.0 %copy-start = (bf16[1,2048,128]{2,1,0:T(8,128)(2,1)S(1)}, bf16[1,2048,128]{2,1,0:T(8,128)(2,1)}, u32[]{:S(2)}) copy-start(bf16[1,2048,128]{2,1,0:T(8,128)(2,1)} %param.10) | copy-start | bytes 1572868
  7.2 109.9 %copy-start.3 = (bf16[1,2,64,256]{3,2,1,0:T(8,128)(2,1)S(1)}, bf16[1,2,64,256]{3,2,1,0:T(8,128)(2,1)}, u32[]{:S(2)}) copy-start(bf16[1,2,64,256]{3,2,1,0:T(8,128)(2,1)} %param.11) | copy-start | bytes 196612
  7.2 85.9 %all-gather.4.cloned.1.call-start = ((), (), s32[]{:S(2)}) async-start(), calls=%async_computation.1 | async-start | bytes 2228224 | tf_op jit(solution)/shard_map/all_gather | solution.py:27
  7.9 153.8 %all-gather.6.cloned.1.call-start = ((), (), s32[]{:S(2)}) async-start(), calls=%async_computation.4 | async-start | bytes 9437184 | tf_op jit(solution)/shard_map/all_gather | solution.py:55
  8.7 294.0 %reduce-scatter.2.cloned.1.call-start = ((), (), s32[]{:S(2)}) async-start(), calls=%async_computation.2 | async-start | bytes 4456448 | tf_op jit(solution)/shard_map/reduce_scatter | solution.py:153
  161.7 8.2 %copy-start.1 = (bf16[1,128,8192]{2,1,0:T(8,128)(2,1)S(1)}, bf16[1,128,8192]{2,1,0:T(8,128)(2,1)}, u32[]{:S(2)}) copy-start(bf16[1,128,8192]{2,1,0:T(8,128)(2,1)} %all-gather.4.cloned.1.call-done) | copy-start | bytes 6291460
  174.6 2.2 copy-start.2
  175.1 2.6 slice-start
  176.8 2.4 slice-start.1
  215.1 166.5 %all-reduce.4.cloned.1.call-start = ((), (), s32[]{:S(2)}) async-start(), calls=%async_computation.3 | async-start | bytes 524288 | tf_op jit(solution)/shard_map/psum | solution.py:154
Sparse Core Ops, SparseCore 0:
  10.1 83.0 all-gather.3
  95.3 66.3 all-gather.5
  215.2 87.4 reduce-scatter.1
  305.4 76.1 all-reduce.3
where the time goes:
time: 391 us; the launch traced here: 390 us
  waiting for transfers between devices  228 us (58%)
  blocking collectives  108 us (28%)
  local copies, waits for them, and re-layouts  19.3 us (5%)
  matrix products  18.3 us (5%)
  between operations  15.2 us (4%)
    reduce_scatter x1, waiting for transfers between devices, body(): lax.psum_scatter(image_gradient_total, 'segment', scatter_dimension=1, ti...  85.8 us
    all_gather x1, waiting for transfers between devices, body(): lax.all_gather(encoder_image_states, 'segment', axis=1, tiled=True)  79.7 us
    psum x1, blocking collectives, body(): down_sum, up_sum = lax.psum((grad_down, up_gradient), 'dp')  61.6 us
    all_gather x1, waiting for transfers between devices, body(): lax.all_gather(local_weight, 'dp', axis=0, tiled=True)  44.3 us
    psum x1, blocking collectives, body(): backward_lowrank = lax.psum(backward_piece, 'mp').astype(jnp.bfloat16)  23.9 us
    psum x1, blocking collectives, body(): lax.psum(jnp.dot(image_fourth, adapter_down_weight[0], preferred_element_...  22.6 us
    psum x1, waiting for transfers between devices, body(): result = lax.psum(shared_sum, 'mp')  17.3 us
    unnamed x15, local copies, waits for them, and re-layouts  15.9 us
  transfers between devices with their start and end apart: 4, of which 4 were waited for; matrix products, arithmetic and copies ran while one was open for 2% of the time, Pallas kernels for 0%

commit v1 on v0

v1 whole, which is shorter than its diff:
```python
import jax
import jax.numpy as jnp
from jax import lax
from jax.sharding import PartitionSpec as P

HD = 128
TILES = 4
SIDE = 4

adapter_scale = 2.0
contract_rows = (((0,), (0,)), ((), ()))
contracted_columns = (((1,), (1,)), ((), ()))
f32 = jnp.float32
bf16 = jnp.bfloat16
AXES = ("segment", "dp", "mp")


def make_body(mesh):
    segments, parts, heads = (mesh.shape[a] for a in AXES)
    runs = segments // SIDE
    ring = runs * heads

    def shift(v, dx, dz, opposite=False):
        pairs = []
        for s in range(segments):
            for d in range(parts):
                for m in range(heads):
                    z_lo, x = divmod(s, SIDE)
                    sign = -1 if (opposite and d % 2) else 1
                    x2 = (x + sign * dx) % SIDE
                    m2, z2 = divmod((m * runs + z_lo + sign * dz) % ring, runs)
                    pairs.append(((s * parts + d) * heads + m, ((z2 * SIDE + x2) * parts + d) * heads + m2))
        return lax.ppermute(v, AXES, pairs)

    def sum_over_mp(v):
        return jnp.sum(lax.all_gather(v, "mp", axis=0), axis=0)

    def body(
        encoder_image_states,
        frozen_key_value,
        adapter_down_weight,
        adapter_up_weight,
        queries,
        cotangent,
        text_token_length,
        image_tile_count,
    ):
        own = encoder_image_states[0]
        tokens, model_width = own.shape
        parallel_index = lax.axis_index("mp")
        segment_index = lax.axis_index("segment")
        lowrank = adapter_up_weight.shape[2]
        columns = adapter_up_weight.shape[3]
        up_key, up_value = adapter_up_weight[0, 0], adapter_up_weight[0, 1]
        down = adapter_down_weight[0]
        fourth = down.shape[0]

        local_weight = frozen_key_value[0].reshape(-1, 2 * columns)
        weight = lax.all_gather(local_weight, "dp", axis=0, tiled=True)

        line = jnp.concatenate([own, shift(own, 0, -1), shift(own, 0, 2, True), shift(own, 0, 1)], axis=0)
        image = jnp.concatenate([line, shift(line, -1, 0), shift(line, 2, 0, True), shift(line, 1, 0)], axis=0)
        rows = image.shape[0]
        offset = jnp.arange(rows, dtype=jnp.int32)
        x_off, z_off, tok = offset // (runs * tokens), (offset // tokens) % runs, offset % tokens
        position = (
            ((segment_index // SIDE + z_off) % runs) * SIDE + (segment_index % SIDE + x_off) % SIDE
        ) * tokens + tok

        image_fourth = lax.dynamic_slice_in_dim(image, parallel_index * fourth, fourth, 1)
        low = sum_over_mp(jnp.dot(image_fourth, down, preferred_element_type=f32)).astype(bf16)
        adapted = jnp.concatenate(
            [
                jnp.dot(low[:, :lowrank], up_key, preferred_element_type=f32),
                jnp.dot(low[:, lowrank:], up_value, preferred_element_type=f32),
            ],
            axis=1,
        )
        key_value = (jnp.dot(image, weight, preferred_element_type=f32) + adapter_scale * adapted).astype(bf16)

        local_kv = columns // HD
        text_rows = queries.shape[2]
        group = queries.shape[3] // HD // local_kv
        query_rows = queries[0, 0].reshape(text_rows, local_kv, group, HD)
        cot_rows = cotangent[0, 0].reshape(text_rows, local_kv, group, HD)
        key_rows = key_value[:, :columns].reshape(rows, local_kv, HD)
        value_rows = key_value[:, columns:].reshape(rows, local_kv, HD)
        key_mask = position < image_tile_count[0] * (rows // TILES)
        row_mask = (jnp.arange(text_rows, dtype=jnp.int32) < text_token_length[0]).astype(f32)
        scores = jnp.einsum("tgrd,jgd->grtj", query_rows, key_rows, preferred_element_type=f32) * HD ** (-0.5)
        masked = jnp.where(key_mask[None, None, None, :], scores, -1e30)
        row_top = jnp.max(masked, axis=-1, keepdims=True)
        shifted = jnp.exp(masked - row_top)
        attention = shifted / jnp.sum(shifted, axis=-1, keepdims=True)
        row_gate = row_mask[None, None, :, None]
        kept = attention.astype(bf16) * row_gate.astype(bf16)
        dweights = jnp.einsum("tgrd,jgd->grtj", cot_rows, value_rows, preferred_element_type=f32)
        row_delta = jnp.sum(attention * dweights, axis=-1, keepdims=True)
        dscore = (attention * (dweights - row_delta) * row_gate * HD ** (-0.5)).astype(bf16)
        key_grad = jnp.einsum("grtj,tgrd->jgd", dscore, query_rows, preferred_element_type=f32)
        value_grad = jnp.einsum("grtj,tgrd->jgd", kept, cot_rows, preferred_element_type=f32)
        kv_grad = jnp.concatenate(
            [key_grad.reshape(rows, columns), value_grad.reshape(rows, columns)], axis=1
        ).astype(bf16)

        block = runs * tokens
        mine = lax.dot_general(kv_grad[:block], weight, contracted_columns, preferred_element_type=f32)
        away = lax.dot_general(kv_grad[block:], weight, contracted_columns, preferred_element_type=f32).astype(bf16)

        def over_x(stay, leave):
            a = shift(leave[:block], 1, 0)
            b = shift(leave[block : 2 * block], 2, 0, True)
            c = shift(leave[2 * block :], -1, 0)
            return stay + a.astype(f32) + b.astype(f32) + c.astype(f32)

        image_grad = over_x(mine, away)

        back = sum_over_mp(
            adapter_scale
            * jnp.concatenate(
                [
                    lax.dot_general(kv_grad[:, :columns], up_key, contracted_columns, preferred_element_type=f32),
                    lax.dot_general(kv_grad[:, columns:], up_value, contracted_columns, preferred_element_type=f32),
                ],
                axis=1,
            )
        ).astype(bf16)
        adapter_grad = lax.dot_general(back, down, contracted_columns, preferred_element_type=f32)
        adapter_grad = over_x(adapter_grad[:block], adapter_grad[block:].astype(bf16))

        down_grad = lax.dot_general(image_fourth, back, contract_rows, preferred_element_type=f32)
        up_grad = adapter_scale * jnp.stack(
            [
                lax.dot_general(low[:, :lowrank], kv_grad[:, :columns], contract_rows, preferred_element_type=f32),
                lax.dot_general(low[:, lowrank:], kv_grad[:, columns:], contract_rows, preferred_element_type=f32),
            ]
        )
        both = jnp.concatenate([down_grad, up_grad.reshape(-1, down_grad.shape[1])], axis=0)
        both = lax.psum_scatter(both, "dp", scatter_dimension=0, tiled=True).astype(bf16)
        both = lax.all_gather(both, "dp", axis=0, tiled=True)
        down_out = both[:fourth]
        up_out = both[fourth:].reshape(up_grad.shape)

        here = lax.dynamic_slice_in_dim(image_grad, parallel_index * fourth, fourth, 1)
        image_grad = lax.dynamic_update_slice_in_dim(
            image_grad, here + adapter_grad, parallel_index * fourth, 1
        )
        send = image_grad[tokens:].astype(bf16)
        image_grad = (
            image_grad[:tokens]
            + shift(send[:tokens], 0, 1).astype(f32)
            + shift(send[tokens : 2 * tokens], 0, 2, True).astype(f32)
            + shift(send[2 * tokens :], 0, -1).astype(f32)
        )
        quarters = image_grad.reshape(tokens, heads, fourth).transpose(1, 0, 2)
        quarter = jnp.sum(lax.all_to_all(quarters, "mp", 0, 0), axis=0)
        result = lax.all_gather(quarter, "mp", axis=1, tiled=True)
        return (down_out[None], up_out[None], result[None])

    return body


def solution(mesh):
    in_specs = (
        P("dp", "segment", None),
        P("segment", "dp", None, "mp"),
        P("segment", "mp", None),
        P("segment", None, None, "mp"),
        P("segment", "dp", None, "mp"),
        P("segment", "dp", None, "mp"),
        P("dp"),
        P("dp"),
    )
    out_specs = (P("segment", "mp", None), P("segment", None, None, "mp"), P("dp", "segment", None))
    return jax.shard_map(make_body(mesh), mesh=mesh, in_specs=in_specs, out_specs=out_specs, check_vma=False)
```

time: 391 us -> 240 us (0.61)
  waiting for transfers between devices: 228 us -> 26.4 us
  starting transfers between devices: 0.16 us -> 53.4 us
  matrix products: 18.3 us -> 28.7 us
  blocking collectives: 108 us -> 98.4 us
  local copies, waits for them, and re-layouts: 19.3 us -> 12.2 us
  other arithmetic: 0.21 us -> 4.37 us
    all_gather x2 -> x1, waiting for transfers between devices: 124 us -> 0.02 us  [body(): weight = lax.all_gather(local_weight, 'dp', axis=0, tiled=True)]
    psum x3 -> x0, blocking collectives: 108 us -> none  [the longest x1 61.6 us: body(): down_sum, up_sum = lax.psum((grad_down, up_gradient), 'dp')]
    reduce_scatter x1, waiting for transfers between devices: 85.8 us -> 0.01 us  [body(): lax.psum_scatter(both, 'dp', scatter_dimension=0, tiled=True).astype(bf16)]
    all_gather x0 -> x4, blocking collectives: none -> 75.7 us  [the longest x2 33.8 us: sum_over_mp(): return jnp.sum(lax.all_gather(v, 'mp', axis=0), axis=0)]
    ppermute x0 -> x15, starting transfers between devices: none -> 53.4 us  [shift(): return lax.ppermute(v, AXES, pairs)]
    ppermute x0 -> x15, waiting for transfers between devices: none -> 26.3 us  [shift(): return lax.ppermute(v, AXES, pairs)]
    all_to_all x0 -> x1, blocking collectives: none -> 22.7 us  [body(): quarter = jnp.sum(lax.all_to_all(quarters, 'mp', 0, 0), axis=0)]
    psum x1 -> x0, waiting for transfers between devices: 17.3 us -> none  [body(): result = lax.psum(shared_sum, 'mp')]
  transfers between devices with their start and end apart: 4 -> 17, of which waited for: 4 -> 5; matrix products, arithmetic and copies ran while one was open for 2% -> 7% of each run, Pallas kernels for 0% -> 0%
where the time goes in v1:
time: 240 us; the launch traced here: 239 us
  blocking collectives  98.4 us (41%)
  starting transfers between devices  53.4 us (22%)
  matrix products  28.7 us (12%)
  waiting for transfers between devices  26.4 us (11%)
  between operations  15.8 us (7%)
  local copies, waits for them, and re-layouts  12.2 us (5%)
  other arithmetic  4.37 us (2%)
    ppermute x15, starting transfers between devices, shift(): return lax.ppermute(v, AXES, pairs)  53.4 us
    all_gather x2, blocking collectives, sum_over_mp(): return jnp.sum(lax.all_gather(v, 'mp', axis=0), axis=0)  33.8 us
    ppermute x15, waiting for transfers between devices, shift(): return lax.ppermute(v, AXES, pairs)  26.3 us
    all_gather x1, blocking collectives, body(): both = lax.all_gather(both, 'dp', axis=0, tiled=True)  25.8 us
    all_to_all x1, blocking collectives, body(): quarter = jnp.sum(lax.all_to_all(quarters, 'mp', 0, 0), axis=0)  22.7 us
    all_gather x1, blocking collectives, body(): result = lax.all_gather(quarter, 'mp', axis=1, tiled=True)  16.1 us
    dot_general x1, matrix products, body(): lax.dot_general(kv_grad[:block], weight, contracted_columns, preferred_el...  6.33 us
    dot_general x1, matrix products, body(): lax.dot_general(kv_grad[block:], weight, contracted_columns, preferred_el...  6.21 us
  transfers between devices with their start and end apart: 17, of which 5 were waited for; matrix products, arithmetic and copies ran while one was open for 7% of the time, Pallas kernels for 0%

profile of v1, /device:TPU:1, one launch (start us, length us, event | category | flops | bytes accessed | tf_op | source)
XLA Modules:
  0.0 239.4 jit_solution(17494728951961401160)
XLA Ops:
  7.2 2.6 %copy.42 = bf16[128,8,2,256]{3,1,2,0:T(8,128)(2,1)} copy(bf16[128,8,2,256]{3,2,1,0:T(2,128)(2,1)} %bitcast.103) | data formatting | bytes 2097152
  9.9 11.9 %collective-permute-start = (bf16[8,8192]{1,0:T(8,128)(2,1)S(1)}, bf16[8,8192]{1,0:T(8,128)(2,1)S(1)}, u32[]{:S(2)}, u32[]{:S(2)}) collective-permute-start(bf16[8,8192]{1,0:T(8,128)(2,1)S(1)} %bitcast.107), channel_id=1, source_target_pairs={{0,387},{1,384},{2,385},{3,386},{4,391},{5,388},{6,389},{7,390},{8... | collective-permute-start | bytes 393224 | tf_op jit(solution)/shard_map/ppermute | solution.py:33
  21.8 3.1 %collective-permute-start.1 = (bf16[8,8192]{1,0:T(8,128)(2,1)S(1)}, bf16[8,8192]{1,0:T(8,128)(2,1)}, u32[]{:S(2)}, u32[]{:S(2)}) collective-permute-start(bf16[8,8192]{1,0:T(8,128)(2,1)S(1)} %bitcast.108), channel_id=1, source_target_pairs={{0,256},{1,257},{2,258},{3,259},{4,263},{5,260},{6,261},{7,262},{8... | collective-permute-start | bytes 393224 | tf_op jit(solution)/shard_map/ppermute | solution.py:33
  24.9 2.6 %collective-permute-start.2 = (bf16[8,8192]{1,0:T(8,128)(2,1)S(1)}, bf16[8,8192]{1,0:T(8,128)(2,1)}, u32[]{:S(2)}, u32[]{:S(2)}) collective-permute-start(bf16[8,8192]{1,0:T(8,128)(2,1)S(1)} %bitcast.109), channel_id=1, source_target_pairs={{0,128},{1,129},{2,130},{3,131},{4,132},{5,133},{6,134},{7,135},{8... | collective-permute-start | bytes 393224 | tf_op jit(solution)/shard_map/ppermute | solution.py:33
  29.6 2.0 copy.40
  32.3 1.9 collective-permute-done.2
  35.4 4.3 %collective-permute-start.3 = (bf16[32,8192]{1,0:T(8,128)(2,1)S(1)}, bf16[32,8192]{1,0:T(8,128)(2,1)S(1)}, u32[]{:S(2)}, u32[]{:S(2)}) collective-permute-start(bf16[32,8192]{1,0:T(8,128)(2,1)S(1)} %pad_maximum_fusion.1), channel_id=1, source_target_pairs={{0,96},{1,97},{2,98},{3,99},{4,100},{5,101},{6,102},{7,103},{8,104... | collective-permute-start | bytes 1572872 | tf_op jit(solution)/shard_map/ppermute | solution.py:33
  39.7 2.4 %collective-permute-start.4 = (bf16[32,8192]{1,0:T(8,128)(2,1)S(1)}, bf16[32,8192]{1,0:T(8,128)(2,1)S(1)}, u32[]{:S(2)}, u32[]{:S(2)}) collective-permute-start(bf16[32,8192]{1,0:T(8,128)(2,1)S(1)} %pad_maximum_fusion.1), channel_id=1, source_target_pairs={{0,64},{1,65},{2,66},{3,67},{4,68},{5,69},{6,70},{7,71},{8,72},{9,... | collective-permute-start | bytes 1572872 | tf_op jit(solution)/shard_map/ppermute | solution.py:33
  42.1 2.5 %collective-permute-start.5 = (bf16[32,8192]{1,0:T(8,128)(2,1)S(1)}, bf16[32,8192]{1,0:T(8,128)(2,1)S(1)}, u32[]{:S(2)}, u32[]{:S(2)}) collective-permute-start(bf16[32,8192]{1,0:T(8,128)(2,1)S(1)} %pad_maximum_fusion.1), channel_id=1, source_target_pairs={{0,32},{1,33},{2,34},{3,35},{4,36},{5,37},{6,38},{7,39},{8,40},{9,... | collective-permute-start | bytes 1572872 | tf_op jit(solution)/shard_map/ppermute | solution.py:33
  46.5 4.3 %collective-permute-done.3 = bf16[32,8192]{1,0:T(8,128)(2,1)S(1)} collective-permute-done((bf16[32,8192]{1,0:T(8,128)(2,1)S(1)}, bf16[32,8192]{1,0:T(8,128)(2,1)S(1)}, u32[]{:S(2)}, u32[]{:S(2)}) %collective-permute-start.3) | collective-permute-done | bytes 524320 | tf_op jit(solution)/shard_map/ppermute | solution.py:33
  50.9 4.8 %collective-permute-done.4 = bf16[32,8192]{1,0:T(8,128)(2,1)S(1)} collective-permute-done((bf16[32,8192]{1,0:T(8,128)(2,1)S(1)}, bf16[32,8192]{1,0:T(8,128)(2,1)S(1)}, u32[]{:S(2)}, u32[]{:S(2)}) %collective-permute-start.4) | collective-permute-done | bytes 524320 | tf_op jit(solution)/shard_map/ppermute | solution.py:33
  55.7 12.5 %collective-permute-done.5 = bf16[32,8192]{1,0:T(8,128)(2,1)S(1)} collective-permute-done((bf16[32,8192]{1,0:T(8,128)(2,1)S(1)}, bf16[32,8192]{1,0:T(8,128)(2,1)S(1)}, u32[]{:S(2)}, u32[]{:S(2)}) %collective-permute-start.5) | collective-permute-done | bytes 524320 | tf_op jit(solution)/shard_map/ppermute | solution.py:33
  68.6 16.8 %all-gather = f32[512,128]{1,0:T(8,128)S(1)} all-gather(f32[128,128]{1,0:T(8,128)S(1)} %fusion.20), channel_id=2, replica_groups=mesh['segment'=16,'dp'=8,'mp'=4] {'mp'}, dimensions={0}, use_global_device_ids=true | all-gather | bytes 327680 | tf_op jit(solution)/shard_map/all_gather | solution.py:36
  85.9 4.6 %fusion.12 = bf16[128,512]{1,0:T(8,128)(2,1)S(1)} fusion(bf16[128,8192]{1,0:T(8,128)(2,1)S(1)} %constant_dynamic-update-slice_fusion, bf16[8192,512]{1,0:T(8,128)(2,1)} %all-gather.3.cloned.1.call-done, f32[128,256]{1,0:T(8,128)S(1)} %fusion.50, f32[128,256]{1,0:T(8,128)S(1)} %fusion.53), kind=kOutput, calls=%fused_computation.17 | convolution fusion | flops 1074003968 | bytes 10878976 | tf_op jit(solution)/shard_map/dot_general | solution.py:79
  91.8 2.5 %fusion.95 = (f32[2,8,128]{2,1,0:T(8,128)S(1)}, f32[2,8,128,128]{2,3,1,0:T(8,128)}) fusion(bf16[128,2,8,128]{0,3,2,1:T(8,128)(2,1)} %bitcast.104, pred[128]{0:T(512)(128)(4,1)S(1)} %fusion.69, bf16[128,2,128,1]{2,1,0,3:T(2,128)(2,1)S(1)} %bitcast.112), kind=kOutput, calls=%fused_computation.130 | convolution fusion | flops 68157568 | bytes 1646720 | tf_op jit(solution)/shard_map/sub | solution.py:93
  96.1 3.0 %fusion.15 = bf16[2,128,128]{1,2,0:T(8,128)(2,1)S(1)} fusion(bf16[128,2,8,128]{0,3,2,1:T(8,128)(2,1)} %bitcast.106, f32[2,8,128,128]{2,3,1,0:T(8,128)} %convolution_bitcast_fusion, f32[128]{0:T(128)S(1)} %get-tuple-element.18, f32[2,8,128,128]{2,3,1,0:T(8,128)} %get-tuple-element.15, f32[2,8,128]{2,1,0:T(8,128)S(1)} %get-tuple-element.14), kind=kOutput, calls=%fused_computation.21 | convolution fusion | flops 69240960 | bytes 2695680 | tf_op jit(solution)/shard_map/grtj,tgrd->jgd/dot_general | solution.py:100
  99.4 6.2 %convolution_convert_fusion = bf16[96,8192]{1,0:T(8,128)(2,1)S(1)} fusion(bf16[8192,512]{1,0:T(8,128)(2,1)} %all-gather.3.cloned.1.call-done, bf16[128,256]{0,1:T(8,128)(2,1)S(1)} %bitcast.93, bf16[128,256]{0,1:T(8,128)(2,1)S(1)} %bitcast.97), kind=kOutput, calls=%fused_computation.2 | convolution fusion | flops 806289408 | bytes 10092544 | tf_op jit(solution)/shard_map/dot_general | solution.py:108
  106.8 1.9 collective-permute-start.6
  108.7 2.4 %collective-permute-start.7 = (bf16[32,8192]{1,0:T(8,128)(2,1)}, bf16[32,8192]{1,0:T(8,128)(2,1)}, u32[]{:S(2)}, u32[]{:S(2)}) collective-permute-start(bf16[32,8192]{1,0:T(8,128)(2,1)} %get-tuple-element.5), channel_id=1, source_target_pairs={{0,64},{1,65},{2,66},{3,67},{4,68},{5,69},{6,70},{7,71},{8,72},{9,... | collective-permute-start | bytes 1572872 | tf_op jit(solution)/shard_map/ppermute | solution.py:33
  111.2 4.0 %collective-permute-start.8 = (bf16[32,8192]{1,0:T(8,128)(2,1)}, bf16[32,8192]{1,0:T(8,128)(2,1)}, u32[]{:S(2)}, u32[]{:S(2)}) collective-permute-start(bf16[32,8192]{1,0:T(8,128)(2,1)} %get-tuple-element.4), channel_id=1, source_target_pairs={{0,96},{1,97},{2,98},{3,99},{4,100},{5,101},{6,102},{7,103},{8,104... | collective-permute-start | bytes 1572872 | tf_op jit(solution)/shard_map/ppermute | solution.py:33
  115.3 16.9 %all_gather.22 = f32[4,128,128]{2,1,0:T(8,128)S(1)} all-gather(f32[1,128,128]{2,1,0:T(8,128)S(1)} %copy.27), channel_id=1, replica_groups=mesh['segment'=16,'dp'=8,'mp'=4] {'mp'}, dimensions={0}, use_global_device_ids=true | all-gather | bytes 327680 | tf_op jit(solution)/shard_map/all_gather | solution.py:36
  134.6 4.4 %collective-permute-start.10 = (bf16[32,2048]{1,0:T(8,128)(2,1)}, bf16[32,2048]{1,0:T(8,128)(2,1)S(1)}, u32[]{:S(2)}, u32[]{:S(2)}) collective-permute-start(bf16[32,2048]{1,0:T(8,128)(2,1)} %get-tuple-element.11), channel_id=1, source_target_pairs={{0,64},{1,65},{2,66},{3,67},{4,68},{5,69},{6,70},{7,71},{8,72},{9,... | collective-permute-start | bytes 393224 | tf_op jit(solution)/shard_map/ppermute | solution.py:33
  139.0 3.1 %collective-permute-start.11 = (bf16[32,2048]{1,0:T(8,128)(2,1)}, bf16[32,2048]{1,0:T(8,128)(2,1)S(1)}, u32[]{:S(2)}, u32[]{:S(2)}) collective-permute-start(bf16[32,2048]{1,0:T(8,128)(2,1)} %get-tuple-element.10), channel_id=1, source_target_pairs={{0,96},{1,97},{2,98},{3,99},{4,100},{5,101},{6,102},{7,103},{8,104... | collective-permute-start | bytes 393224 | tf_op jit(solution)/shard_map/ppermute | solution.py:33
  142.8 2.2 collective-permute-start.9
  145.0 6.3 %convert_add_fusion = f32[32,8192]{1,0:T(8,128)S(1)} fusion(bf16[32,8192]{1,0:T(8,128)(2,1)} %collective-permute-done.8, bf16[32,8192]{1,0:T(8,128)(2,1)} %collective-permute-done.7, bf16[32,8192]{1,0:T(8,128)(2,1)} %collective-permute-done.6, bf16[8192,512]{1,0:T(8,128)(2,1)} %all-gather.3.cloned.1.call-done, bf16[128,256]{0,1:T(8,128)(2,1)S(1)} %bitcast.95, ...), kind=kOutput, calls=%fused_computation.26 | convolution fusion | flops 270073856 | bytes 11141120 | tf_op jit(solution)/shard_map/dot_general | solution.py:107
  152.5 1.9 collective-permute-start.12
  154.4 1.9 collective-permute-start.13
  156.3 4.6 %collective-permute-start.14 = (bf16[8,8192]{1,0:T(8,128)(2,1)S(1)}, bf16[8,8192]{1,0:T(8,128)(2,1)S(1)}, u32[]{:S(2)}, u32[]{:S(2)}) collective-permute-start(bf16[8,8192]{1,0:T(8,128)(2,1)S(1)} %get-tuple-element.7), channel_id=1, source_target_pairs={{0,387},{1,384},{2,385},{3,386},{4,391},{5,388},{6,389},{7,390},{8... | collective-permute-start | bytes 393224 | tf_op jit(solution)/shard_map/ppermute | solution.py:33
  162.0 2.7 %collective-permute-done.14 = bf16[8,8192]{1,0:T(8,128)(2,1)S(1)} collective-permute-done((bf16[8,8192]{1,0:T(8,128)(2,1)S(1)}, bf16[8,8192]{1,0:T(8,128)(2,1)S(1)}, u32[]{:S(2)}, u32[]{:S(2)}) %collective-permute-start.14) | collective-permute-done | bytes 131104 | tf_op jit(solution)/shard_map/ppermute | solution.py:33
  164.8 22.7 %all_to_all.5 = f32[4,8,2048]{2,1,0:T(8,128)S(1)} all-to-all(f32[4,8,2048]{2,1,0:T(8,128)S(1)} %bitcast.100), channel_id=1, replica_groups=mesh['segment'=16,'dp'=8,'mp'=4] {'mp'}, dimensions={0} | all-to-all | bytes 524288 | tf_op jit(solution)/shard_map/all_to_all | solution.py:156
  187.5 16.1 %all_gather.24 = f32[8,8192]{1,0:T(8,128)S(1)} all-gather(f32[8,2048]{1,0:T(8,128)S(1)} %reduce_sum.49), channel_id=1, replica_groups=mesh['segment'=16,'dp'=8,'mp'=4] {'mp'}, dimensions={1}, use_global_device_ids=true | all-gather | bytes 327680 | tf_op jit(solution)/shard_map/all_gather | solution.py:157
  204.6 25.8 %all_gather.23 = bf16[2304,128]{1,0:T(8,128)(2,1)S(1)} all-gather(bf16[288,128]{1,0:T(8,128)(2,1)S(1)} %convert_element_type.76), channel_id=1, replica_groups=mesh['segment'=16,'dp'=8,'mp'=4] {'dp'}, dimensions={0}, use_global_device_ids=true | all-gather | bytes 663552 | tf_op jit(solution)/shard_map/all_gather | solution.py:140
  (67 shorter events, 18.2 us)
Async XLA Ops:
  7.2 61.2 %copy-start = (bf16[1,2048,128]{2,1,0:T(8,128)(2,1)S(1)}, bf16[1,2048,128]{2,1,0:T(8,128)(2,1)}, u32[]{:S(2)}) copy-start(bf16[1,2048,128]{2,1,0:T(8,128)(2,1)} %param.10) | copy-start | bytes 1572868
  7.2 2.7 %copy-start.1 = (bf16[1,8,8192]{2,1,0:T(8,128)(2,1)S(1)}, bf16[1,8,8192]{2,1,0:T(8,128)(2,1)}, u32[]{:S(2)}) copy-start(bf16[1,8,8192]{2,1,0:T(8,128)(2,1)} %param.8) | copy-start | bytes 393220
  7.2 78.7 %all-gather.3.cloned.1.call-start = ((), (), s32[]{:S(2)}) async-start(), calls=%async_computation.2 | async-start | bytes 9437184 | tf_op jit(solution)/shard_map/all_gather | solution.py:59
  9.8 193.8 %reduce-scatter.2.cloned.1.call-start = ((), (), s32[]{:S(2)}) async-start(), calls=%async_computation.3 | async-start | bytes 1327104 | tf_op jit(solution)/shard_map/reduce_scatter | solution.py:139
  9.9 22.4 %collective-permute-start = (bf16[8,8192]{1,0:T(8,128)(2,1)S(1)}, bf16[8,8192]{1,0:T(8,128)(2,1)S(1)}, u32[]{:S(2)}, u32[]{:S(2)}) collective-permute-start(bf16[8,8192]{1,0:T(8,128)(2,1)S(1)} %bitcast.107), channel_id=1, source_target_pairs={{0,387},{1,384},{2,385},{3,386},{4,391},{5,388},{6,389},{7,390},{8... | collective-permute-start | bytes 393224 | tf_op jit(solution)/shard_map/ppermute | solution.py:33
  21.8 10.5 %collective-permute-start.1 = (bf16[8,8192]{1,0:T(8,128)(2,1)S(1)}, bf16[8,8192]{1,0:T(8,128)(2,1)}, u32[]{:S(2)}, u32[]{:S(2)}) collective-permute-start(bf16[8,8192]{1,0:T(8,128)(2,1)S(1)} %bitcast.108), channel_id=1, source_target_pairs={{0,256},{1,257},{2,258},{3,259},{4,263},{5,260},{6,261},{7,262},{8... | collective-permute-start | bytes 393224 | tf_op jit(solution)/shard_map/ppermute | solution.py:33
  24.9 9.4 %collective-permute-start.2 = (bf16[8,8192]{1,0:T(8,128)(2,1)S(1)}, bf16[8,8192]{1,0:T(8,128)(2,1)}, u32[]{:S(2)}, u32[]{:S(2)}) collective-permute-start(bf16[8,8192]{1,0:T(8,128)(2,1)S(1)} %bitcast.109), channel_id=1, source_target_pairs={{0,128},{1,129},{2,130},{3,131},{4,132},{5,133},{6,134},{7,135},{8... | collective-permute-start | bytes 393224 | tf_op jit(solution)/shard_map/ppermute | solution.py:33
  35.4 15.4 %collective-permute-start.3 = (bf16[32,8192]{1,0:T(8,128)(2,1)S(1)}, bf16[32,8192]{1,0:T(8,128)(2,1)S(1)}, u32[]{:S(2)}, u32[]{:S(2)}) collective-permute-start(bf16[32,8192]{1,0:T(8,128)(2,1)S(1)} %pad_maximum_fusion.1), channel_id=1, source_target_pairs={{0,96},{1,97},{2,98},{3,99},{4,100},{5,101},{6,102},{7,103},{8,104... | collective-permute-start | bytes 1572872 | tf_op jit(solution)/shard_map/ppermute | solution.py:33
  39.7 16.0 %collective-permute-start.4 = (bf16[32,8192]{1,0:T(8,128)(2,1)S(1)}, bf16[32,8192]{1,0:T(8,128)(2,1)S(1)}, u32[]{:S(2)}, u32[]{:S(2)}) collective-permute-start(bf16[32,8192]{1,0:T(8,128)(2,1)S(1)} %pad_maximum_fusion.1), channel_id=1, source_target_pairs={{0,64},{1,65},{2,66},{3,67},{4,68},{5,69},{6,70},{7,71},{8,72},{9,... | collective-permute-start | bytes 1572872 | tf_op jit(solution)/shard_map/ppermute | solution.py:33
  42.1 26.1 %collective-permute-start.5 = (bf16[32,8192]{1,0:T(8,128)(2,1)S(1)}, bf16[32,8192]{1,0:T(8,128)(2,1)S(1)}, u32[]{:S(2)}, u32[]{:S(2)}) collective-permute-start(bf16[32,8192]{1,0:T(8,128)(2,1)S(1)} %pad_maximum_fusion.1), channel_id=1, source_target_pairs={{0,32},{1,33},{2,34},{3,35},{4,36},{5,37},{6,38},{7,39},{8,40},{9,... | collective-permute-start | bytes 1572872 | tf_op jit(solution)/shard_map/ppermute | solution.py:33
  50.9 34.6 %copy-start.2 = (bf16[1,2,64,256]{3,2,1,0:T(8,128)(2,1)S(1)}, bf16[1,2,64,256]{3,2,1,0:T(8,128)(2,1)}, u32[]{:S(2)}) copy-start(bf16[1,2,64,256]{3,2,1,0:T(8,128)(2,1)} %param.11) | copy-start | bytes 196612
  106.8 36.0 %collective-permute-start.6 = (bf16[32,8192]{1,0:T(8,128)(2,1)}, bf16[32,8192]{1,0:T(8,128)(2,1)}, u32[]{:S(2)}, u32[]{:S(2)}) collective-permute-start(bf16[32,8192]{1,0:T(8,128)(2,1)} %get-tuple-element.3), channel_id=1, source_target_pairs={{0,32},{1,33},{2,34},{3,35},{4,36},{5,37},{6,38},{7,39},{8,40},{9,... | collective-permute-start | bytes 1572872 | tf_op jit(solution)/shard_map/ppermute | solution.py:33
  108.7 36.2 %collective-permute-start.7 = (bf16[32,8192]{1,0:T(8,128)(2,1)}, bf16[32,8192]{1,0:T(8,128)(2,1)}, u32[]{:S(2)}, u32[]{:S(2)}) collective-permute-start(bf16[32,8192]{1,0:T(8,128)(2,1)} %get-tuple-element.5), channel_id=1, source_target_pairs={{0,64},{1,65},{2,66},{3,67},{4,68},{5,69},{6,70},{7,71},{8,72},{9,... | collective-permute-start | bytes 1572872 | tf_op jit(solution)/shard_map/ppermute | solution.py:33
  111.2 33.8 %collective-permute-start.8 = (bf16[32,8192]{1,0:T(8,128)(2,1)}, bf16[32,8192]{1,0:T(8,128)(2,1)}, u32[]{:S(2)}, u32[]{:S(2)}) collective-permute-start(bf16[32,8192]{1,0:T(8,128)(2,1)} %get-tuple-element.4), channel_id=1, source_target_pairs={{0,96},{1,97},{2,98},{3,99},{4,100},{5,101},{6,102},{7,103},{8,104... | collective-permute-start | bytes 1572872 | tf_op jit(solution)/shard_map/ppermute | solution.py:33
  134.6 16.7 %collective-permute-start.10 = (bf16[32,2048]{1,0:T(8,128)(2,1)}, bf16[32,2048]{1,0:T(8,128)(2,1)S(1)}, u32[]{:S(2)}, u32[]{:S(2)}) collective-permute-start(bf16[32,2048]{1,0:T(8,128)(2,1)} %get-tuple-element.11), channel_id=1, source_target_pairs={{0,64},{1,65},{2,66},{3,67},{4,68},{5,69},{6,70},{7,71},{8,72},{9,... | collective-permute-start | bytes 393224 | tf_op jit(solution)/shard_map/ppermute | solution.py:33
  139.0 12.3 %collective-permute-start.11 = (bf16[32,2048]{1,0:T(8,128)(2,1)}, bf16[32,2048]{1,0:T(8,128)(2,1)S(1)}, u32[]{:S(2)}, u32[]{:S(2)}) collective-permute-start(bf16[32,2048]{1,0:T(8,128)(2,1)} %get-tuple-element.10), channel_id=1, source_target_pairs={{0,96},{1,97},{2,98},{3,99},{4,100},{5,101},{6,102},{7,103},{8,104... | collective-permute-start | bytes 393224 | tf_op jit(solution)/shard_map/ppermute | solution.py:33
  142.8 8.6 %collective-permute-start.9 = (bf16[32,2048]{1,0:T(8,128)(2,1)S(1)}, bf16[32,2048]{1,0:T(8,128)(2,1)S(1)}, u32[]{:S(2)}, u32[]{:S(2)}) collective-permute-start(bf16[32,2048]{1,0:T(8,128)(2,1)S(1)} %get-tuple-element.9), channel_id=1, source_target_pairs={{0,32},{1,33},{2,34},{3,35},{4,36},{5,37},{6,38},{7,39},{8,40},{9,... | collective-permute-start | bytes 393224 | tf_op jit(solution)/shard_map/ppermute | solution.py:33
  152.5 9.6 %collective-permute-start.12 = (bf16[8,8192]{1,0:T(8,128)(2,1)S(1)}, bf16[8,8192]{1,0:T(8,128)(2,1)S(1)}, u32[]{:S(2)}, u32[]{:S(2)}) collective-permute-start(bf16[8,8192]{1,0:T(8,128)(2,1)S(1)} %get-tuple-element.6), channel_id=1, source_target_pairs={{0,128},{1,129},{2,130},{3,131},{4,132},{5,133},{6,134},{7,135},{8... | collective-permute-start | bytes 393224 | tf_op jit(solution)/shard_map/ppermute | solution.py:33
  154.4 7.6 %collective-permute-start.13 = (bf16[8,8192]{1,0:T(8,128)(2,1)S(1)}, bf16[8,8192]{1,0:T(8,128)(2,1)S(1)}, u32[]{:S(2)}, u32[]{:S(2)}) collective-permute-start(bf16[8,8192]{1,0:T(8,128)(2,1)S(1)} %get-tuple-element.8), channel_id=1, source_target_pairs={{0,256},{1,257},{2,258},{3,259},{4,263},{5,260},{6,261},{7,262},{8... | collective-permute-start | bytes 393224 | tf_op jit(solution)/shard_map/ppermute | solution.py:33
  156.3 8.4 %collective-permute-start.14 = (bf16[8,8192]{1,0:T(8,128)(2,1)S(1)}, bf16[8,8192]{1,0:T(8,128)(2,1)S(1)}, u32[]{:S(2)}, u32[]{:S(2)}) collective-permute-start(bf16[8,8192]{1,0:T(8,128)(2,1)S(1)} %get-tuple-element.7), channel_id=1, source_target_pairs={{0,387},{1,384},{2,385},{3,386},{4,391},{5,388},{6,389},{7,390},{8... | collective-permute-start | bytes 393224 | tf_op jit(solution)/shard_map/ppermute | solution.py:33
Sparse Core Ops, SparseCore 0:
  10.1 63.0 all-gather.2
  162.1 40.8 reduce-scatter.1

commit v2 on v1

v2 whole, which is shorter than its diff:
```python
import jax
import jax.numpy as jnp
from jax import lax
from jax.sharding import PartitionSpec as P


HD = 128
TILES = 4
SIDE = 4
CORES = 2

adapter_scale = 2.0
contract_rows = (((0,), (0,)), ((), ()))
contracted_columns = (((1,), (1,)), ((), ()))
f32 = jnp.float32
bf16 = jnp.bfloat16
AXES = ("segment", "dp", "mp")


def make_body(mesh):
    segments, parts, heads = (mesh.shape[a] for a in AXES)
    runs = segments // SIDE
    ring = runs * heads
    lines = parts // CORES

    def shift(v, dx=0, dy=0, dz=0, swap=0, opposite=False):
        pairs = []
        for s in range(segments):
            for d in range(parts):
                for m in range(heads):
                    z_lo, x = divmod(s, SIDE)
                    y, core = divmod(d, CORES)
                    sign = -1 if (opposite and core) else 1
                    x2 = (x + sign * dx) % SIDE
                    d2 = (y + sign * dy) % lines * CORES + (core + swap) % CORES
                    m2, z2 = divmod((m * runs + z_lo + sign * dz) % ring, runs)
                    pairs.append(((s * parts + d) * heads + m, ((z2 * SIDE + x2) * parts + d2) * heads + m2))
        return lax.ppermute(v, AXES, pairs)

    def sum_over_mp(v, out):
        far = shift(v, dz=2 * runs, opposite=True)
        near = shift(v, dz=runs)
        prior = shift(v, dz=-runs)
        return ((v.astype(f32) + far.astype(f32)) + (near.astype(f32) + prior.astype(f32))).astype(out)

    def body(
        encoder_image_states,
        frozen_key_value,
        adapter_down_weight,
        adapter_up_weight,
        queries,
        cotangent,
        text_token_length,
        image_tile_count,
    ):
        tokens, model_width = encoder_image_states.shape[1:]
        parallel_index = lax.axis_index("mp")
        segment_index = lax.axis_index("segment")
        part_index = lax.axis_index("dp")
        y_index, core_index = part_index // CORES, part_index % CORES
        second_core = core_index == 1
        lowrank = adapter_up_weight.shape[2]
        columns = adapter_up_weight.shape[3]
        up_key, up_value = adapter_up_weight[0, 0], adapter_up_weight[0, 1]
        down = adapter_down_weight[0]
        fourth = down.shape[0]
        eighth = fourth // CORES

        def swap_halves(v, axis):
            a, b = jnp.split(v, CORES, axis=axis)
            return jnp.where(second_core, jnp.concatenate([b, a], axis=axis), v)

        def swap_chunks(v):
            w = v.reshape(v.shape[0], lines, CORES, eighth)
            return jnp.where(second_core, w[:, :, ::-1], w).reshape(v.shape)

        def roll_columns(v, by):
            return lax.dynamic_slice_in_dim(jnp.concatenate([v, v], axis=1), by * fourth, model_width, 1)

        own = swap_chunks(roll_columns(encoder_image_states[0], y_index))
        down = swap_halves(down, 0)
        chunk_pair = (parallel_index - y_index) % lines

        line = jnp.concatenate([own, shift(own, dz=-1), shift(own, dz=2, opposite=True), shift(own, dz=1)], axis=0)
        image = jnp.concatenate([line, shift(line, dx=-1), shift(line, dx=2, opposite=True), shift(line, dx=1)], axis=0)
        rows = image.shape[0]
        offset = jnp.arange(rows, dtype=jnp.int32)
        x_off, z_off, tok = offset // (runs * tokens), (offset // tokens) % runs, offset % tokens
        position = (
            ((segment_index // SIDE + z_off) % runs) * SIDE + (segment_index % SIDE + x_off) % SIDE
        ) * tokens + tok

        local_weight = frozen_key_value[0].reshape(-1, CORES * columns)
        half = local_weight.shape[0] // 2
        following = shift(local_weight, dy=-1)
        preceding = shift(local_weight, dy=1)
        first_half, second_half = following[:half], preceding[half:]
        across_a = shift(first_half, dy=-1)
        across_b = shift(second_half, dy=1)
        weight = jnp.concatenate(
            [
                local_weight,
                shift(local_weight, swap=1),
                following,
                shift(following, swap=1),
                across_a,
                across_b,
                shift(across_a, swap=1),
                shift(across_b, swap=1),
                preceding,
                shift(preceding, swap=1),
            ],
            axis=0,
        )

        image_fourth = lax.dynamic_slice_in_dim(image, chunk_pair * fourth, fourth, 1)
        low = jnp.dot(image_fourth, down, preferred_element_type=f32)
        low = sum_over_mp(low, bf16)
        adapted = jnp.concatenate(
            [
                jnp.dot(low[:, :lowrank], up_key, preferred_element_type=f32),
                jnp.dot(low[:, lowrank:], up_value, preferred_element_type=f32),
            ],
            axis=1,
        )
        key_value = (jnp.dot(image, weight, preferred_element_type=f32) + adapter_scale * adapted).astype(bf16)

        local_kv = columns // HD
        text_rows = queries.shape[2]
        group = queries.shape[3] // HD // local_kv
        query_rows = queries[0, 0].reshape(text_rows, local_kv, group, HD)
        cot_rows = cotangent[0, 0].reshape(text_rows, local_kv, group, HD)
        key_rows = key_value[:, :columns].reshape(rows, local_kv, HD)
        value_rows = key_value[:, columns:].reshape(rows, local_kv, HD)
        key_mask = position < image_tile_count[0] * (rows // TILES)
        row_mask = (jnp.arange(text_rows, dtype=jnp.int32) < text_token_length[0]).astype(f32)
        scores = jnp.einsum("tgrd,jgd->grtj", query_rows, key_rows, preferred_element_type=f32) * HD ** (-0.5)
        masked = jnp.where(key_mask[None, None, None, :], scores, -1e30)
        row_top = jnp.max(masked, axis=-1, keepdims=True)
        shifted = jnp.exp(masked - row_top)
        attention = shifted / jnp.sum(shifted, axis=-1, keepdims=True)
        row_gate = row_mask[None, None, :, None]
        kept = attention.astype(bf16) * row_gate.astype(bf16)
        dweights = jnp.einsum("tgrd,jgd->grtj", cot_rows, value_rows, preferred_element_type=f32)
        row_delta = jnp.sum(attention * dweights, axis=-1, keepdims=True)
        dscore = (attention * (dweights - row_delta) * row_gate * HD ** (-0.5)).astype(bf16)
        key_grad = jnp.einsum("grtj,tgrd->jgd", dscore, query_rows, preferred_element_type=f32)
        value_grad = jnp.einsum("grtj,tgrd->jgd", kept, cot_rows, preferred_element_type=f32)
        kv_grad = jnp.concatenate(
            [key_grad.reshape(rows, columns), value_grad.reshape(rows, columns)], axis=1
        ).astype(bf16)

        block = runs * tokens

        def over_x(v):
            v = v.astype(bf16)
            a = shift(v[block : 2 * block], dx=1)
            b = shift(v[2 * block : 3 * block], dx=2, opposite=True)
            c = shift(v[3 * block :], dx=-1)
            return v[:block].astype(f32) + a.astype(f32) + b.astype(f32) + c.astype(f32)

        image_grad = over_x(lax.dot_general(kv_grad, weight, contracted_columns, preferred_element_type=f32))

        back = adapter_scale * jnp.concatenate(
            [
                lax.dot_general(kv_grad[:, :columns], up_key, contracted_columns, preferred_element_type=f32),
                lax.dot_general(kv_grad[:, columns:], up_value, contracted_columns, preferred_element_type=f32),
            ],
            axis=1,
        )
        back = lax.all_gather(back, "mp", axis=0)
        back = jnp.sum(back, axis=0).astype(bf16)
        adapter_grad = over_x(lax.dot_general(back, down, contracted_columns, preferred_element_type=f32))

        down_grad = lax.dot_general(image_fourth, back, contract_rows, preferred_element_type=f32)
        up_grad = adapter_scale * jnp.stack(
            [
                lax.dot_general(low[:, :lowrank], kv_grad[:, :columns], contract_rows, preferred_element_type=f32),
                lax.dot_general(low[:, lowrank:], kv_grad[:, columns:], contract_rows, preferred_element_type=f32),
            ]
        )
        both = jnp.concatenate(
            [swap_halves(down_grad, 0), up_grad.reshape(-1, down_grad.shape[1])], axis=0
        ).reshape(lines, CORES, -1, down_grad.shape[1])
        kept_core = lax.dynamic_index_in_dim(both, core_index, 1, keepdims=False)
        sent_core = lax.dynamic_index_in_dim(both, 1 - core_index, 1, keepdims=False)
        pair = kept_core + shift(sent_core, swap=1)

        def for_line(r):
            return lax.dynamic_index_in_dim(pair, (y_index + r) % lines, 0, keepdims=False)

        both = (
            for_line(0)
            + shift(for_line(1), dy=1)
            + shift(for_line(2), dy=2, opposite=True)
            + shift(for_line(3), dy=-1)
        ).astype(bf16)

        here = lax.dynamic_slice_in_dim(image_grad, chunk_pair * fourth, fourth, 1)
        image_grad = lax.dynamic_update_slice_in_dim(image_grad, here + adapter_grad, chunk_pair * fourth, 1)
        send = image_grad[tokens:].astype(bf16)
        image_grad = (
            image_grad[:tokens]
            + shift(send[:tokens], dz=1).astype(f32)
            + shift(send[tokens : 2 * tokens], dz=2, opposite=True).astype(f32)
            + shift(send[2 * tokens :], dz=-1).astype(f32)
        )
        image_grad = sum_over_mp(image_grad.astype(bf16), f32)
        both = lax.all_gather(both, "dp", axis=0, tiled=True)
        down_out = both[:fourth]
        up_out = both[fourth:].reshape(up_grad.shape)
        result = roll_columns(swap_chunks(image_grad), (lines - y_index) % lines)
        return (down_out[None], up_out[None], result[None])

    return body


def solution(mesh):
    in_specs = (
        P("dp", "segment", None),
        P("segment", "dp", None, "mp"),
        P("segment", "mp", None),
        P("segment", None, None, "mp"),
        P("segment", "dp", None, "mp"),
        P("segment", "dp", None, "mp"),
        P("dp"),
        P("dp"),
    )
    out_specs = (P("segment", "mp", None), P("segment", None, None, "mp"), P("dp", "segment", None))
    body = make_body(mesh)

    return jax.shard_map(body, mesh=mesh, in_specs=in_specs, out_specs=out_specs, check_vma=False)
```

time: 240 us -> 267 us (1.11)
  starting transfers between devices: 53.4 us -> 156 us
  blocking collectives: 98.4 us -> 37 us
  between operations: 15.8 us -> 3.15 us
  matrix products: 28.7 us -> 16.3 us
  local copies, waits for them, and re-layouts: 12.2 us -> 19 us
    ppermute x15 -> x34, starting transfers between devices: 53.4 us -> 156 us  [shift(): return lax.ppermute(v, AXES, pairs)]
    all_gather x3 -> x1, blocking collectives: 49.9 us -> 20.7 us  [body(): back = lax.all_gather(back, 'mp', axis=0)]
    all_to_all x1 -> x0, blocking collectives: 22.7 us -> none  [body(): quarter = jnp.sum(lax.all_to_all(quarters, 'mp', 0, 0), axis=0)]
    all_gather x1, blocking collectives: 25.8 us -> 16.2 us  [body(): both = lax.all_gather(both, 'dp', axis=0, tiled=True)]
    dot_general x3 -> x2, matrix products: 12.8 us -> 6.65 us  [the longest x1 6.29 us: body(): lax.dot_general(kv_grad, weight, contracted_columns, preferred_element_ty...]
    dot_general x1, matrix products: 4.64 us -> 1.39 us  [body(): jnp.dot(image, weight, preferred_element_type=f32) + adapter_scale * adapted]
    unnamed x15 -> x39, local copies, waits for them, and re-layouts: 5.31 us -> 8.12 us
    ppermute x15 -> x34, waiting for transfers between devices: 26.3 us -> 28.1 us  [shift(): return lax.ppermute(v, AXES, pairs)]
  transfers between devices with their start and end apart: 17 -> 34, of which waited for: 5 -> 5; matrix products, arithmetic and copies ran while one was open for 7% -> 7% of each run, Pallas kernels for 0% -> 0%
where the time goes in v2:
time: 267 us; the launch traced here: 265 us
  starting transfers between devices  156 us (58%)
  blocking collectives  37 us (14%)
  waiting for transfers between devices  28.1 us (11%)
  local copies, waits for them, and re-layouts  19 us (7%)
  matrix products  16.3 us (6%)
  other arithmetic  6.14 us (2%)
  between operations  3.15 us (1%)
    ppermute x34, starting transfers between devices, shift(): return lax.ppermute(v, AXES, pairs)  156 us
    ppermute x34, waiting for transfers between devices, shift(): return lax.ppermute(v, AXES, pairs)  28.1 us
    all_gather x1, blocking collectives, body(): back = lax.all_gather(back, 'mp', axis=0)  20.7 us
    all_gather x1, blocking collectives, body(): both = lax.all_gather(both, 'dp', axis=0, tiled=True)  16.2 us
    unnamed x39, local copies, waits for them, and re-layouts  8.12 us
    dot_general x1, matrix products, body(): lax.dot_general(kv_grad, weight, contracted_columns, preferred_element_ty...  6.29 us
  transfers between devices with their start and end apart: 34, of which 5 were waited for; matrix products, arithmetic and copies ran while one was open for 7% of the time, Pallas kernels for 0%

profile of v2, /device:TPU:1, one launch (start us, length us, event | category | flops | bytes accessed | tf_op | source)
XLA Modules:
  0.0 265.2 jit_solution(4343892960024187298)
XLA Ops:
  1.7 11.9 %collective-permute-start = (bf16[8,8192]{1,0:T(8,128)(2,1)S(1)}, bf16[8,8192]{1,0:T(8,128)(2,1)S(1)}, u32[]{:S(2)}, u32[]{:S(2)}) collective-permute-start(bf16[8,8192]{1,0:T(8,128)(2,1)S(1)} %bitcast.116), channel_id=1, source_target_pairs={{0,387},{1,384},{2,385},{3,386},{4,391},{5,388},{6,389},{7,390},{8... | collective-permute-start | bytes 393224 | tf_op jit(solution)/shard_map/ppermute | solution.py:38
  13.6 3.1 %collective-permute-start.1 = (bf16[8,8192]{1,0:T(8,128)(2,1)S(1)}, bf16[8,8192]{1,0:T(8,128)(2,1)S(1)}, u32[]{:S(2)}, u32[]{:S(2)}) collective-permute-start(bf16[8,8192]{1,0:T(8,128)(2,1)S(1)} %bitcast.117), channel_id=1, source_target_pairs={{0,256},{1,257},{2,258},{3,259},{4,263},{5,260},{6,261},{7,262},{8... | collective-permute-start | bytes 393224 | tf_op jit(solution)/shard_map/ppermute | solution.py:38
  16.7 2.6 collective-permute-start.2
  22.8 4.7 %collective-permute-start.7 = (bf16[1024,512]{1,0:T(8,128)(2,1)S(1)}, bf16[1024,512]{1,0:T(8,128)(2,1)}, u32[]{:S(2)}, u32[]{:S(2)}) collective-permute-start(bf16[1024,512]{1,0:T(8,128)(2,1)S(1)} %bitcast.111), channel_id=1, source_target_pairs={{0,24},{1,25},{2,26},{3,27},{4,28},{5,29},{6,30},{7,31},{8,0},{9,1... | collective-permute-start | bytes 3145736 | tf_op jit(solution)/shard_map/ppermute | solution.py:38
  37.9 4.5 %collective-permute-start.3 = (bf16[32,8192]{1,0:T(8,128)(2,1)S(1)}, bf16[32,8192]{1,0:T(8,128)(2,1)S(1)}, u32[]{:S(2)}, u32[]{:S(2)}) collective-permute-start(bf16[32,8192]{1,0:T(8,128)(2,1)S(1)} %pad_maximum_fusion.1), channel_id=1, source_target_pairs={{0,96},{1,97},{2,98},{3,99},{4,100},{5,101},{6,102},{7,103},{8,104... | collective-permute-start | bytes 1572872 | tf_op jit(solution)/shard_map/ppermute | solution.py:38
  42.4 2.4 collective-permute-start.4
  45.8 7.9 %collective-permute-done.3 = bf16[32,8192]{1,0:T(8,128)(2,1)S(1)} collective-permute-done((bf16[32,8192]{1,0:T(8,128)(2,1)S(1)}, bf16[32,8192]{1,0:T(8,128)(2,1)S(1)}, u32[]{:S(2)}, u32[]{:S(2)}) %collective-permute-start.3) | collective-permute-done | bytes 524320 | tf_op jit(solution)/shard_map/ppermute | solution.py:38
  55.8 2.5 collective-permute-done.4
  58.3 7.7 %collective-permute-done.5 = bf16[32,8192]{1,0:T(8,128)(2,1)S(1)} collective-permute-done((bf16[32,8192]{1,0:T(8,128)(2,1)S(1)}, bf16[32,8192]{1,0:T(8,128)(2,1)S(1)}, u32[]{:S(2)}, u32[]{:S(2)}) %collective-permute-start.5) | collective-permute-done | bytes 524320 | tf_op jit(solution)/shard_map/ppermute | solution.py:38
  66.5 23.5 %collective-permute-start.15 = (f32[128,128]{0,1:T(8,128)S(1)}, f32[128,128]{0,1:T(8,128)S(1)}, u32[]{:S(2)}, u32[]{:S(2)}) collective-permute-start(f32[128,128]{0,1:T(8,128)S(1)} %fusion.24), channel_id=1, source_target_pairs={{0,2},{1,3},{2,0},{3,1},{4,6},{5,7},{6,4},{7,5},{8,10},{9,11},{10,... | collective-permute-start | bytes 196616 | tf_op jit(solution)/shard_map/ppermute | solution.py:38
  90.0 3.7 %collective-permute-start.16 = (f32[128,128]{0,1:T(8,128)S(1)}, f32[128,128]{0,1:T(8,128)S(1)}, u32[]{:S(2)}, u32[]{:S(2)}) collective-permute-start(f32[128,128]{0,1:T(8,128)S(1)} %fusion.24), channel_id=1, source_target_pairs={{0,1},{1,2},{2,3},{3,0},{4,5},{5,6},{6,7},{7,4},{8,9},{9,10},{10,1... | collective-permute-start | bytes 196616 | tf_op jit(solution)/shard_map/ppermute | solution.py:38
  93.7 6.8 %collective-permute-start.17 = (f32[128,128]{0,1:T(8,128)S(1)}, f32[128,128]{0,1:T(8,128)S(1)}, u32[]{:S(2)}, u32[]{:S(2)}) collective-permute-start(f32[128,128]{0,1:T(8,128)S(1)} %fusion.24), channel_id=1, source_target_pairs={{0,3},{1,0},{2,1},{3,2},{4,7},{5,4},{6,5},{7,6},{8,11},{9,8},{10,9... | collective-permute-start | bytes 196616 | tf_op jit(solution)/shard_map/ppermute | solution.py:38
  100.5 7.1 %collective-permute-start.8 = (bf16[1024,512]{1,0:T(8,128)(2,1)}, bf16[1024,512]{1,0:T(8,128)(2,1)S(1)}, u32[]{:S(2)}, u32[]{:S(2)}) collective-permute-start(bf16[1024,512]{1,0:T(8,128)(2,1)} %collective-permute-done.7), channel_id=1, source_target_pairs={{0,4},{1,5},{2,6},{3,7},{4,0},{5,1},{6,2},{7,3},{8,12},{9,13},{10,... | collective-permute-start | bytes 3145736 | tf_op jit(solution)/shard_map/ppermute | solution.py:38
  110.7 3.4 %collective-permute-start.11 = (bf16[512,512]{1,0:T(8,128)(2,1)S(1)}, bf16[512,512]{1,0:T(8,128)(2,1)S(1)}, u32[]{:S(2)}, u32[]{:S(2)}) collective-permute-start(bf16[512,512]{1,0:T(8,128)(2,1)S(1)} %slice.102), channel_id=1, source_target_pairs={{0,8},{1,9},{2,10},{3,11},{4,12},{5,13},{6,14},{7,15},{8,16},{9,17... | collective-permute-start | bytes 1572872 | tf_op jit(solution)/shard_map/ppermute | solution.py:38
  114.5 4.3 %collective-permute-start.14 = (bf16[1024,512]{1,0:T(8,128)(2,1)S(1)}, bf16[1024,512]{1,0:T(8,128)(2,1)S(1)}, u32[]{:S(2)}, u32[]{:S(2)}) collective-permute-start(bf16[1024,512]{1,0:T(8,128)(2,1)S(1)} %collective-permute-done.10), channel_id=1, source_target_pairs={{0,4},{1,5},{2,6},{3,7},{4,0},{5,1},{6,2},{7,3},{8,12},{9,13},{10,... | collective-permute-start | bytes 3145736 | tf_op jit(solution)/shard_map/ppermute | solution.py:38
  122.3 4.5 %collective-permute-start.12 = (bf16[512,512]{1,0:T(8,128)(2,1)S(1)}, bf16[512,512]{1,0:T(8,128)(2,1)S(1)}, u32[]{:S(2)}, u32[]{:S(2)}) collective-permute-start(bf16[512,512]{1,0:T(8,128)(2,1)S(1)} %collective-permute-done.9), channel_id=1, source_target_pairs={{0,4},{1,5},{2,6},{3,7},{4,0},{5,1},{6,2},{7,3},{8,12},{9,13},{10,... | collective-permute-start | bytes 1572872 | tf_op jit(solution)/shard_map/ppermute | solution.py:38
  126.9 3.2 %collective-permute-start.13 = (bf16[512,512]{1,0:T(8,128)(2,1)S(1)}, bf16[512,512]{1,0:T(8,128)(2,1)S(1)}, u32[]{:S(2)}, u32[]{:S(2)}) collective-permute-start(bf16[512,512]{1,0:T(8,128)(2,1)S(1)} %collective-permute-done.11), channel_id=1, source_target_pairs={{0,4},{1,5},{2,6},{3,7},{4,0},{5,1},{6,2},{7,3},{8,12},{9,13},{10,... | collective-permute-start | bytes 1572872 | tf_op jit(solution)/shard_map/ppermute | solution.py:38
  140.5 6.3 %convolution_convert_fusion = bf16[128,8192]{1,0:T(8,128)(2,1)S(1)} fusion(bf16[8192,512]{1,0:T(8,128)(2,1)} %copy-done, bf16[128,256]{0,1:T(8,128)(2,1)S(1)} %bitcast.124, bf16[128,256]{0,1:T(8,128)(2,1)S(1)} %bitcast.128), kind=kOutput, calls=%fused_computation.2 | convolution fusion | flops 1075052544 | bytes 10616832 | tf_op jit(solution)/shard_map/dot_general | solution.py:162
  147.1 20.7 %all_gather.7 = f32[4,128,128]{2,1,0:T(8,128)S(1)} all-gather(f32[1,128,128]{2,1,0:T(8,128)S(1)} %copy.27), channel_id=1, replica_groups=mesh['segment'=16,'dp'=8,'mp'=4] {'mp'}, dimensions={0}, use_global_device_ids=true | all-gather | bytes 327680 | tf_op jit(solution)/shard_map/all_gather | solution.py:171
  174.2 5.7 %collective-permute-start.23 = (bf16[32,8192]{1,0:T(8,128)(2,1)}, bf16[32,8192]{1,0:T(8,128)(2,1)}, u32[]{:S(2)}, u32[]{:S(2)}) collective-permute-start(bf16[32,8192]{1,0:T(8,128)(2,1)} %get-tuple-element.5), channel_id=1, source_target_pairs={{0,64},{1,65},{2,66},{3,67},{4,68},{5,69},{6,70},{7,71},{8,72},{9,... | collective-permute-start | bytes 1572872 | tf_op jit(solution)/shard_map/ppermute | solution.py:38
  182.6 3.4 %collective-permute-start.25 = (bf16[32,2048]{1,0:T(8,128)(2,1)}, bf16[32,2048]{1,0:T(8,128)(2,1)}, u32[]{:S(2)}, u32[]{:S(2)}) collective-permute-start(bf16[32,2048]{1,0:T(8,128)(2,1)} %get-tuple-element.14), channel_id=1, source_target_pairs={{0,32},{1,33},{2,34},{3,35},{4,36},{5,37},{6,38},{7,39},{8,40},{9,... | collective-permute-start | bytes 393224 | tf_op jit(solution)/shard_map/ppermute | solution.py:38
  188.3 4.3 %collective-permute-start.27 = (bf16[32,2048]{1,0:T(8,128)(2,1)S(1)}, bf16[32,2048]{1,0:T(8,128)(2,1)S(1)}, u32[]{:S(2)}, u32[]{:S(2)}) collective-permute-start(bf16[32,2048]{1,0:T(8,128)(2,1)S(1)} %get-tuple-element.15), channel_id=1, source_target_pairs={{0,96},{1,97},{2,98},{3,99},{4,100},{5,101},{6,102},{7,103},{8,104... | collective-permute-start | bytes 393224 | tf_op jit(solution)/shard_map/ppermute | solution.py:38
  192.6 7.7 %collective-permute-done.23 = bf16[32,8192]{1,0:T(8,128)(2,1)} collective-permute-done((bf16[32,8192]{1,0:T(8,128)(2,1)}, bf16[32,8192]{1,0:T(8,128)(2,1)}, u32[]{:S(2)}, u32[]{:S(2)}) %collective-permute-start.23) | collective-permute-done | bytes 524320 | tf_op jit(solution)/shard_map/ppermute | solution.py:38
  200.4 5.8 %collective-permute-start.18 = (f32[4,288,128]{2,1,0:T(8,128)S(1)}, f32[4,288,128]{2,1,0:T(8,128)S(1)}, u32[]{:S(2)}, u32[]{:S(2)}) collective-permute-start(f32[4,288,128]{2,1,0:T(8,128)S(1)} %dynamic-slice_bitcast_fusion), channel_id=1, source_target_pairs={{0,4},{1,5},{2,6},{3,7},{4,0},{5,1},{6,2},{7,3},{8,12},{9,13},{10,... | collective-permute-start | bytes 1769480 | tf_op jit(solution)/shard_map/ppermute | solution.py:38
  211.0 7.2 %collective-permute-start.29 = (bf16[8,8192]{1,0:T(8,128)(2,1)S(1)}, bf16[8,8192]{1,0:T(8,128)(2,1)S(1)}, u32[]{:S(2)}, u32[]{:S(2)}) collective-permute-start(bf16[8,8192]{1,0:T(8,128)(2,1)S(1)} %get-tuple-element.13), channel_id=1, source_target_pairs={{0,256},{1,257},{2,258},{3,259},{4,263},{5,260},{6,261},{7,262},{8... | collective-permute-start | bytes 393224 | tf_op jit(solution)/shard_map/ppermute | solution.py:38
  218.1 3.4 %collective-permute-start.30 = (bf16[8,8192]{1,0:T(8,128)(2,1)S(1)}, bf16[8,8192]{1,0:T(8,128)(2,1)S(1)}, u32[]{:S(2)}, u32[]{:S(2)}) collective-permute-start(bf16[8,8192]{1,0:T(8,128)(2,1)S(1)} %get-tuple-element.12), channel_id=1, source_target_pairs={{0,387},{1,384},{2,385},{3,386},{4,391},{5,388},{6,389},{7,390},{8... | collective-permute-start | bytes 393224 | tf_op jit(solution)/shard_map/ppermute | solution.py:38
  223.6 3.1 %collective-permute-start.20 = (f32[288,128]{1,0:T(8,128)S(1)}, f32[288,128]{1,0:T(8,128)S(1)}, u32[]{:S(2)}, u32[]{:S(2)}) collective-permute-start(f32[288,128]{1,0:T(8,128)S(1)} %get-tuple-element.10), channel_id=1, source_target_pairs={{0,16},{1,17},{2,18},{3,19},{4,20},{5,21},{6,22},{7,23},{8,24},{9,... | collective-permute-start | bytes 442376 | tf_op jit(solution)/shard_map/ppermute | solution.py:38
  226.7 3.7 %collective-permute-start.21 = (f32[288,128]{1,0:T(8,128)S(1)}, f32[288,128]{1,0:T(8,128)S(1)}, u32[]{:S(2)}, u32[]{:S(2)}) collective-permute-start(f32[288,128]{1,0:T(8,128)S(1)} %get-tuple-element.9), channel_id=1, source_target_pairs={{0,24},{1,25},{2,26},{3,27},{4,28},{5,29},{6,30},{7,31},{8,0},{9,1... | collective-permute-start | bytes 442376 | tf_op jit(solution)/shard_map/ppermute | solution.py:38
  230.4 6.8 %collective-permute-start.31 = (bf16[8,8192]{1,0:T(8,128)(2,1)S(1)}, bf16[8,8192]{1,0:T(8,128)(2,1)S(1)}, u32[]{:S(2)}, u32[]{:S(2)}) collective-permute-start(bf16[8,8192]{1,0:T(8,128)(2,1)S(1)} %fusion.30), channel_id=1, source_target_pairs={{0,2},{1,3},{2,0},{3,1},{4,6},{5,7},{6,4},{7,5},{8,10},{9,11},{10,... | collective-permute-start | bytes 393224 | tf_op jit(solution)/shard_map/ppermute | solution.py:38
  237.2 3.4 %collective-permute-start.32 = (bf16[8,8192]{1,0:T(8,128)(2,1)S(1)}, bf16[8,8192]{1,0:T(8,128)(2,1)S(1)}, u32[]{:S(2)}, u32[]{:S(2)}) collective-permute-start(bf16[8,8192]{1,0:T(8,128)(2,1)S(1)} %fusion.30), channel_id=1, source_target_pairs={{0,1},{1,2},{2,3},{3,0},{4,5},{5,6},{6,7},{7,4},{8,9},{9,10},{10,1... | collective-permute-start | bytes 393224 | tf_op jit(solution)/shard_map/ppermute | solution.py:38
  240.6 5.8 %collective-permute-start.33 = (bf16[8,8192]{1,0:T(8,128)(2,1)S(1)}, bf16[8,8192]{1,0:T(8,128)(2,1)S(1)}, u32[]{:S(2)}, u32[]{:S(2)}) collective-permute-start(bf16[8,8192]{1,0:T(8,128)(2,1)S(1)} %fusion.30), channel_id=1, source_target_pairs={{0,3},{1,0},{2,1},{3,2},{4,7},{5,4},{6,5},{7,6},{8,11},{9,8},{10,9... | collective-permute-start | bytes 393224 | tf_op jit(solution)/shard_map/ppermute | solution.py:38
  246.5 16.2 %all_gather.8 = bf16[2304,128]{1,0:T(8,128)(2,1)S(1)} all-gather(bf16[288,128]{1,0:T(8,128)(2,1)S(1)} %fusion.34), channel_id=1, replica_groups=mesh['segment'=16,'dp'=8,'mp'=4] {'dp'}, dimensions={0}, use_global_device_ids=true | all-gather | bytes 663552 | tf_op jit(solution)/shard_map/all_gather | solution.py:209
  (133 shorter events, 54.8 us)
Async XLA Ops:
  1.7 33.3 %collective-permute-start = (bf16[8,8192]{1,0:T(8,128)(2,1)S(1)}, bf16[8,8192]{1,0:T(8,128)(2,1)S(1)}, u32[]{:S(2)}, u32[]{:S(2)}) collective-permute-start(bf16[8,8192]{1,0:T(8,128)(2,1)S(1)} %bitcast.116), channel_id=1, source_target_pairs={{0,387},{1,384},{2,385},{3,386},{4,391},{5,388},{6,389},{7,390},{8... | collective-permute-start | bytes 393224 | tf_op jit(solution)/shard_map/ppermute | solution.py:38
  13.6 23.3 %collective-permute-start.1 = (bf16[8,8192]{1,0:T(8,128)(2,1)S(1)}, bf16[8,8192]{1,0:T(8,128)(2,1)S(1)}, u32[]{:S(2)}, u32[]{:S(2)}) collective-permute-start(bf16[8,8192]{1,0:T(8,128)(2,1)S(1)} %bitcast.117), channel_id=1, source_target_pairs={{0,256},{1,257},{2,258},{3,259},{4,263},{5,260},{6,261},{7,262},{8... | collective-permute-start | bytes 393224 | tf_op jit(solution)/shard_map/ppermute | solution.py:38
  16.7 20.2 %collective-permute-start.2 = (bf16[8,8192]{1,0:T(8,128)(2,1)S(1)}, bf16[8,8192]{1,0:T(8,128)(2,1)}, u32[]{:S(2)}, u32[]{:S(2)}) collective-permute-start(bf16[8,8192]{1,0:T(8,128)(2,1)S(1)} %bitcast.118), channel_id=1, source_target_pairs={{0,128},{1,129},{2,130},{3,131},{4,132},{5,133},{6,134},{7,135},{8... | collective-permute-start | bytes 393224 | tf_op jit(solution)/shard_map/ppermute | solution.py:38
  20.8 98.0 %collective-permute-start.6 = (bf16[1024,512]{1,0:T(8,128)(2,1)S(1)}, bf16[1024,512]{1,0:T(8,128)(2,1)}, u32[]{:S(2)}, u32[]{:S(2)}) collective-permute-start(bf16[1024,512]{1,0:T(8,128)(2,1)S(1)} %bitcast.110), channel_id=1, source_target_pairs={{0,4},{1,5},{2,6},{3,7},{4,0},{5,1},{6,2},{7,3},{8,12},{9,13},{10,... | collective-permute-start | bytes 3145736 | tf_op jit(solution)/shard_map/ppermute | solution.py:38
  22.8 77.7 %collective-permute-start.7 = (bf16[1024,512]{1,0:T(8,128)(2,1)S(1)}, bf16[1024,512]{1,0:T(8,128)(2,1)}, u32[]{:S(2)}, u32[]{:S(2)}) collective-permute-start(bf16[1024,512]{1,0:T(8,128)(2,1)S(1)} %bitcast.111), channel_id=1, source_target_pairs={{0,24},{1,25},{2,26},{3,27},{4,28},{5,29},{6,30},{7,31},{8,0},{9,1... | collective-permute-start | bytes 3145736 | tf_op jit(solution)/shard_map/ppermute | solution.py:38
  35.0 75.7 %collective-permute-start.10 = (bf16[1024,512]{1,0:T(8,128)(2,1)S(1)}, bf16[1024,512]{1,0:T(8,128)(2,1)S(1)}, u32[]{:S(2)}, u32[]{:S(2)}) collective-permute-start(bf16[1024,512]{1,0:T(8,128)(2,1)S(1)} %bitcast.113), channel_id=1, source_target_pairs={{0,8},{1,9},{2,10},{3,11},{4,12},{5,13},{6,14},{7,15},{8,16},{9,17... | collective-permute-start | bytes 3145736 | tf_op jit(solution)/shard_map/ppermute | solution.py:38
  37.9 15.8 %collective-permute-start.3 = (bf16[32,8192]{1,0:T(8,128)(2,1)S(1)}, bf16[32,8192]{1,0:T(8,128)(2,1)S(1)}, u32[]{:S(2)}, u32[]{:S(2)}) collective-permute-start(bf16[32,8192]{1,0:T(8,128)(2,1)S(1)} %pad_maximum_fusion.1), channel_id=1, source_target_pairs={{0,96},{1,97},{2,98},{3,99},{4,100},{5,101},{6,102},{7,103},{8,104... | collective-permute-start | bytes 1572872 | tf_op jit(solution)/shard_map/ppermute | solution.py:38
  42.4 15.8 %collective-permute-start.4 = (bf16[32,8192]{1,0:T(8,128)(2,1)S(1)}, bf16[32,8192]{1,0:T(8,128)(2,1)S(1)}, u32[]{:S(2)}, u32[]{:S(2)}) collective-permute-start(bf16[32,8192]{1,0:T(8,128)(2,1)S(1)} %pad_maximum_fusion.1), channel_id=1, source_target_pairs={{0,64},{1,65},{2,66},{3,67},{4,68},{5,69},{6,70},{7,71},{8,72},{9,... | collective-permute-start | bytes 1572872 | tf_op jit(solution)/shard_map/ppermute | solution.py:38
  53.7 12.3 %collective-permute-start.5 = (bf16[32,8192]{1,0:T(8,128)(2,1)S(1)}, bf16[32,8192]{1,0:T(8,128)(2,1)S(1)}, u32[]{:S(2)}, u32[]{:S(2)}) collective-permute-start(bf16[32,8192]{1,0:T(8,128)(2,1)S(1)} %pad_maximum_fusion.1), channel_id=1, source_target_pairs={{0,32},{1,33},{2,34},{3,35},{4,36},{5,37},{6,38},{7,39},{8,40},{9,... | collective-permute-start | bytes 1572872 | tf_op jit(solution)/shard_map/ppermute | solution.py:38
  66.5 27.2 %collective-permute-start.15 = (f32[128,128]{0,1:T(8,128)S(1)}, f32[128,128]{0,1:T(8,128)S(1)}, u32[]{:S(2)}, u32[]{:S(2)}) collective-permute-start(f32[128,128]{0,1:T(8,128)S(1)} %fusion.24), channel_id=1, source_target_pairs={{0,2},{1,3},{2,0},{3,1},{4,6},{5,7},{6,4},{7,5},{8,10},{9,11},{10,... | collective-permute-start | bytes 196616 | tf_op jit(solution)/shard_map/ppermute | solution.py:38
  90.0 17.6 %collective-permute-start.16 = (f32[128,128]{0,1:T(8,128)S(1)}, f32[128,128]{0,1:T(8,128)S(1)}, u32[]{:S(2)}, u32[]{:S(2)}) collective-permute-start(f32[128,128]{0,1:T(8,128)S(1)} %fusion.24), channel_id=1, source_target_pairs={{0,1},{1,2},{2,3},{3,0},{4,5},{5,6},{6,7},{7,4},{8,9},{9,10},{10,1... | collective-permute-start | bytes 196616 | tf_op jit(solution)/shard_map/ppermute | solution.py:38
  93.7 13.9 %collective-permute-start.17 = (f32[128,128]{0,1:T(8,128)S(1)}, f32[128,128]{0,1:T(8,128)S(1)}, u32[]{:S(2)}, u32[]{:S(2)}) collective-permute-start(f32[128,128]{0,1:T(8,128)S(1)} %fusion.24), channel_id=1, source_target_pairs={{0,3},{1,0},{2,1},{3,2},{4,7},{5,4},{6,5},{7,6},{8,11},{9,8},{10,9... | collective-permute-start | bytes 196616 | tf_op jit(solution)/shard_map/ppermute | solution.py:38
  100.5 30.9 %collective-permute-start.8 = (bf16[1024,512]{1,0:T(8,128)(2,1)}, bf16[1024,512]{1,0:T(8,128)(2,1)S(1)}, u32[]{:S(2)}, u32[]{:S(2)}) collective-permute-start(bf16[1024,512]{1,0:T(8,128)(2,1)} %collective-permute-done.7), channel_id=1, source_target_pairs={{0,4},{1,5},{2,6},{3,7},{4,0},{5,1},{6,2},{7,3},{8,12},{9,13},{10,... | collective-permute-start | bytes 3145736 | tf_op jit(solution)/shard_map/ppermute | solution.py:38
  108.8 13.6 %collective-permute-start.9 = (bf16[512,512]{1,0:T(8,128)(2,1)S(1)}, bf16[512,512]{1,0:T(8,128)(2,1)S(1)}, u32[]{:S(2)}, u32[]{:S(2)}) collective-permute-start(bf16[512,512]{1,0:T(8,128)(2,1)S(1)} %slice.101), channel_id=1, source_target_pairs={{0,24},{1,25},{2,26},{3,27},{4,28},{5,29},{6,30},{7,31},{8,0},{9,1... | collective-permute-start | bytes 1572872 | tf_op jit(solution)/shard_map/ppermute | solution.py:38
  110.7 16.2 %collective-permute-start.11 = (bf16[512,512]{1,0:T(8,128)(2,1)S(1)}, bf16[512,512]{1,0:T(8,128)(2,1)S(1)}, u32[]{:S(2)}, u32[]{:S(2)}) collective-permute-start(bf16[512,512]{1,0:T(8,128)(2,1)S(1)} %slice.102), channel_id=1, source_target_pairs={{0,8},{1,9},{2,10},{3,11},{4,12},{5,13},{6,14},{7,15},{8,16},{9,17... | collective-permute-start | bytes 1572872 | tf_op jit(solution)/shard_map/ppermute | solution.py:38
  114.5 17.2 %collective-permute-start.14 = (bf16[1024,512]{1,0:T(8,128)(2,1)S(1)}, bf16[1024,512]{1,0:T(8,128)(2,1)S(1)}, u32[]{:S(2)}, u32[]{:S(2)}) collective-permute-start(bf16[1024,512]{1,0:T(8,128)(2,1)S(1)} %collective-permute-done.10), channel_id=1, source_target_pairs={{0,4},{1,5},{2,6},{3,7},{4,0},{5,1},{6,2},{7,3},{8,12},{9,13},{10,... | collective-permute-start | bytes 3145736 | tf_op jit(solution)/shard_map/ppermute | solution.py:38
  172.3 16.0 %collective-permute-start.22 = (bf16[32,8192]{1,0:T(8,128)(2,1)}, bf16[32,8192]{1,0:T(8,128)(2,1)}, u32[]{:S(2)}, u32[]{:S(2)}) collective-permute-start(bf16[32,8192]{1,0:T(8,128)(2,1)} %get-tuple-element.3), channel_id=1, source_target_pairs={{0,32},{1,33},{2,34},{3,35},{4,36},{5,37},{6,38},{7,39},{8,40},{9,... | collective-permute-start | bytes 1572872 | tf_op jit(solution)/shard_map/ppermute | solution.py:38
  174.2 26.1 %collective-permute-start.23 = (bf16[32,8192]{1,0:T(8,128)(2,1)}, bf16[32,8192]{1,0:T(8,128)(2,1)}, u32[]{:S(2)}, u32[]{:S(2)}) collective-permute-start(bf16[32,8192]{1,0:T(8,128)(2,1)} %get-tuple-element.5), channel_id=1, source_target_pairs={{0,64},{1,65},{2,66},{3,67},{4,68},{5,69},{6,70},{7,71},{8,72},{9,... | collective-permute-start | bytes 1572872 | tf_op jit(solution)/shard_map/ppermute | solution.py:38
  180.0 26.2 %collective-permute-start.24 = (bf16[32,8192]{1,0:T(8,128)(2,1)}, bf16[32,8192]{1,0:T(8,128)(2,1)}, u32[]{:S(2)}, u32[]{:S(2)}) collective-permute-start(bf16[32,8192]{1,0:T(8,128)(2,1)} %get-tuple-element.4), channel_id=1, source_target_pairs={{0,96},{1,97},{2,98},{3,99},{4,100},{5,101},{6,102},{7,103},{8,104... | collective-permute-start | bytes 1572872 | tf_op jit(solution)/shard_map/ppermute | solution.py:38
  182.6 25.1 %collective-permute-start.25 = (bf16[32,2048]{1,0:T(8,128)(2,1)}, bf16[32,2048]{1,0:T(8,128)(2,1)}, u32[]{:S(2)}, u32[]{:S(2)}) collective-permute-start(bf16[32,2048]{1,0:T(8,128)(2,1)} %get-tuple-element.14), channel_id=1, source_target_pairs={{0,32},{1,33},{2,34},{3,35},{4,36},{5,37},{6,38},{7,39},{8,40},{9,... | collective-permute-start | bytes 393224 | tf_op jit(solution)/shard_map/ppermute | solution.py:38
  186.0 21.8 %collective-permute-start.26 = (bf16[32,2048]{1,0:T(8,128)(2,1)}, bf16[32,2048]{1,0:T(8,128)(2,1)}, u32[]{:S(2)}, u32[]{:S(2)}) collective-permute-start(bf16[32,2048]{1,0:T(8,128)(2,1)} %get-tuple-element.16), channel_id=1, source_target_pairs={{0,64},{1,65},{2,66},{3,67},{4,68},{5,69},{6,70},{7,71},{8,72},{9,... | collective-permute-start | bytes 393224 | tf_op jit(solution)/shard_map/ppermute | solution.py:38
  188.3 19.5 %collective-permute-start.27 = (bf16[32,2048]{1,0:T(8,128)(2,1)S(1)}, bf16[32,2048]{1,0:T(8,128)(2,1)S(1)}, u32[]{:S(2)}, u32[]{:S(2)}) collective-permute-start(bf16[32,2048]{1,0:T(8,128)(2,1)S(1)} %get-tuple-element.15), channel_id=1, source_target_pairs={{0,96},{1,97},{2,98},{3,99},{4,100},{5,101},{6,102},{7,103},{8,104... | collective-permute-start | bytes 393224 | tf_op jit(solution)/shard_map/ppermute | solution.py:38
  200.4 21.2 %collective-permute-start.18 = (f32[4,288,128]{2,1,0:T(8,128)S(1)}, f32[4,288,128]{2,1,0:T(8,128)S(1)}, u32[]{:S(2)}, u32[]{:S(2)}) collective-permute-start(f32[4,288,128]{2,1,0:T(8,128)S(1)} %dynamic-slice_bitcast_fusion), channel_id=1, source_target_pairs={{0,4},{1,5},{2,6},{3,7},{4,0},{5,1},{6,2},{7,3},{8,12},{9,13},{10,... | collective-permute-start | bytes 1769480 | tf_op jit(solution)/shard_map/ppermute | solution.py:38
  209.0 17.6 %collective-permute-start.28 = (bf16[8,8192]{1,0:T(8,128)(2,1)S(1)}, bf16[8,8192]{1,0:T(8,128)(2,1)S(1)}, u32[]{:S(2)}, u32[]{:S(2)}) collective-permute-start(bf16[8,8192]{1,0:T(8,128)(2,1)S(1)} %get-tuple-element.11), channel_id=1, source_target_pairs={{0,128},{1,129},{2,130},{3,131},{4,132},{5,133},{6,134},{7,135},{8... | collective-permute-start | bytes 393224 | tf_op jit(solution)/shard_map/ppermute | solution.py:38
  211.0 19.4 %collective-permute-start.29 = (bf16[8,8192]{1,0:T(8,128)(2,1)S(1)}, bf16[8,8192]{1,0:T(8,128)(2,1)S(1)}, u32[]{:S(2)}, u32[]{:S(2)}) collective-permute-start(bf16[8,8192]{1,0:T(8,128)(2,1)S(1)} %get-tuple-element.13), channel_id=1, source_target_pairs={{0,256},{1,257},{2,258},{3,259},{4,263},{5,260},{6,261},{7,262},{8... | collective-permute-start | bytes 393224 | tf_op jit(solution)/shard_map/ppermute | solution.py:38
  218.1 12.2 %collective-permute-start.30 = (bf16[8,8192]{1,0:T(8,128)(2,1)S(1)}, bf16[8,8192]{1,0:T(8,128)(2,1)S(1)}, u32[]{:S(2)}, u32[]{:S(2)}) collective-permute-start(bf16[8,8192]{1,0:T(8,128)(2,1)S(1)} %get-tuple-element.12), channel_id=1, source_target_pairs={{0,387},{1,384},{2,385},{3,386},{4,391},{5,388},{6,389},{7,390},{8... | collective-permute-start | bytes 393224 | tf_op jit(solution)/shard_map/ppermute | solution.py:38
  221.6 19.0 %collective-permute-start.19 = (f32[288,128]{1,0:T(8,128)S(1)}, f32[288,128]{1,0:T(8,128)S(1)}, u32[]{:S(2)}, u32[]{:S(2)}) collective-permute-start(f32[288,128]{1,0:T(8,128)S(1)} %get-tuple-element.8), channel_id=1, source_target_pairs={{0,8},{1,9},{2,10},{3,11},{4,12},{5,13},{6,14},{7,15},{8,16},{9,17... | collective-permute-start | bytes 442376 | tf_op jit(solution)/shard_map/ppermute | solution.py:38
  223.6 22.8 %collective-permute-start.20 = (f32[288,128]{1,0:T(8,128)S(1)}, f32[288,128]{1,0:T(8,128)S(1)}, u32[]{:S(2)}, u32[]{:S(2)}) collective-permute-start(f32[288,128]{1,0:T(8,128)S(1)} %get-tuple-element.10), channel_id=1, source_target_pairs={{0,16},{1,17},{2,18},{3,19},{4,20},{5,21},{6,22},{7,23},{8,24},{9,... | collective-permute-start | bytes 442376 | tf_op jit(solution)/shard_map/ppermute | solution.py:38
  226.7 19.8 %collective-permute-start.21 = (f32[288,128]{1,0:T(8,128)S(1)}, f32[288,128]{1,0:T(8,128)S(1)}, u32[]{:S(2)}, u32[]{:S(2)}) collective-permute-start(f32[288,128]{1,0:T(8,128)S(1)} %get-tuple-element.9), channel_id=1, source_target_pairs={{0,24},{1,25},{2,26},{3,27},{4,28},{5,29},{6,30},{7,31},{8,0},{9,1... | collective-permute-start | bytes 442376 | tf_op jit(solution)/shard_map/ppermute | solution.py:38
  230.4 33.8 %collective-permute-start.31 = (bf16[8,8192]{1,0:T(8,128)(2,1)S(1)}, bf16[8,8192]{1,0:T(8,128)(2,1)S(1)}, u32[]{:S(2)}, u32[]{:S(2)}) collective-permute-start(bf16[8,8192]{1,0:T(8,128)(2,1)S(1)} %fusion.30), channel_id=1, source_target_pairs={{0,2},{1,3},{2,0},{3,1},{4,6},{5,7},{6,4},{7,5},{8,10},{9,11},{10,... | collective-permute-start | bytes 393224 | tf_op jit(solution)/shard_map/ppermute | solution.py:38
  237.2 27.0 %collective-permute-start.32 = (bf16[8,8192]{1,0:T(8,128)(2,1)S(1)}, bf16[8,8192]{1,0:T(8,128)(2,1)S(1)}, u32[]{:S(2)}, u32[]{:S(2)}) collective-permute-start(bf16[8,8192]{1,0:T(8,128)(2,1)S(1)} %fusion.30), channel_id=1, source_target_pairs={{0,1},{1,2},{2,3},{3,0},{4,5},{5,6},{6,7},{7,4},{8,9},{9,10},{10,1... | collective-permute-start | bytes 393224 | tf_op jit(solution)/shard_map/ppermute | solution.py:38
  240.6 23.6 %collective-permute-start.33 = (bf16[8,8192]{1,0:T(8,128)(2,1)S(1)}, bf16[8,8192]{1,0:T(8,128)(2,1)S(1)}, u32[]{:S(2)}, u32[]{:S(2)}) collective-permute-start(bf16[8,8192]{1,0:T(8,128)(2,1)S(1)} %fusion.30), channel_id=1, source_target_pairs={{0,3},{1,0},{2,1},{3,2},{4,7},{5,4},{6,5},{7,6},{8,11},{9,8},{10,9... | collective-permute-start | bytes 393224 | tf_op jit(solution)/shard_map/ppermute | solution.py:38
  (13 other events, 287.6 us)

commit v3 on v2

v3 whole, which is shorter than its diff:
```python
import jax
import jax.numpy as jnp
from jax import lax
from jax.experimental import pallas as pl
from jax.sharding import PartitionSpec as P


HD = 128
TILES = 4
SIDE = 4
CORES = 2

adapter_scale = 2.0
contract_rows = (((0,), (0,)), ((), ()))
contracted_columns = (((1,), (1,)), ((), ()))
f32 = jnp.float32
bf16 = jnp.bfloat16
AXES = ("segment", "dp", "mp")


def image_grad_kernel(kv_ref, back_ref, weight_ref, down_ref, own_ref, *away_refs):
    down = down_ref[...].reshape(weight_ref.shape[0], back_ref.shape[1])
    total = lax.dot_general(kv_ref[...], weight_ref[...], contracted_columns, preferred_element_type=f32)
    total += lax.dot_general(back_ref[...], down, contracted_columns, preferred_element_type=f32)
    block = own_ref.shape[0]
    own_ref[...] = total[:block]
    for i, ref in enumerate(away_refs):
        ref[...] = total[(i + 1) * block : (i + 2) * block].astype(bf16)


def image_grad_blocks(kv_grad, back, weight, down):
    rows, columns = kv_grad.shape
    width = weight.shape[0]
    parts, _, slice_rows, rank = down.shape
    share = parts // CORES
    step = share * slice_rows
    block = rows // SIDE
    out_spec = pl.BlockSpec((block, step), lambda j: (0, j))
    return pl.pallas_call(
        image_grad_kernel,
        grid=(width // step,),
        in_specs=[
            pl.BlockSpec((rows, columns), lambda j: (0, 0)),
            pl.BlockSpec((rows, rank), lambda j: (0, 0)),
            pl.BlockSpec((step, columns), lambda j: (j, 0)),
            pl.BlockSpec((share, 1, slice_rows, rank), lambda j: (j % CORES, j // CORES, 0, 0)),
        ],
        out_specs=[out_spec] * SIDE,
        out_shape=[jax.ShapeDtypeStruct((block, width), f32)]
        + [jax.ShapeDtypeStruct((block, width), bf16)] * (SIDE - 1),
        name="image_grad",
    )(kv_grad, back, weight, down)


def make_body(mesh):
    segments, parts, heads = (mesh.shape[a] for a in AXES)
    runs = segments // SIDE
    ring = runs * heads

    def shift(v, dx=0, dz=0, opposite=False):
        pairs = []
        for s in range(segments):
            for d in range(parts):
                for m in range(heads):
                    z_lo, x = divmod(s, SIDE)
                    sign = -1 if (opposite and d % CORES) else 1
                    x2 = (x + sign * dx) % SIDE
                    m2, z2 = divmod((m * runs + z_lo + sign * dz) % ring, runs)
                    pairs.append(((s * parts + d) * heads + m, ((z2 * SIDE + x2) * parts + d) * heads + m2))
        return lax.ppermute(v, AXES, pairs)

    def sum_over_mp(v, out):
        far = shift(v, dz=2 * runs, opposite=True)
        near = shift(v, dz=runs)
        prior = shift(v, dz=-runs)
        return ((v.astype(f32) + far.astype(f32)) + (near.astype(f32) + prior.astype(f32))).astype(out)

    def body(
        encoder_image_states,
        frozen_key_value,
        adapter_down_weight,
        adapter_up_weight,
        queries,
        cotangent,
        text_token_length,
        image_tile_count,
    ):
        own = encoder_image_states[0]
        tokens, _ = own.shape
        parallel_index = lax.axis_index("mp")
        segment_index = lax.axis_index("segment")
        lowrank = adapter_up_weight.shape[2]
        columns = adapter_up_weight.shape[3]
        up_key, up_value = adapter_up_weight[0, 0], adapter_up_weight[0, 1]
        down = adapter_down_weight[0]
        fourth = down.shape[0]

        line = jnp.concatenate([own, shift(own, dz=-1), shift(own, dz=2, opposite=True), shift(own, dz=1)], axis=0)
        image = jnp.concatenate([line, shift(line, dx=-1), shift(line, dx=2, opposite=True), shift(line, dx=1)], axis=0)
        rows = image.shape[0]
        offset = jnp.arange(rows, dtype=jnp.int32)
        x_off, z_off, tok = offset // (runs * tokens), (offset // tokens) % runs, offset % tokens
        position = (
            ((segment_index // SIDE + z_off) % runs) * SIDE + (segment_index % SIDE + x_off) % SIDE
        ) * tokens + tok

        local_weight = frozen_key_value[0].reshape(-1, CORES * columns)
        weight = lax.all_gather(local_weight, "dp", axis=0, tiled=True)
        slice_rows = fourth // parts
        down_slices = lax.all_gather(
            lax.dynamic_slice_in_dim(down, lax.axis_index("dp") * slice_rows, slice_rows, 0),
            "mp",
            axis=0,
            tiled=True,
        )
        all_down = lax.all_gather(down_slices, "dp", axis=0, tiled=True)
        all_down = all_down.reshape(parts, heads, slice_rows, down.shape[1])

        image_fourth = lax.dynamic_slice_in_dim(image, parallel_index * fourth, fourth, 1)
        low = jnp.dot(image_fourth, down, preferred_element_type=f32)
        low = lax.all_gather(low, "mp", axis=0)
        low = jnp.sum(low, axis=0).astype(bf16)
        adapted = jnp.concatenate(
            [
                jnp.dot(low[:, :lowrank], up_key, preferred_element_type=f32),
                jnp.dot(low[:, lowrank:], up_value, preferred_element_type=f32),
            ],
            axis=1,
        )
        key_value = (jnp.dot(image, weight, preferred_element_type=f32) + adapter_scale * adapted).astype(bf16)

        local_kv = columns // HD
        text_rows = queries.shape[2]
        group = queries.shape[3] // HD // local_kv
        query_rows = queries[0, 0].reshape(text_rows, local_kv, group, HD)
        cot_rows = cotangent[0, 0].reshape(text_rows, local_kv, group, HD)
        key_rows = key_value[:, :columns].reshape(rows, local_kv, HD)
        value_rows = key_value[:, columns:].reshape(rows, local_kv, HD)
        key_mask = position < image_tile_count[0] * (rows // TILES)
        row_mask = (jnp.arange(text_rows, dtype=jnp.int32) < text_token_length[0]).astype(f32)
        scores = jnp.einsum("tgrd,jgd->grtj", query_rows, key_rows, preferred_element_type=f32) * HD ** (-0.5)
        masked = jnp.where(key_mask[None, None, None, :], scores, -1e30)
        row_top = jnp.max(masked, axis=-1, keepdims=True)
        shifted = jnp.exp(masked - row_top)
        attention = shifted / jnp.sum(shifted, axis=-1, keepdims=True)
        row_gate = row_mask[None, None, :, None]
        kept = attention.astype(bf16) * row_gate.astype(bf16)
        dweights = jnp.einsum("tgrd,jgd->grtj", cot_rows, value_rows, preferred_element_type=f32)
        row_delta = jnp.sum(attention * dweights, axis=-1, keepdims=True)
        dscore = (attention * (dweights - row_delta) * row_gate * HD ** (-0.5)).astype(bf16)
        key_grad = jnp.einsum("grtj,tgrd->jgd", dscore, query_rows, preferred_element_type=f32)
        value_grad = jnp.einsum("grtj,tgrd->jgd", kept, cot_rows, preferred_element_type=f32)
        kv_grad = jnp.concatenate(
            [key_grad.reshape(rows, columns), value_grad.reshape(rows, columns)], axis=1
        ).astype(bf16)

        back = adapter_scale * jnp.concatenate(
            [
                lax.dot_general(kv_grad[:, :columns], up_key, contracted_columns, preferred_element_type=f32),
                lax.dot_general(kv_grad[:, columns:], up_value, contracted_columns, preferred_element_type=f32),
            ],
            axis=1,
        )

        stay, next_x, far_x, prior_x = image_grad_blocks(kv_grad, back.astype(bf16), weight, all_down)
        image_grad = (
            stay
            + shift(next_x, dx=1).astype(f32)
            + shift(far_x, dx=2, opposite=True).astype(f32)
            + shift(prior_x, dx=-1).astype(f32)
        )

        back = lax.all_gather(back, "mp", axis=0)
        back = jnp.sum(back, axis=0).astype(bf16)
        down_grad = lax.dot_general(image_fourth, back, contract_rows, preferred_element_type=f32)
        up_grad = adapter_scale * jnp.stack(
            [
                lax.dot_general(low[:, :lowrank], kv_grad[:, :columns], contract_rows, preferred_element_type=f32),
                lax.dot_general(low[:, lowrank:], kv_grad[:, columns:], contract_rows, preferred_element_type=f32),
            ]
        )
        both = jnp.concatenate([down_grad, up_grad.reshape(-1, down_grad.shape[1])], axis=0)
        both = lax.psum_scatter(both, "dp", scatter_dimension=0, tiled=True)
        both = both.astype(bf16)

        send = image_grad[tokens:].astype(bf16)
        image_grad = (
            image_grad[:tokens]
            + shift(send[:tokens], dz=1).astype(f32)
            + shift(send[tokens : 2 * tokens], dz=2, opposite=True).astype(f32)
            + shift(send[2 * tokens :], dz=-1).astype(f32)
        )
        result = sum_over_mp(image_grad.astype(bf16), f32)
        both = lax.all_gather(both, "dp", axis=0, tiled=True)
        down_out = both[:fourth]
        up_out = both[fourth:].reshape(up_grad.shape)
        return (down_out[None], up_out[None], result[None])

    return body


def solution(mesh):
    in_specs = (
        P("dp", "segment", None),
        P("segment", "dp", None, "mp"),
        P("segment", "mp", None),
        P("segment", None, None, "mp"),
        P("segment", "dp", None, "mp"),
        P("segment", "dp", None, "mp"),
        P("dp"),
        P("dp"),
    )
    out_specs = (P("segment", "mp", None), P("segment", None, None, "mp"), P("dp", "segment", None))
    body = make_body(mesh)

    return jax.shard_map(body, mesh=mesh, in_specs=in_specs, out_specs=out_specs, check_vma=False)
```

time: 267 us -> 239 us (0.90)
  starting transfers between devices: 156 us -> 60.7 us
  blocking collectives: 37 us -> 69.2 us
  waiting for transfers between devices: 28.1 us -> 50.1 us
  between operations: 3.15 us -> 15.5 us
  Pallas kernels: 0 us -> 9.27 us
  local copies, waits for them, and re-layouts: 19 us -> 10.5 us
    ppermute x34 -> x15, starting transfers between devices: 156 us -> 60.6 us  [shift(): return lax.ppermute(v, AXES, pairs)]
    all_gather x0 -> x2, blocking collectives: none -> 33.6 us  [the longest x1 16.9 us: body(): lax.all_gather(lax.dynamic_slice_in_dim(down, lax.axis_index('dp') * slic...]
    ppermute x34 -> x15, waiting for transfers between devices: 28.1 us -> 44.8 us  [shift(): return lax.ppermute(v, AXES, pairs)]
    pallas_call x0 -> x1, Pallas kernels: none -> 9.27 us  [image_grad_blocks(): pl.pallas_call(image_grad_kernel, grid=(width // step,), in_specs=[pl.Blo...]
    dot_general x2 -> x0, matrix products: 7.57 us -> none  [the longest x1 6.29 us: body(): lax.dot_general(kv_grad, weight, contracted_columns, preferred_element_ty...]
    reduce_scatter x0 -> x1, waiting for transfers between devices: none -> 5.27 us  [body(): both = lax.psum_scatter(both, 'dp', scatter_dimension=0, tiled=True)]
    unnamed x39 -> x16, local copies, waits for them, and re-layouts: 8.12 us -> 4.4 us
    dot_general x1, matrix products: 1.39 us -> 4.75 us  [body(): jnp.dot(image, weight, preferred_element_type=f32) + adapter_scale * adapted]
  transfers between devices with their start and end apart: 34 -> 18, of which waited for: 5 -> 9; matrix products, arithmetic and copies ran while one was open for 7% -> 11% of each run, Pallas kernels for 0% -> 0%
where the time goes in v3:
time: 239 us; the launch traced here: 238 us
  blocking collectives  69.2 us (29%)
  starting transfers between devices  60.7 us (25%)
  waiting for transfers between devices  50.1 us (21%)
  between operations  15.5 us (6%)
  matrix products  14.8 us (6%)
  local copies, waits for them, and re-layouts  10.5 us (4%)
  Pallas kernels  9.27 us (4%)
  other arithmetic  7.32 us (3%)
    ppermute x15, starting transfers between devices, shift(): return lax.ppermute(v, AXES, pairs)  60.6 us
    ppermute x15, waiting for transfers between devices, shift(): return lax.ppermute(v, AXES, pairs)  44.8 us
    all_gather x1, blocking collectives, body(): both = lax.all_gather(both, 'dp', axis=0, tiled=True)  18.1 us
    all_gather x1, blocking collectives, body(): back = lax.all_gather(back, 'mp', axis=0)  17.5 us
    all_gather x1, blocking collectives, body(): lax.all_gather(lax.dynamic_slice_in_dim(down, lax.axis_index('dp') * slic...  16.9 us
    all_gather x1, blocking collectives, body(): low = lax.all_gather(low, 'mp', axis=0)  16.7 us
    pallas_call x1, Pallas kernels, image_grad_blocks(): pl.pallas_call(image_grad_kernel, grid=(width // step,), in_specs=[pl.Blo...  9.27 us
    reduce_scatter x1, waiting for transfers between devices, body(): both = lax.psum_scatter(both, 'dp', scatter_dimension=0, tiled=True)  5.27 us
  transfers between devices with their start and end apart: 18, of which 9 were waited for; matrix products, arithmetic and copies ran while one was open for 11% of the time, Pallas kernels for 0%

profile of v3, /device:TPU:1, one launch (start us, length us, event | category | flops | bytes accessed | tf_op | source)
XLA Modules:
  0.0 237.5 jit_solution(2956129251693467454)
XLA Ops:
  7.2 2.5 %copy.52 = bf16[128,8,2,256]{3,1,2,0:T(8,128)(2,1)} copy(bf16[128,8,2,256]{3,2,1,0:T(2,128)(2,1)} %bitcast.84) | data formatting | bytes 2097152
  9.8 11.9 %collective-permute-start = (bf16[8,8192]{1,0:T(8,128)(2,1)S(1)}, bf16[8,8192]{1,0:T(8,128)(2,1)S(1)}, u32[]{:S(2)}, u32[]{:S(2)}) collective-permute-start(bf16[8,8192]{1,0:T(8,128)(2,1)S(1)} %bitcast.94), channel_id=1, source_target_pairs={{0,387},{1,384},{2,385},{3,386},{4,391},{5,388},{6,389},{7,390},{8... | collective-permute-start | bytes 393224 | tf_op jit(solution)/shard_map/ppermute | solution.py:70
  21.8 3.1 %collective-permute-start.1 = (bf16[8,8192]{1,0:T(8,128)(2,1)S(1)}, bf16[8,8192]{1,0:T(8,128)(2,1)S(1)}, u32[]{:S(2)}, u32[]{:S(2)}) collective-permute-start(bf16[8,8192]{1,0:T(8,128)(2,1)S(1)} %bitcast.95), channel_id=1, source_target_pairs={{0,256},{1,257},{2,258},{3,259},{4,263},{5,260},{6,261},{7,262},{8... | collective-permute-start | bytes 393224 | tf_op jit(solution)/shard_map/ppermute | solution.py:70
  24.9 2.6 %collective-permute-start.2 = (bf16[8,8192]{1,0:T(8,128)(2,1)S(1)}, bf16[8,8192]{1,0:T(8,128)(2,1)}, u32[]{:S(2)}, u32[]{:S(2)}) collective-permute-start(bf16[8,8192]{1,0:T(8,128)(2,1)S(1)} %bitcast.96), channel_id=1, source_target_pairs={{0,128},{1,129},{2,130},{3,131},{4,132},{5,133},{6,134},{7,135},{8... | collective-permute-start | bytes 393224 | tf_op jit(solution)/shard_map/ppermute | solution.py:70
  27.6 16.9 %all-gather.1 = bf16[1,1024,128]{2,1,0:T(8,128)(2,1)} all-gather(bf16[1,256,128]{2,1,0:T(8,128)(2,1)S(1)} %constant_dynamic-slice_fusion), channel_id=3, replica_groups=mesh['segment'=16,'dp'=8,'mp'=4] {'mp'}, dimensions={1}, use_global_device_ids=true | all-gather | bytes 327680 | tf_op jit(solution)/shard_map/all_gather | solution.py:110
  47.3 2.0 copy.50
  50.3 4.4 %collective-permute-start.3 = (bf16[32,8192]{1,0:T(8,128)(2,1)S(1)}, bf16[32,8192]{1,0:T(8,128)(2,1)S(1)}, u32[]{:S(2)}, u32[]{:S(2)}) collective-permute-start(bf16[32,8192]{1,0:T(8,128)(2,1)S(1)} %pad_maximum_fusion.1), channel_id=1, source_target_pairs={{0,96},{1,97},{2,98},{3,99},{4,100},{5,101},{6,102},{7,103},{8,104... | collective-permute-start | bytes 1572872 | tf_op jit(solution)/shard_map/ppermute | solution.py:70
  54.7 2.4 %collective-permute-start.4 = (bf16[32,8192]{1,0:T(8,128)(2,1)S(1)}, bf16[32,8192]{1,0:T(8,128)(2,1)S(1)}, u32[]{:S(2)}, u32[]{:S(2)}) collective-permute-start(bf16[32,8192]{1,0:T(8,128)(2,1)S(1)} %pad_maximum_fusion.1), channel_id=1, source_target_pairs={{0,64},{1,65},{2,66},{3,67},{4,68},{5,69},{6,70},{7,71},{8,72},{9,... | collective-permute-start | bytes 1572872 | tf_op jit(solution)/shard_map/ppermute | solution.py:70
  57.1 2.5 %collective-permute-start.5 = (bf16[32,8192]{1,0:T(8,128)(2,1)S(1)}, bf16[32,8192]{1,0:T(8,128)(2,1)S(1)}, u32[]{:S(2)}, u32[]{:S(2)}) collective-permute-start(bf16[32,8192]{1,0:T(8,128)(2,1)S(1)} %pad_maximum_fusion.1), channel_id=1, source_target_pairs={{0,32},{1,33},{2,34},{3,35},{4,36},{5,37},{6,38},{7,39},{8,40},{9,... | collective-permute-start | bytes 1572872 | tf_op jit(solution)/shard_map/ppermute | solution.py:70
  60.6 2.6 %collective-permute-done.3 = bf16[32,8192]{1,0:T(8,128)(2,1)S(1)} collective-permute-done((bf16[32,8192]{1,0:T(8,128)(2,1)S(1)}, bf16[32,8192]{1,0:T(8,128)(2,1)S(1)}, u32[]{:S(2)}, u32[]{:S(2)}) %collective-permute-start.3) | collective-permute-done | bytes 524320 | tf_op jit(solution)/shard_map/ppermute | solution.py:70
  63.3 4.6 %collective-permute-done.4 = bf16[32,8192]{1,0:T(8,128)(2,1)S(1)} collective-permute-done((bf16[32,8192]{1,0:T(8,128)(2,1)S(1)}, bf16[32,8192]{1,0:T(8,128)(2,1)S(1)}, u32[]{:S(2)}, u32[]{:S(2)}) %collective-permute-start.4) | collective-permute-done | bytes 524320 | tf_op jit(solution)/shard_map/ppermute | solution.py:70
  67.9 15.3 %collective-permute-done.5 = bf16[32,8192]{1,0:T(8,128)(2,1)S(1)} collective-permute-done((bf16[32,8192]{1,0:T(8,128)(2,1)S(1)}, bf16[32,8192]{1,0:T(8,128)(2,1)S(1)}, u32[]{:S(2)}, u32[]{:S(2)}) %collective-permute-start.5) | collective-permute-done | bytes 524320 | tf_op jit(solution)/shard_map/ppermute | solution.py:70
  83.5 16.7 %all-gather = f32[512,128]{1,0:T(8,128)S(1)} all-gather(f32[128,128]{1,0:T(8,128)S(1)} %fusion.18), channel_id=2, replica_groups=mesh['segment'=16,'dp'=8,'mp'=4] {'mp'}, dimensions={0}, use_global_device_ids=true | all-gather | bytes 327680 | tf_op jit(solution)/shard_map/all_gather | solution.py:121
  100.6 4.8 %fusion.12 = bf16[128,512]{1,0:T(8,128)(2,1)S(1)} fusion(bf16[128,8192]{1,0:T(8,128)(2,1)S(1)} %constant_dynamic-update-slice_fusion, bf16[8192,512]{1,0:T(8,128)(2,1)} %all-gather.6.cloned.1.call-done.weight_ref, f32[128,256]{1,0:T(8,128)S(1)} %fusion.38, f32[128,256]{1,0:T(8,128)S(1)} %fusion.42), kind=kOutput, calls=%fused_computation.16 | convolution fusion | flops 1074003968 | bytes 10878976 | tf_op jit(solution)/shard_map/dot_general | solution.py:130
  105.4 2.5 %fusion.80 = (f32[2,8,128]{2,1,0:T(8,128)S(1)}, f32[2,8,128,128]{2,3,1,0:T(8,128)}) fusion(bf16[128,2,8,128]{0,3,2,1:T(8,128)(2,1)} %bitcast.91, pred[128]{0:T(512)(128)(4,1)S(1)} %fusion.55, bf16[128,2,128,1]{2,1,0,3:T(2,128)(2,1)S(1)} %bitcast.101), kind=kOutput, calls=%fused_computation.116 | convolution fusion | flops 68157568 | bytes 1646720 | tf_op jit(solution)/shard_map/sub | solution.py:144
  111.1 2.9 %fusion.15 = bf16[2,128,128]{1,2,0:T(8,128)(2,1)S(1)} fusion(bf16[128,2,8,128]{0,3,2,1:T(8,128)(2,1)} %bitcast.93, f32[2,8,128,128]{2,3,1,0:T(8,128)} %convolution_bitcast_fusion, f32[128]{0:T(128)S(1)} %get-tuple-element.20, f32[2,8,128,128]{2,3,1,0:T(8,128)} %get-tuple-element.19, f32[2,8,128]{2,1,0:T(8,128)S(1)} %get-tuple-element.18), kind=kOutput, calls=%fused_computation.20 | convolution fusion | flops 69240960 | bytes 2695680 | tf_op jit(solution)/shard_map/grtj,tgrd->jgd/dot_general | solution.py:151
  116.4 9.3 %image_grad.1 = (f32[32,8192]{1,0:T(8,128)}, bf16[32,8192]{1,0:T(8,128)(2,1)}, bf16[32,8192]{1,0:T(8,128)(2,1)}, bf16[32,8192]{1,0:T(8,128)(2,1)}) custom-call(bf16[128,512]{1,0:T(8,128)(2,1)} %pad_maximum_fusion.2.kv_ref, bf16[128,128]{1,0:T(8,128)(2,1)} %fusion.31.back_ref, bf16[8192,512]{1,0:T(8,128)(2,1)} %all-gather.6.cloned.1.call-done.weight_ref, ...), custom_call_target="tpu_custom_call" | custom-call | tf_op jit(solution)/shard_map/image_grad/pallas_call | solution.py:39
  127.5 2.2 collective-permute-start.7
  129.7 3.1 %collective-permute-start.6 = (bf16[32,8192]{1,0:T(8,128)(2,1)}, bf16[32,8192]{1,0:T(8,128)(2,1)}, u32[]{:S(2)}, u32[]{:S(2)}) collective-permute-start(bf16[32,8192]{1,0:T(8,128)(2,1)} %get-tuple-element.8), channel_id=1, source_target_pairs={{0,32},{1,33},{2,34},{3,35},{4,36},{5,37},{6,38},{7,39},{8,40},{9,... | collective-permute-start | bytes 1572872 | tf_op jit(solution)/shard_map/ppermute | solution.py:70
  133.6 17.5 %all_gather.25 = f32[4,128,128]{2,1,0:T(8,128)S(1)} all-gather(f32[1,128,128]{2,1,0:T(8,128)} %copy.33), channel_id=1, replica_groups=mesh['segment'=16,'dp'=8,'mp'=4] {'mp'}, dimensions={0}, use_global_device_ids=true | all-gather | bytes 327680 | tf_op jit(solution)/shard_map/all_gather | solution.py:173
  153.0 3.3 %collective-permute-done.6 = bf16[32,8192]{1,0:T(8,128)(2,1)} collective-permute-done((bf16[32,8192]{1,0:T(8,128)(2,1)}, bf16[32,8192]{1,0:T(8,128)(2,1)}, u32[]{:S(2)}, u32[]{:S(2)}) %collective-permute-start.6) | collective-permute-done | bytes 524320 | tf_op jit(solution)/shard_map/ppermute | solution.py:70
  157.8 4.5 %collective-permute-start.11 = (bf16[8,8192]{1,0:T(8,128)(2,1)S(1)}, bf16[8,8192]{1,0:T(8,128)(2,1)S(1)}, u32[]{:S(2)}, u32[]{:S(2)}) collective-permute-start(bf16[8,8192]{1,0:T(8,128)(2,1)S(1)} %get-tuple-element.14), channel_id=1, source_target_pairs={{0,387},{1,384},{2,385},{3,386},{4,391},{5,388},{6,389},{7,390},{8... | collective-permute-start | bytes 393224 | tf_op jit(solution)/shard_map/ppermute | solution.py:70
  162.3 2.8 %collective-permute-start.10 = (bf16[8,8192]{1,0:T(8,128)(2,1)S(1)}, bf16[8,8192]{1,0:T(8,128)(2,1)S(1)}, u32[]{:S(2)}, u32[]{:S(2)}) collective-permute-start(bf16[8,8192]{1,0:T(8,128)(2,1)S(1)} %get-tuple-element.15), channel_id=1, source_target_pairs={{0,256},{1,257},{2,258},{3,259},{4,263},{5,260},{6,261},{7,262},{8... | collective-permute-start | bytes 393224 | tf_op jit(solution)/shard_map/ppermute | solution.py:70
  165.1 2.3 collective-permute-start.9
  168.5 2.6 %collective-permute-done.10 = bf16[8,8192]{1,0:T(8,128)(2,1)S(1)} collective-permute-done((bf16[8,8192]{1,0:T(8,128)(2,1)S(1)}, bf16[8,8192]{1,0:T(8,128)(2,1)S(1)}, u32[]{:S(2)}, u32[]{:S(2)}) %collective-permute-start.10) | collective-permute-done | bytes 131104 | tf_op jit(solution)/shard_map/ppermute | solution.py:70
  172.8 8.0 %collective-permute-start.14 = (bf16[8,8192]{1,0:T(8,128)(2,1)S(1)}, bf16[8,8192]{1,0:T(8,128)(2,1)S(1)}, u32[]{:S(2)}, u32[]{:S(2)}) collective-permute-start(bf16[8,8192]{1,0:T(8,128)(2,1)S(1)} %fusion.29), channel_id=1, source_target_pairs={{0,3},{1,0},{2,1},{3,2},{4,7},{5,4},{6,5},{7,6},{8,11},{9,8},{10,9... | collective-permute-start | bytes 393224 | tf_op jit(solution)/shard_map/ppermute | solution.py:70
  180.9 1.9 collective-permute-start.13
  182.8 7.0 %collective-permute-start.12 = (bf16[8,8192]{1,0:T(8,128)(2,1)S(1)}, bf16[8,8192]{1,0:T(8,128)(2,1)S(1)}, u32[]{:S(2)}, u32[]{:S(2)}) collective-permute-start(bf16[8,8192]{1,0:T(8,128)(2,1)S(1)} %fusion.29), channel_id=1, source_target_pairs={{0,2},{1,3},{2,0},{3,1},{4,6},{5,7},{6,4},{7,5},{8,10},{9,11},{10,... | collective-permute-start | bytes 393224 | tf_op jit(solution)/shard_map/ppermute | solution.py:70
  189.8 2.2 collective-permute-done.14
  192.0 12.5 %collective-permute-done.12 = bf16[8,8192]{1,0:T(8,128)(2,1)S(1)} collective-permute-done((bf16[8,8192]{1,0:T(8,128)(2,1)S(1)}, bf16[8,8192]{1,0:T(8,128)(2,1)S(1)}, u32[]{:S(2)}, u32[]{:S(2)}) %collective-permute-start.12) | collective-permute-done | bytes 131104 | tf_op jit(solution)/shard_map/ppermute | solution.py:70
  205.2 5.3 %reduce-scatter.2.cloned.1.call-done = f32[288,128]{1,0:T(8,128)} async-done(((f32[2304,128]{1,0:T(8,128)}), f32[288,128]{1,0:T(8,128)}) %reduce-scatter.2.cloned.1.call-update) | async-done | bytes 147472 | tf_op jit(solution)/shard_map/reduce_scatter | solution.py:183
  211.4 18.1 %all_gather.26 = bf16[2304,128]{1,0:T(8,128)(2,1)S(1)} all-gather(bf16[288,128]{1,0:T(8,128)(2,1)S(1)} %convert_element_type.81), channel_id=1, replica_groups=mesh['segment'=16,'dp'=8,'mp'=4] {'dp'}, dimensions={0}, use_global_device_ids=true | all-gather | bytes 663552 | tf_op jit(solution)/shard_map/all_gather | solution.py:194
  (72 shorter events, 21.8 us)
Async XLA Ops:
  7.2 20.4 %copy-start = (bf16[1,2048,128]{2,1,0:T(8,128)(2,1)S(1)}, bf16[1,2048,128]{2,1,0:T(8,128)(2,1)}, u32[]{:S(2)}) copy-start(bf16[1,2048,128]{2,1,0:T(8,128)(2,1)} %param.10) | copy-start | bytes 1572868
  7.2 2.6 %copy-start.2 = (bf16[1,8,8192]{2,1,0:T(8,128)(2,1)S(1)}, bf16[1,8,8192]{2,1,0:T(8,128)(2,1)}, u32[]{:S(2)}) copy-start(bf16[1,8,8192]{2,1,0:T(8,128)(2,1)} %param.8) | copy-start | bytes 393220
  7.2 93.4 %all-gather.6.cloned.1.call-start = ((), (), s32[]{:S(2)}) async-start(), calls=%async_computation.1 | async-start | bytes 9437184 | tf_op jit(solution)/shard_map/all_gather | solution.py:108
  9.8 106.6 %all-gather.8.cloned.1.call-start = ((), (), s32[]{:S(2)}) async-start(), calls=%async_computation.3 | async-start | bytes 2359296 | tf_op jit(solution)/shard_map/all_gather | solution.py:116
  9.8 39.5 %collective-permute-start = (bf16[8,8192]{1,0:T(8,128)(2,1)S(1)}, bf16[8,8192]{1,0:T(8,128)(2,1)S(1)}, u32[]{:S(2)}, u32[]{:S(2)}) collective-permute-start(bf16[8,8192]{1,0:T(8,128)(2,1)S(1)} %bitcast.94), channel_id=1, source_target_pairs={{0,387},{1,384},{2,385},{3,386},{4,391},{5,388},{6,389},{7,390},{8... | collective-permute-start | bytes 393224 | tf_op jit(solution)/shard_map/ppermute | solution.py:70
  21.8 27.6 %collective-permute-start.1 = (bf16[8,8192]{1,0:T(8,128)(2,1)S(1)}, bf16[8,8192]{1,0:T(8,128)(2,1)S(1)}, u32[]{:S(2)}, u32[]{:S(2)}) collective-permute-start(bf16[8,8192]{1,0:T(8,128)(2,1)S(1)} %bitcast.95), channel_id=1, source_target_pairs={{0,256},{1,257},{2,258},{3,259},{4,263},{5,260},{6,261},{7,262},{8... | collective-permute-start | bytes 393224 | tf_op jit(solution)/shard_map/ppermute | solution.py:70
  24.9 24.5 %collective-permute-start.2 = (bf16[8,8192]{1,0:T(8,128)(2,1)S(1)}, bf16[8,8192]{1,0:T(8,128)(2,1)}, u32[]{:S(2)}, u32[]{:S(2)}) collective-permute-start(bf16[8,8192]{1,0:T(8,128)(2,1)S(1)} %bitcast.96), channel_id=1, source_target_pairs={{0,128},{1,129},{2,130},{3,131},{4,132},{5,133},{6,134},{7,135},{8... | collective-permute-start | bytes 393224 | tf_op jit(solution)/shard_map/ppermute | solution.py:70
  44.5 166.0 %reduce-scatter.2.cloned.1.call-start = ((), (), s32[]{:S(2)}) async-start(), calls=%async_computation.2 | async-start | bytes 1327104 | tf_op jit(solution)/shard_map/reduce_scatter | solution.py:183
  50.3 12.9 %collective-permute-start.3 = (bf16[32,8192]{1,0:T(8,128)(2,1)S(1)}, bf16[32,8192]{1,0:T(8,128)(2,1)S(1)}, u32[]{:S(2)}, u32[]{:S(2)}) collective-permute-start(bf16[32,8192]{1,0:T(8,128)(2,1)S(1)} %pad_maximum_fusion.1), channel_id=1, source_target_pairs={{0,96},{1,97},{2,98},{3,99},{4,100},{5,101},{6,102},{7,103},{8,104... | collective-permute-start | bytes 1572872 | tf_op jit(solution)/shard_map/ppermute | solution.py:70
  54.7 13.1 %collective-permute-start.4 = (bf16[32,8192]{1,0:T(8,128)(2,1)S(1)}, bf16[32,8192]{1,0:T(8,128)(2,1)S(1)}, u32[]{:S(2)}, u32[]{:S(2)}) collective-permute-start(bf16[32,8192]{1,0:T(8,128)(2,1)S(1)} %pad_maximum_fusion.1), channel_id=1, source_target_pairs={{0,64},{1,65},{2,66},{3,67},{4,68},{5,69},{6,70},{7,71},{8,72},{9,... | collective-permute-start | bytes 1572872 | tf_op jit(solution)/shard_map/ppermute | solution.py:70
  57.1 26.0 %collective-permute-start.5 = (bf16[32,8192]{1,0:T(8,128)(2,1)S(1)}, bf16[32,8192]{1,0:T(8,128)(2,1)S(1)}, u32[]{:S(2)}, u32[]{:S(2)}) collective-permute-start(bf16[32,8192]{1,0:T(8,128)(2,1)S(1)} %pad_maximum_fusion.1), channel_id=1, source_target_pairs={{0,32},{1,33},{2,34},{3,35},{4,36},{5,37},{6,38},{7,39},{8,40},{9,... | collective-permute-start | bytes 1572872 | tf_op jit(solution)/shard_map/ppermute | solution.py:70
  63.2 37.0 %copy-start.3 = (bf16[1,2,64,256]{3,2,1,0:T(8,128)(2,1)S(1)}, bf16[1,2,64,256]{3,2,1,0:T(8,128)(2,1)}, u32[]{:S(2)}) copy-start(bf16[1,2,64,256]{3,2,1,0:T(8,128)(2,1)} %param.11) | copy-start | bytes 196612
  125.6 27.4 %collective-permute-start.8 = (bf16[32,8192]{1,0:T(8,128)(2,1)}, bf16[32,8192]{1,0:T(8,128)(2,1)S(1)}, u32[]{:S(2)}, u32[]{:S(2)}) collective-permute-start(bf16[32,8192]{1,0:T(8,128)(2,1)} %get-tuple-element.10), channel_id=1, source_target_pairs={{0,96},{1,97},{2,98},{3,99},{4,100},{5,101},{6,102},{7,103},{8,104... | collective-permute-start | bytes 1572872 | tf_op jit(solution)/shard_map/ppermute | solution.py:70
  127.5 25.5 %collective-permute-start.7 = (bf16[32,8192]{1,0:T(8,128)(2,1)}, bf16[32,8192]{1,0:T(8,128)(2,1)}, u32[]{:S(2)}, u32[]{:S(2)}) collective-permute-start(bf16[32,8192]{1,0:T(8,128)(2,1)} %get-tuple-element.9), channel_id=1, source_target_pairs={{0,64},{1,65},{2,66},{3,67},{4,68},{5,69},{6,70},{7,71},{8,72},{9,... | collective-permute-start | bytes 1572872 | tf_op jit(solution)/shard_map/ppermute | solution.py:70
  129.7 26.6 %collective-permute-start.6 = (bf16[32,8192]{1,0:T(8,128)(2,1)}, bf16[32,8192]{1,0:T(8,128)(2,1)}, u32[]{:S(2)}, u32[]{:S(2)}) collective-permute-start(bf16[32,8192]{1,0:T(8,128)(2,1)} %get-tuple-element.8), channel_id=1, source_target_pairs={{0,32},{1,33},{2,34},{3,35},{4,36},{5,37},{6,38},{7,39},{8,40},{9,... | collective-permute-start | bytes 1572872 | tf_op jit(solution)/shard_map/ppermute | solution.py:70
  152.7 3.7 %copy-start.1 = (f32[32,8192]{1,0:T(8,128)S(1)}, f32[32,8192]{1,0:T(8,128)}, u32[]{:S(2)}) copy-start(f32[32,8192]{1,0:T(8,128)} %get-tuple-element.7) | copy-start | bytes 3145732
  157.8 10.6 %collective-permute-start.11 = (bf16[8,8192]{1,0:T(8,128)(2,1)S(1)}, bf16[8,8192]{1,0:T(8,128)(2,1)S(1)}, u32[]{:S(2)}, u32[]{:S(2)}) collective-permute-start(bf16[8,8192]{1,0:T(8,128)(2,1)S(1)} %get-tuple-element.14), channel_id=1, source_target_pairs={{0,387},{1,384},{2,385},{3,386},{4,391},{5,388},{6,389},{7,390},{8... | collective-permute-start | bytes 393224 | tf_op jit(solution)/shard_map/ppermute | solution.py:70
  162.3 8.7 %collective-permute-start.10 = (bf16[8,8192]{1,0:T(8,128)(2,1)S(1)}, bf16[8,8192]{1,0:T(8,128)(2,1)S(1)}, u32[]{:S(2)}, u32[]{:S(2)}) collective-permute-start(bf16[8,8192]{1,0:T(8,128)(2,1)S(1)} %get-tuple-element.15), channel_id=1, source_target_pairs={{0,256},{1,257},{2,258},{3,259},{4,263},{5,260},{6,261},{7,262},{8... | collective-permute-start | bytes 393224 | tf_op jit(solution)/shard_map/ppermute | solution.py:70
  165.1 7.7 %collective-permute-start.9 = (bf16[8,8192]{1,0:T(8,128)(2,1)S(1)}, bf16[8,8192]{1,0:T(8,128)(2,1)S(1)}, u32[]{:S(2)}, u32[]{:S(2)}) collective-permute-start(bf16[8,8192]{1,0:T(8,128)(2,1)S(1)} %get-tuple-element.13), channel_id=1, source_target_pairs={{0,128},{1,129},{2,130},{3,131},{4,132},{5,133},{6,134},{7,135},{8... | collective-permute-start | bytes 393224 | tf_op jit(solution)/shard_map/ppermute | solution.py:70
  172.8 19.1 %collective-permute-start.14 = (bf16[8,8192]{1,0:T(8,128)(2,1)S(1)}, bf16[8,8192]{1,0:T(8,128)(2,1)S(1)}, u32[]{:S(2)}, u32[]{:S(2)}) collective-permute-start(bf16[8,8192]{1,0:T(8,128)(2,1)S(1)} %fusion.29), channel_id=1, source_target_pairs={{0,3},{1,0},{2,1},{3,2},{4,7},{5,4},{6,5},{7,6},{8,11},{9,8},{10,9... | collective-permute-start | bytes 393224 | tf_op jit(solution)/shard_map/ppermute | solution.py:70
  180.9 11.1 %collective-permute-start.13 = (bf16[8,8192]{1,0:T(8,128)(2,1)S(1)}, bf16[8,8192]{1,0:T(8,128)(2,1)S(1)}, u32[]{:S(2)}, u32[]{:S(2)}) collective-permute-start(bf16[8,8192]{1,0:T(8,128)(2,1)S(1)} %fusion.29), channel_id=1, source_target_pairs={{0,1},{1,2},{2,3},{3,0},{4,5},{5,6},{6,7},{7,4},{8,9},{9,10},{10,1... | collective-permute-start | bytes 393224 | tf_op jit(solution)/shard_map/ppermute | solution.py:70
  182.8 21.7 %collective-permute-start.12 = (bf16[8,8192]{1,0:T(8,128)(2,1)S(1)}, bf16[8,8192]{1,0:T(8,128)(2,1)S(1)}, u32[]{:S(2)}, u32[]{:S(2)}) collective-permute-start(bf16[8,8192]{1,0:T(8,128)(2,1)S(1)} %fusion.29), channel_id=1, source_target_pairs={{0,2},{1,3},{2,0},{3,1},{4,6},{5,7},{6,4},{7,5},{8,10},{9,11},{10,... | collective-permute-start | bytes 393224 | tf_op jit(solution)/shard_map/ppermute | solution.py:70
Sparse Core Ops, SparseCore 0:
  10.1 63.0 all-gather.5
  75.4 33.1 all-gather.7
  168.6 41.8 reduce-scatter.1

commit v4 on v3

v4 whole, which is shorter than its diff:
```python
import jax
import jax.numpy as jnp
from jax import lax
from jax.experimental import pallas as pl
from jax.experimental.pallas import tpu as pltpu
from jax.sharding import PartitionSpec as P


HD = 128
TILES = 4
SIDE = 4
CORES = 2

adapter_scale = 2.0
contract_rows = (((0,), (0,)), ((), ()))
contracted_columns = (((1,), (1,)), ((), ()))
f32 = jnp.float32
bf16 = jnp.bfloat16
AXES = ("segment", "dp", "mp")


def layer_kernel(
    image_ref,
    weight_ref,
    low_ref,
    up_ref,
    query_ref,
    cot_ref,
    valid_ref,
    live_ref,
    kv_grad_ref,
    back_ref,
    own_ref,
    *rest,
):
    *away_refs, sum_ref = rest
    step = pl.program_id(0)
    forward_steps = pl.num_programs(0) // 2
    columns = weight_ref.shape[1] // 2
    local_kv = columns // HD
    group = query_ref.shape[1] // HD // local_kv
    block = own_ref.shape[0]

    @pl.when(step < forward_steps)
    def _():
        part = jnp.dot(image_ref[...], weight_ref[...], preferred_element_type=f32)

        @pl.when(step == 0)
        def _():
            sum_ref[...] = part

        @pl.when(step > 0)
        def _():
            sum_ref[...] += part

    @pl.when(step == forward_steps - 1)
    def _():
        adapted = jnp.dot(low_ref[...], up_ref[...], preferred_element_type=f32)
        key_value = (sum_ref[...] + adapter_scale * adapted).astype(bf16)
        valid = valid_ref[...] > 0
        live = live_ref[0:1, :]
        for g in range(local_kv):
            key_at, value_at = g * HD, columns + g * HD
            keys = key_value[:, key_at : key_at + HD]
            values = key_value[:, value_at : value_at + HD]
            key_grad = value_grad = None
            for r in range(group):
                at = (g * group + r) * HD
                query, cot = query_ref[:, at : at + HD], cot_ref[:, at : at + HD]
                scores = lax.dot_general(keys, query, contracted_columns, preferred_element_type=f32) * HD ** (-0.5)
                masked = jnp.where(valid, scores, -1e30)
                shifted = jnp.exp(masked - jnp.max(masked, axis=0, keepdims=True))
                attention = shifted * (1.0 / jnp.sum(shifted, axis=0, keepdims=True))
                dweights = lax.dot_general(values, cot, contracted_columns, preferred_element_type=f32)
                delta = jnp.sum(attention * dweights, axis=0, keepdims=True)
                dscore = (attention * (dweights - delta) * (live * HD ** (-0.5))).astype(bf16)
                kept = (attention * live).astype(bf16)
                dk = jnp.dot(dscore, query, preferred_element_type=f32)
                dv = jnp.dot(kept, cot, preferred_element_type=f32)
                key_grad = dk if r == 0 else key_grad + dk
                value_grad = dv if r == 0 else value_grad + dv
            kv_grad_ref[:, key_at : key_at + HD] = key_grad.astype(bf16)
            kv_grad_ref[:, value_at : value_at + HD] = value_grad.astype(bf16)
        back_ref[...] = adapter_scale * lax.dot_general(
            kv_grad_ref[...], up_ref[...], contracted_columns, preferred_element_type=f32
        )

    @pl.when(step >= forward_steps)
    def _():
        total = lax.dot_general(kv_grad_ref[...], weight_ref[...], contracted_columns, preferred_element_type=f32)
        own_ref[...] = total[:block]
        for i, ref in enumerate(away_refs):
            ref[...] = total[(i + 1) * block : (i + 2) * block].astype(bf16)


def layer(image, weight, low, up, query, cot, valid, live):
    rows, width = image.shape
    columns = weight.shape[1]
    rank = low.shape[1]
    steps = 8
    share = width // steps
    block = rows // SIDE

    def whole(v):
        return pl.BlockSpec(v.shape, lambda j: (0, 0))

    def turn(j):
        return jnp.minimum(j, 2 * steps - 1 - j)

    out_spec = pl.BlockSpec((block, share), lambda j: (0, jnp.minimum(steps - 1, 2 * steps - 1 - j)))
    return pl.pallas_call(
        layer_kernel,
        grid=(2 * steps,),
        in_specs=[
            pl.BlockSpec((rows, share), lambda j: (0, jnp.minimum(j, steps - 1))),
            pl.BlockSpec((share, columns), lambda j: (turn(j), 0)),
            whole(low),
            whole(up),
            whole(query),
            whole(cot),
            whole(valid),
            whole(live),
        ],
        out_specs=[
            pl.BlockSpec((rows, columns), lambda j: (0, 0)),
            pl.BlockSpec((rows, rank), lambda j: (0, 0)),
        ]
        + [out_spec] * SIDE,
        out_shape=[
            jax.ShapeDtypeStruct((rows, columns), bf16),
            jax.ShapeDtypeStruct((rows, rank), f32),
            jax.ShapeDtypeStruct((block, width), f32),
        ]
        + [jax.ShapeDtypeStruct((block, width), bf16)] * (SIDE - 1),
        scratch_shapes=[pltpu.VMEM((rows, columns), f32)],
        name="layer",
    )(image, weight, low, up, query, cot, valid, live)


def make_body(mesh):
    segments, parts, heads = (mesh.shape[a] for a in AXES)
    runs = segments // SIDE
    ring = runs * heads

    def shift(v, dx=0, dz=0, opposite=False):
        pairs = []
        for s in range(segments):
            for d in range(parts):
                for m in range(heads):
                    z_lo, x = divmod(s, SIDE)
                    sign = -1 if (opposite and d % CORES) else 1
                    x2 = (x + sign * dx) % SIDE
                    m2, z2 = divmod((m * runs + z_lo + sign * dz) % ring, runs)
                    pairs.append(((s * parts + d) * heads + m, ((z2 * SIDE + x2) * parts + d) * heads + m2))
        return lax.ppermute(v, AXES, pairs)

    def sum_over_mp(v, out):
        far = shift(v, dz=2 * runs, opposite=True)
        near = shift(v, dz=runs)
        prior = shift(v, dz=-runs)
        return ((v.astype(f32) + far.astype(f32)) + (near.astype(f32) + prior.astype(f32))).astype(out)

    def body(
        encoder_image_states,
        frozen_key_value,
        adapter_down_weight,
        adapter_up_weight,
        queries,
        cotangent,
        text_token_length,
        image_tile_count,
    ):
        own = encoder_image_states[0]
        tokens, _ = own.shape
        parallel_index = lax.axis_index("mp")
        segment_index = lax.axis_index("segment")
        lowrank, columns = adapter_up_weight.shape[2:]
        up_key, up_value = adapter_up_weight[0, 0], adapter_up_weight[0, 1]
        down = adapter_down_weight[0]
        fourth = down.shape[0]

        line = [shift(own, dz=-1), shift(own, dz=2, opposite=True), shift(own, dz=1)]
        others = jnp.concatenate(line, axis=0)
        image = jnp.concatenate(
            [
                own,
                *line,
                shift(own, dx=-1),
                shift(others, dx=-1),
                shift(own, dx=2, opposite=True),
                shift(others, dx=2, opposite=True),
                shift(own, dx=1),
                shift(others, dx=1),
            ],
            axis=0,
        )
        rows = image.shape[0]
        offset = jnp.arange(rows, dtype=jnp.int32)
        x_off, z_off, tok = offset // (runs * tokens), (offset // tokens) % runs, offset % tokens
        position = (
            ((segment_index // SIDE + z_off) % runs) * SIDE + (segment_index % SIDE + x_off) % SIDE
        ) * tokens + tok

        local_weight = frozen_key_value[0].reshape(-1, CORES * columns)
        weight = lax.all_gather(local_weight, "dp", axis=0, tiled=True)
        image_fourth = lax.dynamic_slice_in_dim(image, parallel_index * fourth, fourth, 1)
        low = jnp.dot(image_fourth, down, preferred_element_type=f32)
        low = lax.all_gather(low, "mp", axis=0)
        low = jnp.sum(low, axis=0).astype(bf16)
        text_rows = queries.shape[2]
        none = jnp.zeros_like(up_key)
        up_both = jnp.concatenate(
            [jnp.concatenate([up_key, none], axis=1), jnp.concatenate([none, up_value], axis=1)], axis=0
        )
        valid = (position < image_tile_count[0] * (rows // TILES)).astype(f32)
        live = (jnp.arange(text_rows, dtype=jnp.int32) < text_token_length[0]).astype(f32)
        kv_grad, back, stay, next_x, far_x, prior_x = layer(
            image,
            weight,
            low,
            up_both,
            queries[0, 0],
            cotangent[0, 0],
            jnp.broadcast_to(valid[:, None], (rows, text_rows)),
            jnp.broadcast_to(live[None, :], (8, text_rows)),
        )

        image_grad = (
            stay
            + shift(next_x, dx=1).astype(f32)
            + shift(far_x, dx=2, opposite=True).astype(f32)
            + shift(prior_x, dx=-1).astype(f32)
        )

        back = lax.all_gather(back, "mp", axis=0)
        back = jnp.sum(back, axis=0).astype(bf16)
        adapter_grad = lax.dot_general(back, down, contracted_columns, preferred_element_type=f32)
        block = stay.shape[0]
        adapter_away = adapter_grad.astype(bf16)
        adapter_grad = (
            adapter_grad[:block]
            + shift(adapter_away[block : 2 * block], dx=1).astype(f32)
            + shift(adapter_away[2 * block : 3 * block], dx=2, opposite=True).astype(f32)
            + shift(adapter_away[3 * block :], dx=-1).astype(f32)
        )
        here = lax.dynamic_slice_in_dim(image_grad, parallel_index * fourth, fourth, 1)
        image_grad = lax.dynamic_update_slice_in_dim(image_grad, here + adapter_grad, parallel_index * fourth, 1)

        down_grad = lax.dot_general(image_fourth, back, contract_rows, preferred_element_type=f32)
        up_grad = adapter_scale * jnp.stack(
            [
                lax.dot_general(low[:, :lowrank], kv_grad[:, :columns], contract_rows, preferred_element_type=f32),
                lax.dot_general(low[:, lowrank:], kv_grad[:, columns:], contract_rows, preferred_element_type=f32),
            ]
        )
        both = jnp.concatenate([down_grad, up_grad.reshape(-1, down_grad.shape[1])], axis=0)
        both = lax.psum_scatter(both, "dp", scatter_dimension=0, tiled=True)
        both = both.astype(bf16)

        send = image_grad[tokens:].astype(bf16)
        image_grad = (
            image_grad[:tokens]
            + shift(send[:tokens], dz=1).astype(f32)
            + shift(send[tokens : 2 * tokens], dz=2, opposite=True).astype(f32)
            + shift(send[2 * tokens :], dz=-1).astype(f32)
        )
        result = sum_over_mp(image_grad.astype(bf16), f32)
        both = lax.all_gather(both, "dp", axis=0, tiled=True)
        down_out = both[:fourth]
        up_out = both[fourth:].reshape(up_grad.shape)
        return (down_out[None], up_out[None], result[None])

    return body


def solution(mesh):
    in_specs = (
        P("dp", "segment", None),
        P("segment", "dp", None, "mp"),
        P("segment", "mp", None),
        P("segment", None, None, "mp"),
        P("segment", "dp", None, "mp"),
        P("segment", "dp", None, "mp"),
        P("dp"),
        P("dp"),
    )
    out_specs = (P("segment", "mp", None), P("segment", None, None, "mp"), P("dp", "segment", None))
    body = make_body(mesh)

    return jax.shard_map(body, mesh=mesh, in_specs=in_specs, out_specs=out_specs, check_vma=False)
```

time: 239 us -> 225 us (0.941)
  blocking collectives: 69.2 us -> 48 us
  starting transfers between devices: 60.7 us -> 81.7 us
  matrix products: 14.8 us -> 2.38 us
  Pallas kernels: 9.27 us -> 20.1 us
  waiting for transfers between devices: 50.1 us -> 43.8 us
  local copies, waits for them, and re-layouts: 10.5 us -> 6.31 us
    ppermute x15 -> x21, starting transfers between devices: 60.6 us -> 81.7 us  [shift(): return lax.ppermute(v, AXES, pairs)]
    all_gather x1 -> x0, blocking collectives: 16.9 us -> none  [body(): lax.all_gather(lax.dynamic_slice_in_dim(down, lax.axis_index('dp') * slic...]
    dot_general x8 -> x1, matrix products: 11.3 us -> 0.3 us  [body(): lax.dot_general(back, down, contracted_columns, preferred_element_type=f32)]
    pallas_call x1, Pallas kernels: 9.27 us -> 20.1 us  [layer(): pl.pallas_call(layer_kernel, grid=(2 * steps,), in_specs=[pl.BlockSpec((r...]
    ppermute x15 -> x21, waiting for transfers between devices: 44.8 us -> 38.8 us  [shift(): return lax.ppermute(v, AXES, pairs)]
    another operation x2 -> x0, local copies, waits for them, and re-layouts: 3.36 us -> none  [the longest x1 2.05 us: body(): query_rows = queries[0, 0].reshape(text_rows, local_kv, group, HD)]
    all_gather x1, blocking collectives: 18.1 us -> 15.5 us  [body(): both = lax.all_gather(both, 'dp', axis=0, tiled=True)]
    sub x1 -> x0, matrix products: 2.48 us -> none  [body(): shifted = jnp.exp(masked - row_top)]
  transfers between devices with their start and end apart: 18 -> 23, of which waited for: 9 -> 8; matrix products, arithmetic and copies ran while one was open for 11% -> 4% of each run, Pallas kernels for 0% -> 0%
where the time goes in v4:
time: 225 us; the launch traced here: 224 us
  starting transfers between devices  81.7 us (36%)
  blocking collectives  48 us (21%)
  waiting for transfers between devices  43.8 us (19%)
  Pallas kernels  20.1 us (9%)
  between operations  15.9 us (7%)
  local copies, waits for them, and re-layouts  6.31 us (3%)
  other arithmetic  6.05 us (3%)
  matrix products  2.38 us (1%)
    ppermute x21, starting transfers between devices, shift(): return lax.ppermute(v, AXES, pairs)  81.7 us
    ppermute x21, waiting for transfers between devices, shift(): return lax.ppermute(v, AXES, pairs)  38.8 us
    pallas_call x1, Pallas kernels, layer(): pl.pallas_call(layer_kernel, grid=(2 * steps,), in_specs=[pl.BlockSpec((r...  20.1 us
    all_gather x1, blocking collectives, body(): low = lax.all_gather(low, 'mp', axis=0)  16.4 us
    all_gather x1, blocking collectives, body(): back = lax.all_gather(back, 'mp', axis=0)  16.2 us
    all_gather x1, blocking collectives, body(): both = lax.all_gather(both, 'dp', axis=0, tiled=True)  15.5 us
    reduce_scatter x1, waiting for transfers between devices, body(): both = lax.psum_scatter(both, 'dp', scatter_dimension=0, tiled=True)  4.99 us
  transfers between devices with their start and end apart: 23, of which 8 were waited for; matrix products, arithmetic and copies ran while one was open for 4% of the time, Pallas kernels for 0%

profile of v4, /device:TPU:1, one launch (start us, length us, event | category | flops | bytes accessed | tf_op | source)
XLA Modules:
  0.0 224.3 jit_solution(8178427990314500234)
XLA Ops:
  7.2 2.5 %copy.11 = bf16[128,8,2,256]{3,1,2,0:T(8,128)(2,1)} copy(bf16[128,8,2,256]{3,2,1,0:T(2,128)(2,1)} %bitcast.36) | data formatting | bytes 2097152
  9.8 11.9 %collective-permute-start = (bf16[8,8192]{1,0:T(8,128)(2,1)S(1)}, bf16[8,8192]{1,0:T(8,128)(2,1)S(1)}, u32[]{:S(2)}, u32[]{:S(2)}) collective-permute-start(bf16[8,8192]{1,0:T(8,128)(2,1)S(1)} %bitcast.39), channel_id=1, source_target_pairs={{0,387},{1,384},{2,385},{3,386},{4,391},{5,388},{6,389},{7,390},{8... | collective-permute-start | bytes 393224 | tf_op jit(solution)/shard_map/ppermute | solution.py:155
  21.8 3.1 %collective-permute-start.1 = (bf16[8,8192]{1,0:T(8,128)(2,1)S(1)}, bf16[8,8192]{1,0:T(8,128)(2,1)S(1)}, u32[]{:S(2)}, u32[]{:S(2)}) collective-permute-start(bf16[8,8192]{1,0:T(8,128)(2,1)S(1)} %bitcast.40), channel_id=1, source_target_pairs={{0,256},{1,257},{2,258},{3,259},{4,263},{5,260},{6,261},{7,262},{8... | collective-permute-start | bytes 393224 | tf_op jit(solution)/shard_map/ppermute | solution.py:155
  24.9 2.6 %collective-permute-start.2 = (bf16[8,8192]{1,0:T(8,128)(2,1)S(1)}, bf16[8,8192]{1,0:T(8,128)(2,1)S(1)}, u32[]{:S(2)}, u32[]{:S(2)}) collective-permute-start(bf16[8,8192]{1,0:T(8,128)(2,1)S(1)} %bitcast.41), channel_id=1, source_target_pairs={{0,128},{1,129},{2,130},{3,131},{4,132},{5,133},{6,134},{7,135},{8... | collective-permute-start | bytes 393224 | tf_op jit(solution)/shard_map/ppermute | solution.py:155
  27.5 4.4 %collective-permute-start.3 = (bf16[8,8192]{1,0:T(8,128)(2,1)S(1)}, bf16[8,8192]{1,0:T(8,128)(2,1)S(1)}, u32[]{:S(2)}, u32[]{:S(2)}) collective-permute-start(bf16[8,8192]{1,0:T(8,128)(2,1)S(1)} %bitcast.42), channel_id=1, source_target_pairs={{0,96},{1,97},{2,98},{3,99},{4,100},{5,101},{6,102},{7,103},{8,104... | collective-permute-start | bytes 393224 | tf_op jit(solution)/shard_map/ppermute | solution.py:155
  31.9 2.4 %collective-permute-start.5 = (bf16[8,8192]{1,0:T(8,128)(2,1)S(1)}, bf16[8,8192]{1,0:T(8,128)(2,1)S(1)}, u32[]{:S(2)}, u32[]{:S(2)}) collective-permute-start(bf16[8,8192]{1,0:T(8,128)(2,1)S(1)} %bitcast.43), channel_id=1, source_target_pairs={{0,64},{1,65},{2,66},{3,67},{4,68},{5,69},{6,70},{7,71},{8,72},{9,... | collective-permute-start | bytes 393224 | tf_op jit(solution)/shard_map/ppermute | solution.py:155
  36.4 2.5 %collective-permute-start.7 = (bf16[8,8192]{1,0:T(8,128)(2,1)S(1)}, bf16[8,8192]{1,0:T(8,128)(2,1)S(1)}, u32[]{:S(2)}, u32[]{:S(2)}) collective-permute-start(bf16[8,8192]{1,0:T(8,128)(2,1)S(1)} %bitcast.44), channel_id=1, source_target_pairs={{0,32},{1,33},{2,34},{3,35},{4,36},{5,37},{6,38},{7,39},{8,40},{9,... | collective-permute-start | bytes 393224 | tf_op jit(solution)/shard_map/ppermute | solution.py:155
  39.0 4.0 %collective-permute-start.4 = (bf16[24,8192]{1,0:T(8,128)(2,1)S(1)}, bf16[24,8192]{1,0:T(8,128)(2,1)S(1)}, u32[]{:S(2)}, u32[]{:S(2)}) collective-permute-start(bf16[24,8192]{1,0:T(8,128)(2,1)S(1)} %get-tuple-element.21), channel_id=1, source_target_pairs={{0,96},{1,97},{2,98},{3,99},{4,100},{5,101},{6,102},{7,103},{8,104... | collective-permute-start | bytes 1179656 | tf_op jit(solution)/shard_map/ppermute | solution.py:155
  43.0 3.1 %collective-permute-start.6 = (bf16[24,8192]{1,0:T(8,128)(2,1)S(1)}, bf16[24,8192]{1,0:T(8,128)(2,1)S(1)}, u32[]{:S(2)}, u32[]{:S(2)}) collective-permute-start(bf16[24,8192]{1,0:T(8,128)(2,1)S(1)} %get-tuple-element.21), channel_id=1, source_target_pairs={{0,64},{1,65},{2,66},{3,67},{4,68},{5,69},{6,70},{7,71},{8,72},{9,... | collective-permute-start | bytes 1179656 | tf_op jit(solution)/shard_map/ppermute | solution.py:155
  46.2 1.9 collective-permute-start.8
  48.2 11.7 %collective-permute-done.4 = bf16[24,8192]{1,0:T(8,128)(2,1)S(1)} collective-permute-done((bf16[24,8192]{1,0:T(8,128)(2,1)S(1)}, bf16[24,8192]{1,0:T(8,128)(2,1)S(1)}, u32[]{:S(2)}, u32[]{:S(2)}) %collective-permute-start.4) | collective-permute-done | bytes 393248 | tf_op jit(solution)/shard_map/ppermute | solution.py:155
  60.0 6.0 %collective-permute-done.8 = bf16[24,8192]{1,0:T(8,128)(2,1)S(1)} collective-permute-done((bf16[24,8192]{1,0:T(8,128)(2,1)S(1)}, bf16[24,8192]{1,0:T(8,128)(2,1)S(1)}, u32[]{:S(2)}, u32[]{:S(2)}) %collective-permute-start.8) | collective-permute-done | bytes 393248 | tf_op jit(solution)/shard_map/ppermute | solution.py:155
  66.4 16.4 %all-gather = f32[512,128]{1,0:T(8,128)S(1)} all-gather(f32[128,128]{1,0:T(8,128)S(1)} %fusion.2), channel_id=2, replica_groups=mesh['segment'=16,'dp'=8,'mp'=4] {'mp'}, dimensions={0}, use_global_device_ids=true | all-gather | bytes 327680 | tf_op jit(solution)/shard_map/all_gather | solution.py:208
  84.7 20.1 %layer.1 = (bf16[128,512]{1,0:T(8,128)(2,1)}, f32[128,128]{1,0:T(8,128)}, f32[32,8192]{1,0:T(8,128)}, bf16[32,8192]{1,0:T(8,128)(2,1)}, bf16[32,8192]{1,0:T(8,128)(2,1)}, /*index=5*/bf16[32,8192]{1,0:T(8,128)(2,1)}) custom-call(bf16[128,8192]{1,0:T(8,128)(2,1)} %copy-done.1, bf16[8192,512]{1,0:T(8,128)(2,1)} %all-gather.4.cloned.1.call-done.weight_ref, ...), custom_call_target="tpu_custom_call" | custom-call | tf_op jit(solution)/shard_map/layer/pallas_call | solution.py:111
  104.8 2.6 %collective-permute-start.10 = (bf16[32,8192]{1,0:T(8,128)(2,1)}, bf16[32,8192]{1,0:T(8,128)(2,1)S(1)}, u32[]{:S(2)}, u32[]{:S(2)}) collective-permute-start(bf16[32,8192]{1,0:T(8,128)(2,1)} %get-tuple-element.13), channel_id=1, source_target_pairs={{0,64},{1,65},{2,66},{3,67},{4,68},{5,69},{6,70},{7,71},{8,72},{9,... | collective-permute-start | bytes 1572872 | tf_op jit(solution)/shard_map/ppermute | solution.py:155
  107.4 2.7 %collective-permute-start.11 = (bf16[32,8192]{1,0:T(8,128)(2,1)}, bf16[32,8192]{1,0:T(8,128)(2,1)}, u32[]{:S(2)}, u32[]{:S(2)}) collective-permute-start(bf16[32,8192]{1,0:T(8,128)(2,1)} %get-tuple-element.14), channel_id=1, source_target_pairs={{0,96},{1,97},{2,98},{3,99},{4,100},{5,101},{6,102},{7,103},{8,104... | collective-permute-start | bytes 1572872 | tf_op jit(solution)/shard_map/ppermute | solution.py:155
  110.1 2.6 %collective-permute-start.9 = (bf16[32,8192]{1,0:T(8,128)(2,1)}, bf16[32,8192]{1,0:T(8,128)(2,1)}, u32[]{:S(2)}, u32[]{:S(2)}) collective-permute-start(bf16[32,8192]{1,0:T(8,128)(2,1)} %get-tuple-element.12), channel_id=1, source_target_pairs={{0,32},{1,33},{2,34},{3,35},{4,36},{5,37},{6,38},{7,39},{8,40},{9,... | collective-permute-start | bytes 1572872 | tf_op jit(solution)/shard_map/ppermute | solution.py:155
  112.7 16.2 %all-gather.1 = f32[512,128]{1,0:T(8,128)S(1)} all-gather(f32[128,128]{1,0:T(8,128)} %get-tuple-element.9), channel_id=3, replica_groups=mesh['segment'=16,'dp'=8,'mp'=4] {'mp'}, dimensions={0}, use_global_device_ids=true | all-gather | bytes 327680 | tf_op jit(solution)/shard_map/all_gather | solution.py:235
  129.9 3.2 %collective-permute-start.12 = (bf16[32,2048]{1,0:T(8,128)(2,1)}, bf16[32,2048]{1,0:T(8,128)(2,1)S(1)}, u32[]{:S(2)}, u32[]{:S(2)}) collective-permute-start(bf16[32,2048]{1,0:T(8,128)(2,1)} %get-tuple-element.18), channel_id=1, source_target_pairs={{0,32},{1,33},{2,34},{3,35},{4,36},{5,37},{6,38},{7,39},{8,40},{9,... | collective-permute-start | bytes 393224 | tf_op jit(solution)/shard_map/ppermute | solution.py:155
  133.1 3.9 %collective-permute-start.13 = (bf16[32,2048]{1,0:T(8,128)(2,1)}, bf16[32,2048]{1,0:T(8,128)(2,1)S(1)}, u32[]{:S(2)}, u32[]{:S(2)}) collective-permute-start(bf16[32,2048]{1,0:T(8,128)(2,1)} %get-tuple-element.20), channel_id=1, source_target_pairs={{0,64},{1,65},{2,66},{3,67},{4,68},{5,69},{6,70},{7,71},{8,72},{9,... | collective-permute-start | bytes 393224 | tf_op jit(solution)/shard_map/ppermute | solution.py:155
  138.8 3.3 %collective-permute-start.14 = (bf16[32,2048]{1,0:T(8,128)(2,1)}, bf16[32,2048]{1,0:T(8,128)(2,1)S(1)}, u32[]{:S(2)}, u32[]{:S(2)}) collective-permute-start(bf16[32,2048]{1,0:T(8,128)(2,1)} %get-tuple-element.19), channel_id=1, source_target_pairs={{0,96},{1,97},{2,98},{3,99},{4,100},{5,101},{6,102},{7,103},{8,104... | collective-permute-start | bytes 393224 | tf_op jit(solution)/shard_map/ppermute | solution.py:155
  145.2 2.3 %collective-permute-start.15 = (bf16[8,8192]{1,0:T(8,128)(2,1)S(1)}, bf16[8,8192]{1,0:T(8,128)(2,1)S(1)}, u32[]{:S(2)}, u32[]{:S(2)}) collective-permute-start(bf16[8,8192]{1,0:T(8,128)(2,1)S(1)} %get-tuple-element.15), channel_id=1, source_target_pairs={{0,128},{1,129},{2,130},{3,131},{4,132},{5,133},{6,134},{7,135},{8... | collective-permute-start | bytes 393224 | tf_op jit(solution)/shard_map/ppermute | solution.py:155
  147.5 6.7 %collective-permute-start.16 = (bf16[8,8192]{1,0:T(8,128)(2,1)S(1)}, bf16[8,8192]{1,0:T(8,128)(2,1)S(1)}, u32[]{:S(2)}, u32[]{:S(2)}) collective-permute-start(bf16[8,8192]{1,0:T(8,128)(2,1)S(1)} %get-tuple-element.17), channel_id=1, source_target_pairs={{0,256},{1,257},{2,258},{3,259},{4,263},{5,260},{6,261},{7,262},{8... | collective-permute-start | bytes 393224 | tf_op jit(solution)/shard_map/ppermute | solution.py:155
  154.3 1.9 collective-permute-start.17
  157.3 2.0 collective-permute-done.16
  161.0 7.3 %collective-permute-start.18 = (bf16[8,8192]{1,0:T(8,128)(2,1)S(1)}, bf16[8,8192]{1,0:T(8,128)(2,1)S(1)}, u32[]{:S(2)}, u32[]{:S(2)}) collective-permute-start(bf16[8,8192]{1,0:T(8,128)(2,1)S(1)} %fusion.9), channel_id=1, source_target_pairs={{0,2},{1,3},{2,0},{3,1},{4,6},{5,7},{6,4},{7,5},{8,10},{9,11},{10,... | collective-permute-start | bytes 393224 | tf_op jit(solution)/shard_map/ppermute | solution.py:155
  168.4 5.8 %collective-permute-start.19 = (bf16[8,8192]{1,0:T(8,128)(2,1)S(1)}, bf16[8,8192]{1,0:T(8,128)(2,1)S(1)}, u32[]{:S(2)}, u32[]{:S(2)}) collective-permute-start(bf16[8,8192]{1,0:T(8,128)(2,1)S(1)} %fusion.9), channel_id=1, source_target_pairs={{0,1},{1,2},{2,3},{3,0},{4,5},{5,6},{6,7},{7,4},{8,9},{9,10},{10,1... | collective-permute-start | bytes 393224 | tf_op jit(solution)/shard_map/ppermute | solution.py:155
  174.2 3.4 %collective-permute-start.20 = (bf16[8,8192]{1,0:T(8,128)(2,1)S(1)}, bf16[8,8192]{1,0:T(8,128)(2,1)S(1)}, u32[]{:S(2)}, u32[]{:S(2)}) collective-permute-start(bf16[8,8192]{1,0:T(8,128)(2,1)S(1)} %fusion.9), channel_id=1, source_target_pairs={{0,3},{1,0},{2,1},{3,2},{4,7},{5,4},{6,5},{7,6},{8,11},{9,8},{10,9... | collective-permute-start | bytes 393224 | tf_op jit(solution)/shard_map/ppermute | solution.py:155
  177.6 8.5 %collective-permute-done.19 = bf16[8,8192]{1,0:T(8,128)(2,1)S(1)} collective-permute-done((bf16[8,8192]{1,0:T(8,128)(2,1)S(1)}, bf16[8,8192]{1,0:T(8,128)(2,1)S(1)}, u32[]{:S(2)}, u32[]{:S(2)}) %collective-permute-start.19) | collective-permute-done | bytes 131104 | tf_op jit(solution)/shard_map/ppermute | solution.py:155
  186.1 7.8 %collective-permute-done.20 = bf16[8,8192]{1,0:T(8,128)(2,1)S(1)} collective-permute-done((bf16[8,8192]{1,0:T(8,128)(2,1)S(1)}, bf16[8,8192]{1,0:T(8,128)(2,1)S(1)}, u32[]{:S(2)}, u32[]{:S(2)}) %collective-permute-start.20) | collective-permute-done | bytes 131104 | tf_op jit(solution)/shard_map/ppermute | solution.py:155
  194.6 5.0 %reduce-scatter.2.cloned.1.call-done = f32[288,128]{1,0:T(8,128)} async-done(((f32[2304,128]{1,0:T(8,128)}), f32[288,128]{1,0:T(8,128)}) %reduce-scatter.2.cloned.1.call-update) | async-done | bytes 147472 | tf_op jit(solution)/shard_map/reduce_scatter | solution.py:257
  200.5 15.5 %all_gather.23 = bf16[2304,128]{1,0:T(8,128)(2,1)S(1)} all-gather(bf16[288,128]{1,0:T(8,128)(2,1)S(1)} %convert_element_type.73), channel_id=1, replica_groups=mesh['segment'=16,'dp'=8,'mp'=4] {'dp'}, dimensions={0}, use_global_device_ids=true | all-gather | bytes 663552 | tf_op jit(solution)/shard_map/all_gather | solution.py:268
  (70 shorter events, 15.1 us)
Async XLA Ops:
  7.2 58.9 %copy-start = (bf16[1,2048,128]{2,1,0:T(8,128)(2,1)S(1)}, bf16[1,2048,128]{2,1,0:T(8,128)(2,1)}, u32[]{:S(2)}) copy-start(bf16[1,2048,128]{2,1,0:T(8,128)(2,1)} %param.10) | copy-start | bytes 1572868
  7.2 2.6 %copy-start.3 = (bf16[1,8,8192]{2,1,0:T(8,128)(2,1)S(1)}, bf16[1,8,8192]{2,1,0:T(8,128)(2,1)}, u32[]{:S(2)}) copy-start(bf16[1,8,8192]{2,1,0:T(8,128)(2,1)} %param.8) | copy-start | bytes 393220
  7.2 28.5 %copy-start.5 = (bf16[1,2,64,256]{3,2,1,0:T(8,128)(2,1)S(1)}, bf16[1,2,64,256]{3,2,1,0:T(8,128)(2,1)}, u32[]{:S(2)}) copy-start(bf16[1,2,64,256]{3,2,1,0:T(8,128)(2,1)} %param.11) | copy-start | bytes 196612
  7.2 76.2 %all-gather.4.cloned.1.call-start = ((), (), s32[]{:S(2)}) async-start(), calls=%async_computation.1 | async-start | bytes 9437184 | tf_op jit(solution)/shard_map/all_gather | solution.py:205
  9.8 189.8 %reduce-scatter.2.cloned.1.call-start = ((), (), s32[]{:S(2)}) async-start(), calls=%async_computation.2 | async-start | bytes 1327104 | tf_op jit(solution)/shard_map/reduce_scatter | solution.py:257
  9.8 26.6 %collective-permute-start = (bf16[8,8192]{1,0:T(8,128)(2,1)S(1)}, bf16[8,8192]{1,0:T(8,128)(2,1)S(1)}, u32[]{:S(2)}, u32[]{:S(2)}) collective-permute-start(bf16[8,8192]{1,0:T(8,128)(2,1)S(1)} %bitcast.39), channel_id=1, source_target_pairs={{0,387},{1,384},{2,385},{3,386},{4,391},{5,388},{6,389},{7,390},{8... | collective-permute-start | bytes 393224 | tf_op jit(solution)/shard_map/ppermute | solution.py:155
  21.8 17.2 %collective-permute-start.1 = (bf16[8,8192]{1,0:T(8,128)(2,1)S(1)}, bf16[8,8192]{1,0:T(8,128)(2,1)S(1)}, u32[]{:S(2)}, u32[]{:S(2)}) collective-permute-start(bf16[8,8192]{1,0:T(8,128)(2,1)S(1)} %bitcast.40), channel_id=1, source_target_pairs={{0,256},{1,257},{2,258},{3,259},{4,263},{5,260},{6,261},{7,262},{8... | collective-permute-start | bytes 393224 | tf_op jit(solution)/shard_map/ppermute | solution.py:155
  24.9 14.1 %collective-permute-start.2 = (bf16[8,8192]{1,0:T(8,128)(2,1)S(1)}, bf16[8,8192]{1,0:T(8,128)(2,1)S(1)}, u32[]{:S(2)}, u32[]{:S(2)}) collective-permute-start(bf16[8,8192]{1,0:T(8,128)(2,1)S(1)} %bitcast.41), channel_id=1, source_target_pairs={{0,128},{1,129},{2,130},{3,131},{4,132},{5,133},{6,134},{7,135},{8... | collective-permute-start | bytes 393224 | tf_op jit(solution)/shard_map/ppermute | solution.py:155
  27.5 18.7 %collective-permute-start.3 = (bf16[8,8192]{1,0:T(8,128)(2,1)S(1)}, bf16[8,8192]{1,0:T(8,128)(2,1)S(1)}, u32[]{:S(2)}, u32[]{:S(2)}) collective-permute-start(bf16[8,8192]{1,0:T(8,128)(2,1)S(1)} %bitcast.42), channel_id=1, source_target_pairs={{0,96},{1,97},{2,98},{3,99},{4,100},{5,101},{6,102},{7,103},{8,104... | collective-permute-start | bytes 393224 | tf_op jit(solution)/shard_map/ppermute | solution.py:155
  31.9 28.0 %collective-permute-start.5 = (bf16[8,8192]{1,0:T(8,128)(2,1)S(1)}, bf16[8,8192]{1,0:T(8,128)(2,1)S(1)}, u32[]{:S(2)}, u32[]{:S(2)}) collective-permute-start(bf16[8,8192]{1,0:T(8,128)(2,1)S(1)} %bitcast.43), channel_id=1, source_target_pairs={{0,64},{1,65},{2,66},{3,67},{4,68},{5,69},{6,70},{7,71},{8,72},{9,... | collective-permute-start | bytes 393224 | tf_op jit(solution)/shard_map/ppermute | solution.py:155
  36.4 23.5 %collective-permute-start.7 = (bf16[8,8192]{1,0:T(8,128)(2,1)S(1)}, bf16[8,8192]{1,0:T(8,128)(2,1)S(1)}, u32[]{:S(2)}, u32[]{:S(2)}) collective-permute-start(bf16[8,8192]{1,0:T(8,128)(2,1)S(1)} %bitcast.44), channel_id=1, source_target_pairs={{0,32},{1,33},{2,34},{3,35},{4,36},{5,37},{6,38},{7,39},{8,40},{9,... | collective-permute-start | bytes 393224 | tf_op jit(solution)/shard_map/ppermute | solution.py:155
  39.0 20.8 %collective-permute-start.4 = (bf16[24,8192]{1,0:T(8,128)(2,1)S(1)}, bf16[24,8192]{1,0:T(8,128)(2,1)S(1)}, u32[]{:S(2)}, u32[]{:S(2)}) collective-permute-start(bf16[24,8192]{1,0:T(8,128)(2,1)S(1)} %get-tuple-element.21), channel_id=1, source_target_pairs={{0,96},{1,97},{2,98},{3,99},{4,100},{5,101},{6,102},{7,103},{8,104... | collective-permute-start | bytes 1179656 | tf_op jit(solution)/shard_map/ppermute | solution.py:155
  43.0 16.9 %collective-permute-start.6 = (bf16[24,8192]{1,0:T(8,128)(2,1)S(1)}, bf16[24,8192]{1,0:T(8,128)(2,1)S(1)}, u32[]{:S(2)}, u32[]{:S(2)}) collective-permute-start(bf16[24,8192]{1,0:T(8,128)(2,1)S(1)} %get-tuple-element.21), channel_id=1, source_target_pairs={{0,64},{1,65},{2,66},{3,67},{4,68},{5,69},{6,70},{7,71},{8,72},{9,... | collective-permute-start | bytes 1179656 | tf_op jit(solution)/shard_map/ppermute | solution.py:155
  46.2 19.8 %collective-permute-start.8 = (bf16[24,8192]{1,0:T(8,128)(2,1)S(1)}, bf16[24,8192]{1,0:T(8,128)(2,1)S(1)}, u32[]{:S(2)}, u32[]{:S(2)}) collective-permute-start(bf16[24,8192]{1,0:T(8,128)(2,1)S(1)} %get-tuple-element.21), channel_id=1, source_target_pairs={{0,32},{1,33},{2,34},{3,35},{4,36},{5,37},{6,38},{7,39},{8,40},{9,... | collective-permute-start | bytes 1179656 | tf_op jit(solution)/shard_map/ppermute | solution.py:155
  66.1 18.6 %copy-start.1 = (bf16[128,8192]{1,0:T(8,128)(2,1)}, bf16[128,8192]{1,0:T(8,128)(2,1)S(1)}, u32[]{:S(2)}) copy-start(bf16[128,8192]{1,0:T(8,128)(2,1)S(1)} %constant_dynamic-update-slice_fusion.3.image_ref) | copy-start | bytes 6291460
  104.8 32.2 %copy-start.2 = (bf16[128,128]{1,0:T(8,128)(2,1)S(1)}, bf16[128,128]{1,0:T(8,128)(2,1)}, u32[]{:S(2)}) copy-start(bf16[128,128]{1,0:T(8,128)(2,1)} %reduce_sum.18.low_ref) | copy-start | bytes 98308
  104.8 32.2 %copy-start.4 = (bf16[128,512]{1,0:T(8,128)(2,1)S(1)}, bf16[128,512]{1,0:T(8,128)(2,1)}, u32[]{:S(2)}) copy-start(bf16[128,512]{1,0:T(8,128)(2,1)} %get-tuple-element.10) | copy-start | bytes 393220
  104.8 34.0 %collective-permute-start.10 = (bf16[32,8192]{1,0:T(8,128)(2,1)}, bf16[32,8192]{1,0:T(8,128)(2,1)S(1)}, u32[]{:S(2)}, u32[]{:S(2)}) collective-permute-start(bf16[32,8192]{1,0:T(8,128)(2,1)} %get-tuple-element.13), channel_id=1, source_target_pairs={{0,64},{1,65},{2,66},{3,67},{4,68},{5,69},{6,70},{7,71},{8,72},{9,... | collective-permute-start | bytes 1572872 | tf_op jit(solution)/shard_map/ppermute | solution.py:155
  107.4 34.8 %collective-permute-start.11 = (bf16[32,8192]{1,0:T(8,128)(2,1)}, bf16[32,8192]{1,0:T(8,128)(2,1)}, u32[]{:S(2)}, u32[]{:S(2)}) collective-permute-start(bf16[32,8192]{1,0:T(8,128)(2,1)} %get-tuple-element.14), channel_id=1, source_target_pairs={{0,96},{1,97},{2,98},{3,99},{4,100},{5,101},{6,102},{7,103},{8,104... | collective-permute-start | bytes 1572872 | tf_op jit(solution)/shard_map/ppermute | solution.py:155
  110.1 32.1 %collective-permute-start.9 = (bf16[32,8192]{1,0:T(8,128)(2,1)}, bf16[32,8192]{1,0:T(8,128)(2,1)}, u32[]{:S(2)}, u32[]{:S(2)}) collective-permute-start(bf16[32,8192]{1,0:T(8,128)(2,1)} %get-tuple-element.12), channel_id=1, source_target_pairs={{0,32},{1,33},{2,34},{3,35},{4,36},{5,37},{6,38},{7,39},{8,40},{9,... | collective-permute-start | bytes 1572872 | tf_op jit(solution)/shard_map/ppermute | solution.py:155
  129.9 14.0 %collective-permute-start.12 = (bf16[32,2048]{1,0:T(8,128)(2,1)}, bf16[32,2048]{1,0:T(8,128)(2,1)S(1)}, u32[]{:S(2)}, u32[]{:S(2)}) collective-permute-start(bf16[32,2048]{1,0:T(8,128)(2,1)} %get-tuple-element.18), channel_id=1, source_target_pairs={{0,32},{1,33},{2,34},{3,35},{4,36},{5,37},{6,38},{7,39},{8,40},{9,... | collective-permute-start | bytes 393224 | tf_op jit(solution)/shard_map/ppermute | solution.py:155
  133.1 10.8 %collective-permute-start.13 = (bf16[32,2048]{1,0:T(8,128)(2,1)}, bf16[32,2048]{1,0:T(8,128)(2,1)S(1)}, u32[]{:S(2)}, u32[]{:S(2)}) collective-permute-start(bf16[32,2048]{1,0:T(8,128)(2,1)} %get-tuple-element.20), channel_id=1, source_target_pairs={{0,64},{1,65},{2,66},{3,67},{4,68},{5,69},{6,70},{7,71},{8,72},{9,... | collective-permute-start | bytes 393224 | tf_op jit(solution)/shard_map/ppermute | solution.py:155
  138.8 6.2 %collective-permute-start.14 = (bf16[32,2048]{1,0:T(8,128)(2,1)}, bf16[32,2048]{1,0:T(8,128)(2,1)S(1)}, u32[]{:S(2)}, u32[]{:S(2)}) collective-permute-start(bf16[32,2048]{1,0:T(8,128)(2,1)} %get-tuple-element.19), channel_id=1, source_target_pairs={{0,96},{1,97},{2,98},{3,99},{4,100},{5,101},{6,102},{7,103},{8,104... | collective-permute-start | bytes 393224 | tf_op jit(solution)/shard_map/ppermute | solution.py:155
  145.2 12.1 %collective-permute-start.15 = (bf16[8,8192]{1,0:T(8,128)(2,1)S(1)}, bf16[8,8192]{1,0:T(8,128)(2,1)S(1)}, u32[]{:S(2)}, u32[]{:S(2)}) collective-permute-start(bf16[8,8192]{1,0:T(8,128)(2,1)S(1)} %get-tuple-element.15), channel_id=1, source_target_pairs={{0,128},{1,129},{2,130},{3,131},{4,132},{5,133},{6,134},{7,135},{8... | collective-permute-start | bytes 393224 | tf_op jit(solution)/shard_map/ppermute | solution.py:155
  147.5 11.8 %collective-permute-start.16 = (bf16[8,8192]{1,0:T(8,128)(2,1)S(1)}, bf16[8,8192]{1,0:T(8,128)(2,1)S(1)}, u32[]{:S(2)}, u32[]{:S(2)}) collective-permute-start(bf16[8,8192]{1,0:T(8,128)(2,1)S(1)} %get-tuple-element.17), channel_id=1, source_target_pairs={{0,256},{1,257},{2,258},{3,259},{4,263},{5,260},{6,261},{7,262},{8... | collective-permute-start | bytes 393224 | tf_op jit(solution)/shard_map/ppermute | solution.py:155
  154.3 6.7 %collective-permute-start.17 = (bf16[8,8192]{1,0:T(8,128)(2,1)S(1)}, bf16[8,8192]{1,0:T(8,128)(2,1)S(1)}, u32[]{:S(2)}, u32[]{:S(2)}) collective-permute-start(bf16[8,8192]{1,0:T(8,128)(2,1)S(1)} %get-tuple-element.16), channel_id=1, source_target_pairs={{0,387},{1,384},{2,385},{3,386},{4,391},{5,388},{6,389},{7,390},{8... | collective-permute-start | bytes 393224 | tf_op jit(solution)/shard_map/ppermute | solution.py:155
  161.0 16.5 %collective-permute-start.18 = (bf16[8,8192]{1,0:T(8,128)(2,1)S(1)}, bf16[8,8192]{1,0:T(8,128)(2,1)S(1)}, u32[]{:S(2)}, u32[]{:S(2)}) collective-permute-start(bf16[8,8192]{1,0:T(8,128)(2,1)S(1)} %fusion.9), channel_id=1, source_target_pairs={{0,2},{1,3},{2,0},{3,1},{4,6},{5,7},{6,4},{7,5},{8,10},{9,11},{10,... | collective-permute-start | bytes 393224 | tf_op jit(solution)/shard_map/ppermute | solution.py:155
  168.4 17.7 %collective-permute-start.19 = (bf16[8,8192]{1,0:T(8,128)(2,1)S(1)}, bf16[8,8192]{1,0:T(8,128)(2,1)S(1)}, u32[]{:S(2)}, u32[]{:S(2)}) collective-permute-start(bf16[8,8192]{1,0:T(8,128)(2,1)S(1)} %fusion.9), channel_id=1, source_target_pairs={{0,1},{1,2},{2,3},{3,0},{4,5},{5,6},{6,7},{7,4},{8,9},{9,10},{10,1... | collective-permute-start | bytes 393224 | tf_op jit(solution)/shard_map/ppermute | solution.py:155
  174.2 19.6 %collective-permute-start.20 = (bf16[8,8192]{1,0:T(8,128)(2,1)S(1)}, bf16[8,8192]{1,0:T(8,128)(2,1)S(1)}, u32[]{:S(2)}, u32[]{:S(2)}) collective-permute-start(bf16[8,8192]{1,0:T(8,128)(2,1)S(1)} %fusion.9), channel_id=1, source_target_pairs={{0,3},{1,0},{2,1},{3,2},{4,7},{5,4},{6,5},{7,6},{8,11},{9,8},{10,9... | collective-permute-start | bytes 393224 | tf_op jit(solution)/shard_map/ppermute | solution.py:155
Sparse Core Ops, SparseCore 0:
  10.2 63.0 all-gather.3
  157.4 42.1 reduce-scatter.1

commit v5 on v4

--- a/solution.py
+++ b/solution.py
@@ -19,13 +19,16 @@
 AXES = ("segment", "dp", "mp")
 
 
+CHUNKS = 8
+
+
 def layer_kernel(
-    image_ref,
-    weight_ref,
+    image_hbm,
+    weight_hbm,
+    query_hbm,
+    cot_hbm,
     low_ref,
     up_ref,
-    query_ref,
-    cot_ref,
     valid_ref,
     live_ref,
     kv_grad_ref,
@@ -33,108 +36,96 @@
     own_ref,
     *rest,
 ):
-    *away_refs, sum_ref = rest
-    step = pl.program_id(0)
-    forward_steps = pl.num_programs(0) // 2
+    *away_refs, image_ref, weight_ref, query_ref, cot_ref, sems = rest
     columns = weight_ref.shape[1] // 2
     local_kv = columns // HD
     group = query_ref.shape[1] // HD // local_kv
     block = own_ref.shape[0]
-
-    @pl.when(step < forward_steps)
-    def _():
-        part = jnp.dot(image_ref[...], weight_ref[...], preferred_element_type=f32)
-
-        @pl.when(step == 0)
-        def _():
-            sum_ref[...] = part
-
-        @pl.when(step > 0)
-        def _():
-            sum_ref[...] += part
-
-    @pl.when(step == forward_steps - 1)
-    def _():
-        adapted = jnp.dot(low_ref[...], up_ref[...], preferred_element_type=f32)
-        key_value = (sum_ref[...] + adapter_scale * adapted).astype(bf16)
-        valid = valid_ref[...] > 0
-        live = live_ref[0:1, :]
-        for g in range(local_kv):
-            key_at, value_at = g * HD, columns + g * HD
-            keys = key_value[:, key_at : key_at + HD]
-            values = key_value[:, value_at : value_at + HD]
-            key_grad = value_grad = None
-            for r in range(group):
-                at = (g * group + r) * HD
-                query, cot = query_ref[:, at : at + HD], cot_ref[:, at : at + HD]
-                scores = lax.dot_general(keys, query, contracted_columns, preferred_element_type=f32) * HD ** (-0.5)
-                masked = jnp.where(valid, scores, -1e30)
-                shifted = jnp.exp(masked - jnp.max(masked, axis=0, keepdims=True))
-                attention = shifted * (1.0 / jnp.sum(shifted, axis=0, keepdims=True))
-                dweights = lax.dot_general(values, cot, contracted_columns, preferred_element_type=f32)
-                delta = jnp.sum(attention * dweights, axis=0, keepdims=True)
-                dscore = (attention * (dweights - delta) * (live * HD ** (-0.5))).astype(bf16)
-                kept = (attention * live).astype(bf16)
-                dk = jnp.dot(dscore, query, preferred_element_type=f32)
-                dv = jnp.dot(kept, cot, preferred_element_type=f32)
-                key_grad = dk if r == 0 else key_grad + dk
-                value_grad = dv if r == 0 else value_grad + dv
-            kv_grad_ref[:, key_at : key_at + HD] = key_grad.astype(bf16)
-            kv_grad_ref[:, value_at : value_at + HD] = value_grad.astype(bf16)
-        back_ref[...] = adapter_scale * lax.dot_general(
-            kv_grad_ref[...], up_ref[...], contracted_columns, preferred_element_type=f32
-        )
-
-    @pl.when(step >= forward_steps)
-    def _():
-        total = lax.dot_general(kv_grad_ref[...], weight_ref[...], contracted_columns, preferred_element_type=f32)
-        own_ref[...] = total[:block]
+    share = weight_ref.shape[0] // CHUNKS
+
+    def chunk(c):
+        return pl.ds(c * share, share)
+
+    image_copy = pltpu.make_async_copy(image_hbm, image_ref, sems.at[CHUNKS])
+    query_copy = pltpu.make_async_copy(query_hbm, query_ref, sems.at[CHUNKS + 1])
+    cot_copy = pltpu.make_async_copy(cot_hbm, cot_ref, sems.at[CHUNKS + 2])
+    weight_copies = [
+        pltpu.make_async_copy(weight_hbm.at[chunk(c)], weight_ref.at[chunk(c)], sems.at[c]) for c in range(CHUNKS)
+    ]
+    image_copy.start()
+    for copy in weight_copies:
+        copy.start()
+    query_copy.start()
+    cot_copy.start()
+
+    key_value = adapter_scale * jnp.dot(low_ref[...], up_ref[...], preferred_element_type=f32)
+    image_copy.wait()
+    for c, copy in enumerate(weight_copies):
+        copy.wait()
+        key_value += jnp.dot(image_ref[:, chunk(c)], weight_ref[chunk(c), :], preferred_element_type=f32)
+    key_value = key_value.astype(bf16)
+    query_copy.wait()
+    cot_copy.wait()
+    valid = valid_ref[...] > 0
+    live = live_ref[0:1, :]
+    for g in range(local_kv):
+        key_at, value_at = g * HD, columns + g * HD
+        keys = key_value[:, key_at : key_at + HD]
+        values = key_value[:, value_at : value_at + HD]
+        key_grad = value_grad = None
+        for r in range(group):
+            at = (g * group + r) * HD
+            query, cot = query_ref[:, at : at + HD], cot_ref[:, at : at + HD]
+            scores = lax.dot_general(keys, query, contracted_columns, preferred_element_type=f32) * HD ** (-0.5)
+            masked = jnp.where(valid, scores, -1e30)
+            shifted = jnp.exp(masked - jnp.max(masked, axis=0, keepdims=True))
+            attention = shifted * (1.0 / jnp.sum(shifted, axis=0, keepdims=True))
+            dweights = lax.dot_general(values, cot, contracted_columns, preferred_element_type=f32)
+            delta = jnp.sum(attention * dweights, axis=0, keepdims=True)
+            dscore = (attention * (dweights - delta) * (live * HD ** (-0.5))).astype(bf16)
+            kept = (attention * live).astype(bf16)
+            dk = jnp.dot(dscore, query, preferred_element_type=f32)
+            dv = jnp.dot(kept, cot, preferred_element_type=f32)
+            key_grad = dk if r == 0 else key_grad + dk
+            value_grad = dv if r == 0 else value_grad + dv
+        kv_grad_ref[:, key_at : key_at + HD] = key_grad.astype(bf16)
+        kv_grad_ref[:, value_at : value_at + HD] = value_grad.astype(bf16)
+    kv_grad = kv_grad_ref[...]
+    back = adapter_scale * lax.dot_general(kv_grad, up_ref[...], contracted_columns, preferred_element_type=f32)
+    back_ref[...] = back.astype(bf16)
+    for c in range(CHUNKS):
+        total = lax.dot_general(kv_grad, weight_ref[chunk(c), :], contracted_columns, preferred_element_type=f32)
+        own_ref[:, chunk(c)] = total[:block]
         for i, ref in enumerate(away_refs):
-            ref[...] = total[(i + 1) * block : (i + 2) * block].astype(bf16)
+            ref[:, chunk(c)] = total[(i + 1) * block : (i + 2) * block].astype(bf16)
 
 
 def layer(image, weight, low, up, query, cot, valid, live):
     rows, width = image.shape
     columns = weight.shape[1]
     rank = low.shape[1]
-    steps = 8
-    share = width // steps
     block = rows // SIDE
-
-    def whole(v):
-        return pl.BlockSpec(v.shape, lambda j: (0, 0))
-
-    def turn(j):
-        return jnp.minimum(j, 2 * steps - 1 - j)
-
-    out_spec = pl.BlockSpec((block, share), lambda j: (0, jnp.minimum(steps - 1, 2 * steps - 1 - j)))
+    outside = pl.BlockSpec(memory_space=pl.ANY)
+    inside_vmem = pl.BlockSpec(memory_space=pltpu.VMEM)
     return pl.pallas_call(
         layer_kernel,
-        grid=(2 * steps,),
-        in_specs=[
-            pl.BlockSpec((rows, share), lambda j: (0, jnp.minimum(j, steps - 1))),
-            pl.BlockSpec((share, columns), lambda j: (turn(j), 0)),
-            whole(low),
-            whole(up),
-            whole(query),
-            whole(cot),
-            whole(valid),
-            whole(live),
-        ],
-        out_specs=[
-            pl.BlockSpec((rows, columns), lambda j: (0, 0)),
-            pl.BlockSpec((rows, rank), lambda j: (0, 0)),
-        ]
-        + [out_spec] * SIDE,
+        in_specs=[outside] * 4 + [inside_vmem] * 4,
+        out_specs=[inside_vmem] * (2 + SIDE),
         out_shape=[
             jax.ShapeDtypeStruct((rows, columns), bf16),
-            jax.ShapeDtypeStruct((rows, rank), f32),
+            jax.ShapeDtypeStruct((rows, rank), bf16),
             jax.ShapeDtypeStruct((block, width), f32),
         ]
         + [jax.ShapeDtypeStruct((block, width), bf16)] * (SIDE - 1),
-        scratch_shapes=[pltpu.VMEM((rows, columns), f32)],
+        scratch_shapes=[
+            pltpu.VMEM(image.shape, bf16),
+            pltpu.VMEM(weight.shape, bf16),
+            pltpu.VMEM(query.shape, bf16),
+            pltpu.VMEM(cot.shape, bf16),
+            pltpu.SemaphoreType.DMA((CHUNKS + 3,)),
+        ],
         name="layer",
-    )(image, weight, low, up, query, cot, valid, live)
+    )(image, weight, query, cot, low, up, valid, live)
 
 
 def make_body(mesh):
@@ -214,6 +205,8 @@
         )
         valid = (position < image_tile_count[0] * (rows // TILES)).astype(f32)
         live = (jnp.arange(text_rows, dtype=jnp.int32) < text_token_length[0]).astype(f32)
+        valid = jnp.broadcast_to(valid[:, None], (rows, text_rows))
+        live = jnp.broadcast_to(live[None, :], (8, text_rows))
         kv_grad, back, stay, next_x, far_x, prior_x = layer(
             image,
             weight,
@@ -221,8 +214,8 @@
             up_both,
             queries[0, 0],
             cotangent[0, 0],
-            jnp.broadcast_to(valid[:, None], (rows, text_rows)),
-            jnp.broadcast_to(live[None, :], (8, text_rows)),
+            valid,
+            live,
         )
 
         image_grad = (
@@ -233,7 +226,7 @@
         )
 
         back = lax.all_gather(back, "mp", axis=0)
-        back = jnp.sum(back, axis=0).astype(bf16)
+        back = jnp.sum(back.astype(f32), axis=0).astype(bf16)
         adapter_grad = lax.dot_general(back, down, contracted_columns, preferred_element_type=f32)
         block = stay.shape[0]
         adapter_away = adapter_grad.astype(bf16)

time: 225 us -> 217 us (0.964)
  Pallas kernels: 20.1 us -> 12.9 us
    pallas_call x1, Pallas kernels: 20.1 us -> 12.9 us  [layer(): pl.pallas_call(layer_kernel, in_specs=[outside] * 4 + [inside_vmem] * 4,...]
  transfers between devices with their start and end apart: 23 -> 23, of which waited for: 8 -> 9; matrix products, arithmetic and copies ran while one was open for 4% -> 4% of each run, Pallas kernels for 0% -> 0%
where the time goes in v5:
time: 217 us; the launch traced here: 216 us
  starting transfers between devices  80.5 us (37%)
  blocking collectives  46.8 us (22%)
  waiting for transfers between devices  44.8 us (21%)
  between operations  15.9 us (7%)
  Pallas kernels  12.9 us (6%)
  local copies, waits for them, and re-layouts  6.31 us (3%)
  other arithmetic  6.07 us (3%)
  matrix products  2.38 us (1%)
    ppermute x21, starting transfers between devices, shift(): return lax.ppermute(v, AXES, pairs)  80.4 us
    ppermute x21, waiting for transfers between devices, shift(): return lax.ppermute(v, AXES, pairs)  40 us
    all_gather x1, blocking collectives, body(): low = lax.all_gather(low, 'mp', axis=0)  16.4 us
    all_gather x1, blocking collectives, body(): both = lax.all_gather(both, 'dp', axis=0, tiled=True)  15.3 us
    all_gather x1, blocking collectives, body(): back = lax.all_gather(back, 'mp', axis=0)  15.1 us
    pallas_call x1, Pallas kernels, layer(): pl.pallas_call(layer_kernel, in_specs=[outside] * 4 + [inside_vmem] * 4,...  12.9 us
    reduce_scatter x1, waiting for transfers between devices, body(): both = lax.psum_scatter(both, 'dp', scatter_dimension=0, tiled=True)  4.77 us
  transfers between devices with their start and end apart: 23, of which 9 were waited for; matrix products, arithmetic and copies ran while one was open for 4% of the time, Pallas kernels for 0%

profile of v5, /device:TPU:1, one launch (start us, length us, event | category | flops | bytes accessed | tf_op | source)
XLA Modules:
  0.0 215.7 jit_solution(14057156740228145823)
XLA Ops:
  7.2 2.5 %copy.11 = bf16[128,8,2,256]{3,1,2,0:T(8,128)(2,1)} copy(bf16[128,8,2,256]{3,2,1,0:T(2,128)(2,1)} %bitcast.35) | data formatting | bytes 2097152
  9.8 11.9 %collective-permute-start = (bf16[8,8192]{1,0:T(8,128)(2,1)S(1)}, bf16[8,8192]{1,0:T(8,128)(2,1)S(1)}, u32[]{:S(2)}, u32[]{:S(2)}) collective-permute-start(bf16[8,8192]{1,0:T(8,128)(2,1)S(1)} %bitcast.39), channel_id=1, source_target_pairs={{0,387},{1,384},{2,385},{3,386},{4,391},{5,388},{6,389},{7,390},{8... | collective-permute-start | bytes 393224 | tf_op jit(solution)/shard_map/ppermute | solution.py:146
  21.8 3.1 %collective-permute-start.1 = (bf16[8,8192]{1,0:T(8,128)(2,1)S(1)}, bf16[8,8192]{1,0:T(8,128)(2,1)S(1)}, u32[]{:S(2)}, u32[]{:S(2)}) collective-permute-start(bf16[8,8192]{1,0:T(8,128)(2,1)S(1)} %bitcast.40), channel_id=1, source_target_pairs={{0,256},{1,257},{2,258},{3,259},{4,263},{5,260},{6,261},{7,262},{8... | collective-permute-start | bytes 393224 | tf_op jit(solution)/shard_map/ppermute | solution.py:146
  24.9 2.6 %collective-permute-start.2 = (bf16[8,8192]{1,0:T(8,128)(2,1)S(1)}, bf16[8,8192]{1,0:T(8,128)(2,1)S(1)}, u32[]{:S(2)}, u32[]{:S(2)}) collective-permute-start(bf16[8,8192]{1,0:T(8,128)(2,1)S(1)} %bitcast.41), channel_id=1, source_target_pairs={{0,128},{1,129},{2,130},{3,131},{4,132},{5,133},{6,134},{7,135},{8... | collective-permute-start | bytes 393224 | tf_op jit(solution)/shard_map/ppermute | solution.py:146
  27.5 4.4 %collective-permute-start.3 = (bf16[8,8192]{1,0:T(8,128)(2,1)S(1)}, bf16[8,8192]{1,0:T(8,128)(2,1)S(1)}, u32[]{:S(2)}, u32[]{:S(2)}) collective-permute-start(bf16[8,8192]{1,0:T(8,128)(2,1)S(1)} %bitcast.42), channel_id=1, source_target_pairs={{0,96},{1,97},{2,98},{3,99},{4,100},{5,101},{6,102},{7,103},{8,104... | collective-permute-start | bytes 393224 | tf_op jit(solution)/shard_map/ppermute | solution.py:146
  31.9 2.4 %collective-permute-start.5 = (bf16[8,8192]{1,0:T(8,128)(2,1)S(1)}, bf16[8,8192]{1,0:T(8,128)(2,1)S(1)}, u32[]{:S(2)}, u32[]{:S(2)}) collective-permute-start(bf16[8,8192]{1,0:T(8,128)(2,1)S(1)} %bitcast.43), channel_id=1, source_target_pairs={{0,64},{1,65},{2,66},{3,67},{4,68},{5,69},{6,70},{7,71},{8,72},{9,... | collective-permute-start | bytes 393224 | tf_op jit(solution)/shard_map/ppermute | solution.py:146
  36.4 2.5 %collective-permute-start.7 = (bf16[8,8192]{1,0:T(8,128)(2,1)S(1)}, bf16[8,8192]{1,0:T(8,128)(2,1)S(1)}, u32[]{:S(2)}, u32[]{:S(2)}) collective-permute-start(bf16[8,8192]{1,0:T(8,128)(2,1)S(1)} %bitcast.44), channel_id=1, source_target_pairs={{0,32},{1,33},{2,34},{3,35},{4,36},{5,37},{6,38},{7,39},{8,40},{9,... | collective-permute-start | bytes 393224 | tf_op jit(solution)/shard_map/ppermute | solution.py:146
  39.0 4.0 %collective-permute-start.4 = (bf16[24,8192]{1,0:T(8,128)(2,1)S(1)}, bf16[24,8192]{1,0:T(8,128)(2,1)S(1)}, u32[]{:S(2)}, u32[]{:S(2)}) collective-permute-start(bf16[24,8192]{1,0:T(8,128)(2,1)S(1)} %get-tuple-element.21), channel_id=1, source_target_pairs={{0,96},{1,97},{2,98},{3,99},{4,100},{5,101},{6,102},{7,103},{8,104... | collective-permute-start | bytes 1179656 | tf_op jit(solution)/shard_map/ppermute | solution.py:146
  43.0 3.1 %collective-permute-start.6 = (bf16[24,8192]{1,0:T(8,128)(2,1)S(1)}, bf16[24,8192]{1,0:T(8,128)(2,1)S(1)}, u32[]{:S(2)}, u32[]{:S(2)}) collective-permute-start(bf16[24,8192]{1,0:T(8,128)(2,1)S(1)} %get-tuple-element.21), channel_id=1, source_target_pairs={{0,64},{1,65},{2,66},{3,67},{4,68},{5,69},{6,70},{7,71},{8,72},{9,... | collective-permute-start | bytes 1179656 | tf_op jit(solution)/shard_map/ppermute | solution.py:146
  46.2 1.9 collective-permute-start.8
  48.2 11.7 %collective-permute-done.4 = bf16[24,8192]{1,0:T(8,128)(2,1)S(1)} collective-permute-done((bf16[24,8192]{1,0:T(8,128)(2,1)S(1)}, bf16[24,8192]{1,0:T(8,128)(2,1)S(1)}, u32[]{:S(2)}, u32[]{:S(2)}) %collective-permute-start.4) | collective-permute-done | bytes 393248 | tf_op jit(solution)/shard_map/ppermute | solution.py:146
  60.0 6.0 %collective-permute-done.8 = bf16[24,8192]{1,0:T(8,128)(2,1)S(1)} collective-permute-done((bf16[24,8192]{1,0:T(8,128)(2,1)S(1)}, bf16[24,8192]{1,0:T(8,128)(2,1)S(1)}, u32[]{:S(2)}, u32[]{:S(2)}) %collective-permute-start.8) | collective-permute-done | bytes 393248 | tf_op jit(solution)/shard_map/ppermute | solution.py:146
  66.4 16.4 %all-gather = f32[512,128]{1,0:T(8,128)S(1)} all-gather(f32[128,128]{1,0:T(8,128)S(1)} %fusion.2), channel_id=2, replica_groups=mesh['segment'=16,'dp'=8,'mp'=4] {'mp'}, dimensions={0}, use_global_device_ids=true | all-gather | bytes 327680 | tf_op jit(solution)/shard_map/all_gather | solution.py:199
  84.7 12.9 %layer.1 = (bf16[128,512]{1,0:T(8,128)(2,1)}, bf16[128,128]{1,0:T(8,128)(2,1)}, f32[32,8192]{1,0:T(8,128)}, bf16[32,8192]{1,0:T(8,128)(2,1)}, bf16[32,8192]{1,0:T(8,128)(2,1)}, /*index=5*/bf16[32,8192]{1,0:T(8,128)(2,1)}) custom-call(bf16[128,8192]{1,0:T(8,128)(2,1)} %copy-done.1, bf16[8192,512]{1,0:T(8,128)(2,1)} %all-gather.4.cloned.1.call-done.weight_hbm, ...), custom_call_target="tpu_custom_call" | custom-call | tf_op jit(solution)/shard_map/layer/pallas_call | solution.py:110
  97.6 2.5 %collective-permute-start.10 = (bf16[32,8192]{1,0:T(8,128)(2,1)}, bf16[32,8192]{1,0:T(8,128)(2,1)S(1)}, u32[]{:S(2)}, u32[]{:S(2)}) collective-permute-start(bf16[32,8192]{1,0:T(8,128)(2,1)} %get-tuple-element.13), channel_id=1, source_target_pairs={{0,64},{1,65},{2,66},{3,67},{4,68},{5,69},{6,70},{7,71},{8,72},{9,... | collective-permute-start | bytes 1572872 | tf_op jit(solution)/shard_map/ppermute | solution.py:146
  100.2 2.7 %collective-permute-start.11 = (bf16[32,8192]{1,0:T(8,128)(2,1)}, bf16[32,8192]{1,0:T(8,128)(2,1)}, u32[]{:S(2)}, u32[]{:S(2)}) collective-permute-start(bf16[32,8192]{1,0:T(8,128)(2,1)} %get-tuple-element.14), channel_id=1, source_target_pairs={{0,96},{1,97},{2,98},{3,99},{4,100},{5,101},{6,102},{7,103},{8,104... | collective-permute-start | bytes 1572872 | tf_op jit(solution)/shard_map/ppermute | solution.py:146
  102.9 2.6 %collective-permute-start.9 = (bf16[32,8192]{1,0:T(8,128)(2,1)}, bf16[32,8192]{1,0:T(8,128)(2,1)}, u32[]{:S(2)}, u32[]{:S(2)}) collective-permute-start(bf16[32,8192]{1,0:T(8,128)(2,1)} %get-tuple-element.12), channel_id=1, source_target_pairs={{0,32},{1,33},{2,34},{3,35},{4,36},{5,37},{6,38},{7,39},{8,40},{9,... | collective-permute-start | bytes 1572872 | tf_op jit(solution)/shard_map/ppermute | solution.py:146
  105.5 15.1 %all-gather.1 = bf16[512,128]{1,0:T(8,128)(2,1)S(1)} all-gather(bf16[128,128]{1,0:T(8,128)(2,1)} %get-tuple-element.9), channel_id=3, replica_groups=mesh['segment'=16,'dp'=8,'mp'=4] {'mp'}, dimensions={0}, use_global_device_ids=true | all-gather | bytes 163840 | tf_op jit(solution)/shard_map/all_gather | solution.py:228
  121.6 2.6 %collective-permute-start.12 = (bf16[32,2048]{1,0:T(8,128)(2,1)}, bf16[32,2048]{1,0:T(8,128)(2,1)S(1)}, u32[]{:S(2)}, u32[]{:S(2)}) collective-permute-start(bf16[32,2048]{1,0:T(8,128)(2,1)} %get-tuple-element.18), channel_id=1, source_target_pairs={{0,32},{1,33},{2,34},{3,35},{4,36},{5,37},{6,38},{7,39},{8,40},{9,... | collective-permute-start | bytes 393224 | tf_op jit(solution)/shard_map/ppermute | solution.py:146
  124.2 4.3 %collective-permute-start.13 = (bf16[32,2048]{1,0:T(8,128)(2,1)}, bf16[32,2048]{1,0:T(8,128)(2,1)S(1)}, u32[]{:S(2)}, u32[]{:S(2)}) collective-permute-start(bf16[32,2048]{1,0:T(8,128)(2,1)} %get-tuple-element.20), channel_id=1, source_target_pairs={{0,64},{1,65},{2,66},{3,67},{4,68},{5,69},{6,70},{7,71},{8,72},{9,... | collective-permute-start | bytes 393224 | tf_op jit(solution)/shard_map/ppermute | solution.py:146
  130.4 3.3 %collective-permute-start.14 = (bf16[32,2048]{1,0:T(8,128)(2,1)}, bf16[32,2048]{1,0:T(8,128)(2,1)S(1)}, u32[]{:S(2)}, u32[]{:S(2)}) collective-permute-start(bf16[32,2048]{1,0:T(8,128)(2,1)} %get-tuple-element.19), channel_id=1, source_target_pairs={{0,96},{1,97},{2,98},{3,99},{4,100},{5,101},{6,102},{7,103},{8,104... | collective-permute-start | bytes 393224 | tf_op jit(solution)/shard_map/ppermute | solution.py:146
  136.5 2.5 %collective-permute-start.15 = (bf16[8,8192]{1,0:T(8,128)(2,1)S(1)}, bf16[8,8192]{1,0:T(8,128)(2,1)S(1)}, u32[]{:S(2)}, u32[]{:S(2)}) collective-permute-start(bf16[8,8192]{1,0:T(8,128)(2,1)S(1)} %get-tuple-element.15), channel_id=1, source_target_pairs={{0,128},{1,129},{2,130},{3,131},{4,132},{5,133},{6,134},{7,135},{8... | collective-permute-start | bytes 393224 | tf_op jit(solution)/shard_map/ppermute | solution.py:146
  139.0 5.8 %collective-permute-start.16 = (bf16[8,8192]{1,0:T(8,128)(2,1)S(1)}, bf16[8,8192]{1,0:T(8,128)(2,1)S(1)}, u32[]{:S(2)}, u32[]{:S(2)}) collective-permute-start(bf16[8,8192]{1,0:T(8,128)(2,1)S(1)} %get-tuple-element.17), channel_id=1, source_target_pairs={{0,256},{1,257},{2,258},{3,259},{4,263},{5,260},{6,261},{7,262},{8... | collective-permute-start | bytes 393224 | tf_op jit(solution)/shard_map/ppermute | solution.py:146
  144.8 1.9 collective-permute-start.17
  148.4 2.1 collective-permute-done.17
  150.6 7.0 %collective-permute-start.18 = (bf16[8,8192]{1,0:T(8,128)(2,1)S(1)}, bf16[8,8192]{1,0:T(8,128)(2,1)S(1)}, u32[]{:S(2)}, u32[]{:S(2)}) collective-permute-start(bf16[8,8192]{1,0:T(8,128)(2,1)S(1)} %fusion.9), channel_id=1, source_target_pairs={{0,2},{1,3},{2,0},{3,1},{4,6},{5,7},{6,4},{7,5},{8,10},{9,11},{10,... | collective-permute-start | bytes 393224 | tf_op jit(solution)/shard_map/ppermute | solution.py:146
  157.6 5.3 %collective-permute-start.19 = (bf16[8,8192]{1,0:T(8,128)(2,1)S(1)}, bf16[8,8192]{1,0:T(8,128)(2,1)S(1)}, u32[]{:S(2)}, u32[]{:S(2)}) collective-permute-start(bf16[8,8192]{1,0:T(8,128)(2,1)S(1)} %fusion.9), channel_id=1, source_target_pairs={{0,1},{1,2},{2,3},{3,0},{4,5},{5,6},{6,7},{7,4},{8,9},{9,10},{10,1... | collective-permute-start | bytes 393224 | tf_op jit(solution)/shard_map/ppermute | solution.py:146
  162.9 3.9 %collective-permute-start.20 = (bf16[8,8192]{1,0:T(8,128)(2,1)S(1)}, bf16[8,8192]{1,0:T(8,128)(2,1)S(1)}, u32[]{:S(2)}, u32[]{:S(2)}) collective-permute-start(bf16[8,8192]{1,0:T(8,128)(2,1)S(1)} %fusion.9), channel_id=1, source_target_pairs={{0,3},{1,0},{2,1},{3,2},{4,7},{5,4},{6,5},{7,6},{8,11},{9,8},{10,9... | collective-permute-start | bytes 393224 | tf_op jit(solution)/shard_map/ppermute | solution.py:146
  166.9 2.2 %collective-permute-done.19 = bf16[8,8192]{1,0:T(8,128)(2,1)S(1)} collective-permute-done((bf16[8,8192]{1,0:T(8,128)(2,1)S(1)}, bf16[8,8192]{1,0:T(8,128)(2,1)S(1)}, u32[]{:S(2)}, u32[]{:S(2)}) %collective-permute-start.19) | collective-permute-done | bytes 131104 | tf_op jit(solution)/shard_map/ppermute | solution.py:146
  169.2 16.4 %collective-permute-done.20 = bf16[8,8192]{1,0:T(8,128)(2,1)S(1)} collective-permute-done((bf16[8,8192]{1,0:T(8,128)(2,1)S(1)}, bf16[8,8192]{1,0:T(8,128)(2,1)S(1)}, u32[]{:S(2)}, u32[]{:S(2)}) %collective-permute-start.20) | collective-permute-done | bytes 131104 | tf_op jit(solution)/shard_map/ppermute | solution.py:146
  186.4 4.8 %reduce-scatter.2.cloned.1.call-done = f32[288,128]{1,0:T(8,128)} async-done(((f32[2304,128]{1,0:T(8,128)}), f32[288,128]{1,0:T(8,128)}) %reduce-scatter.2.cloned.1.call-update) | async-done | bytes 147472 | tf_op jit(solution)/shard_map/reduce_scatter | solution.py:250
  192.0 15.3 %all_gather.23 = bf16[2304,128]{1,0:T(8,128)(2,1)S(1)} all-gather(bf16[288,128]{1,0:T(8,128)(2,1)S(1)} %convert_element_type.71), channel_id=1, replica_groups=mesh['segment'=16,'dp'=8,'mp'=4] {'dp'}, dimensions={0}, use_global_device_ids=true | all-gather | bytes 663552 | tf_op jit(solution)/shard_map/all_gather | solution.py:261
  (70 shorter events, 13.9 us)
Async XLA Ops:
  7.2 58.9 %copy-start = (bf16[1,2048,128]{2,1,0:T(8,128)(2,1)S(1)}, bf16[1,2048,128]{2,1,0:T(8,128)(2,1)}, u32[]{:S(2)}) copy-start(bf16[1,2048,128]{2,1,0:T(8,128)(2,1)} %param.10) | copy-start | bytes 1572868
  7.2 2.6 %copy-start.3 = (bf16[1,8,8192]{2,1,0:T(8,128)(2,1)S(1)}, bf16[1,8,8192]{2,1,0:T(8,128)(2,1)}, u32[]{:S(2)}) copy-start(bf16[1,8,8192]{2,1,0:T(8,128)(2,1)} %param.8) | copy-start | bytes 393220
  7.2 28.5 %copy-start.5 = (bf16[1,2,64,256]{3,2,1,0:T(8,128)(2,1)S(1)}, bf16[1,2,64,256]{3,2,1,0:T(8,128)(2,1)}, u32[]{:S(2)}) copy-start(bf16[1,2,64,256]{3,2,1,0:T(8,128)(2,1)} %param.11) | copy-start | bytes 196612
  7.2 76.2 %all-gather.4.cloned.1.call-start = ((), (), s32[]{:S(2)}) async-start(), calls=%async_computation.1 | async-start | bytes 9437184 | tf_op jit(solution)/shard_map/all_gather | solution.py:196
  9.8 181.3 %reduce-scatter.2.cloned.1.call-start = ((), (), s32[]{:S(2)}) async-start(), calls=%async_computation.2 | async-start | bytes 1327104 | tf_op jit(solution)/shard_map/reduce_scatter | solution.py:250
  9.8 26.6 %collective-permute-start = (bf16[8,8192]{1,0:T(8,128)(2,1)S(1)}, bf16[8,8192]{1,0:T(8,128)(2,1)S(1)}, u32[]{:S(2)}, u32[]{:S(2)}) collective-permute-start(bf16[8,8192]{1,0:T(8,128)(2,1)S(1)} %bitcast.39), channel_id=1, source_target_pairs={{0,387},{1,384},{2,385},{3,386},{4,391},{5,388},{6,389},{7,390},{8... | collective-permute-start | bytes 393224 | tf_op jit(solution)/shard_map/ppermute | solution.py:146
  21.8 17.2 %collective-permute-start.1 = (bf16[8,8192]{1,0:T(8,128)(2,1)S(1)}, bf16[8,8192]{1,0:T(8,128)(2,1)S(1)}, u32[]{:S(2)}, u32[]{:S(2)}) collective-permute-start(bf16[8,8192]{1,0:T(8,128)(2,1)S(1)} %bitcast.40), channel_id=1, source_target_pairs={{0,256},{1,257},{2,258},{3,259},{4,263},{5,260},{6,261},{7,262},{8... | collective-permute-start | bytes 393224 | tf_op jit(solution)/shard_map/ppermute | solution.py:146
  24.9 14.1 %collective-permute-start.2 = (bf16[8,8192]{1,0:T(8,128)(2,1)S(1)}, bf16[8,8192]{1,0:T(8,128)(2,1)S(1)}, u32[]{:S(2)}, u32[]{:S(2)}) collective-permute-start(bf16[8,8192]{1,0:T(8,128)(2,1)S(1)} %bitcast.41), channel_id=1, source_target_pairs={{0,128},{1,129},{2,130},{3,131},{4,132},{5,133},{6,134},{7,135},{8... | collective-permute-start | bytes 393224 | tf_op jit(solution)/shard_map/ppermute | solution.py:146
  27.5 18.7 %collective-permute-start.3 = (bf16[8,8192]{1,0:T(8,128)(2,1)S(1)}, bf16[8,8192]{1,0:T(8,128)(2,1)S(1)}, u32[]{:S(2)}, u32[]{:S(2)}) collective-permute-start(bf16[8,8192]{1,0:T(8,128)(2,1)S(1)} %bitcast.42), channel_id=1, source_target_pairs={{0,96},{1,97},{2,98},{3,99},{4,100},{5,101},{6,102},{7,103},{8,104... | collective-permute-start | bytes 393224 | tf_op jit(solution)/shard_map/ppermute | solution.py:146
  31.9 28.0 %collective-permute-start.5 = (bf16[8,8192]{1,0:T(8,128)(2,1)S(1)}, bf16[8,8192]{1,0:T(8,128)(2,1)S(1)}, u32[]{:S(2)}, u32[]{:S(2)}) collective-permute-start(bf16[8,8192]{1,0:T(8,128)(2,1)S(1)} %bitcast.43), channel_id=1, source_target_pairs={{0,64},{1,65},{2,66},{3,67},{4,68},{5,69},{6,70},{7,71},{8,72},{9,... | collective-permute-start | bytes 393224 | tf_op jit(solution)/shard_map/ppermute | solution.py:146
  36.4 23.5 %collective-permute-start.7 = (bf16[8,8192]{1,0:T(8,128)(2,1)S(1)}, bf16[8,8192]{1,0:T(8,128)(2,1)S(1)}, u32[]{:S(2)}, u32[]{:S(2)}) collective-permute-start(bf16[8,8192]{1,0:T(8,128)(2,1)S(1)} %bitcast.44), channel_id=1, source_target_pairs={{0,32},{1,33},{2,34},{3,35},{4,36},{5,37},{6,38},{7,39},{8,40},{9,... | collective-permute-start | bytes 393224 | tf_op jit(solution)/shard_map/ppermute | solution.py:146
  39.0 20.8 %collective-permute-start.4 = (bf16[24,8192]{1,0:T(8,128)(2,1)S(1)}, bf16[24,8192]{1,0:T(8,128)(2,1)S(1)}, u32[]{:S(2)}, u32[]{:S(2)}) collective-permute-start(bf16[24,8192]{1,0:T(8,128)(2,1)S(1)} %get-tuple-element.21), channel_id=1, source_target_pairs={{0,96},{1,97},{2,98},{3,99},{4,100},{5,101},{6,102},{7,103},{8,104... | collective-permute-start | bytes 1179656 | tf_op jit(solution)/shard_map/ppermute | solution.py:146
  43.0 16.9 %collective-permute-start.6 = (bf16[24,8192]{1,0:T(8,128)(2,1)S(1)}, bf16[24,8192]{1,0:T(8,128)(2,1)S(1)}, u32[]{:S(2)}, u32[]{:S(2)}) collective-permute-start(bf16[24,8192]{1,0:T(8,128)(2,1)S(1)} %get-tuple-element.21), channel_id=1, source_target_pairs={{0,64},{1,65},{2,66},{3,67},{4,68},{5,69},{6,70},{7,71},{8,72},{9,... | collective-permute-start | bytes 1179656 | tf_op jit(solution)/shard_map/ppermute | solution.py:146
  46.2 19.8 %collective-permute-start.8 = (bf16[24,8192]{1,0:T(8,128)(2,1)S(1)}, bf16[24,8192]{1,0:T(8,128)(2,1)S(1)}, u32[]{:S(2)}, u32[]{:S(2)}) collective-permute-start(bf16[24,8192]{1,0:T(8,128)(2,1)S(1)} %get-tuple-element.21), channel_id=1, source_target_pairs={{0,32},{1,33},{2,34},{3,35},{4,36},{5,37},{6,38},{7,39},{8,40},{9,... | collective-permute-start | bytes 1179656 | tf_op jit(solution)/shard_map/ppermute | solution.py:146
  66.1 18.7 %copy-start.1 = (bf16[128,8192]{1,0:T(8,128)(2,1)}, bf16[128,8192]{1,0:T(8,128)(2,1)S(1)}, u32[]{:S(2)}) copy-start(bf16[128,8192]{1,0:T(8,128)(2,1)S(1)} %constant_dynamic-update-slice_fusion.3.image_hbm) | copy-start | bytes 6291460
  97.6 30.9 %copy-start.2 = (bf16[128,128]{1,0:T(8,128)(2,1)S(1)}, bf16[128,128]{1,0:T(8,128)(2,1)}, u32[]{:S(2)}) copy-start(bf16[128,128]{1,0:T(8,128)(2,1)} %reduce_sum.21.low_ref) | copy-start | bytes 98308
  97.6 30.9 %copy-start.4 = (bf16[128,512]{1,0:T(8,128)(2,1)S(1)}, bf16[128,512]{1,0:T(8,128)(2,1)}, u32[]{:S(2)}) copy-start(bf16[128,512]{1,0:T(8,128)(2,1)} %get-tuple-element.10) | copy-start | bytes 393220
  97.6 32.7 %collective-permute-start.10 = (bf16[32,8192]{1,0:T(8,128)(2,1)}, bf16[32,8192]{1,0:T(8,128)(2,1)S(1)}, u32[]{:S(2)}, u32[]{:S(2)}) collective-permute-start(bf16[32,8192]{1,0:T(8,128)(2,1)} %get-tuple-element.13), channel_id=1, source_target_pairs={{0,64},{1,65},{2,66},{3,67},{4,68},{5,69},{6,70},{7,71},{8,72},{9,... | collective-permute-start | bytes 1572872 | tf_op jit(solution)/shard_map/ppermute | solution.py:146
  100.2 33.5 %collective-permute-start.11 = (bf16[32,8192]{1,0:T(8,128)(2,1)}, bf16[32,8192]{1,0:T(8,128)(2,1)}, u32[]{:S(2)}, u32[]{:S(2)}) collective-permute-start(bf16[32,8192]{1,0:T(8,128)(2,1)} %get-tuple-element.14), channel_id=1, source_target_pairs={{0,96},{1,97},{2,98},{3,99},{4,100},{5,101},{6,102},{7,103},{8,104... | collective-permute-start | bytes 1572872 | tf_op jit(solution)/shard_map/ppermute | solution.py:146
  102.9 30.8 %collective-permute-start.9 = (bf16[32,8192]{1,0:T(8,128)(2,1)}, bf16[32,8192]{1,0:T(8,128)(2,1)}, u32[]{:S(2)}, u32[]{:S(2)}) collective-permute-start(bf16[32,8192]{1,0:T(8,128)(2,1)} %get-tuple-element.12), channel_id=1, source_target_pairs={{0,32},{1,33},{2,34},{3,35},{4,36},{5,37},{6,38},{7,39},{8,40},{9,... | collective-permute-start | bytes 1572872 | tf_op jit(solution)/shard_map/ppermute | solution.py:146
  121.6 13.8 %collective-permute-start.12 = (bf16[32,2048]{1,0:T(8,128)(2,1)}, bf16[32,2048]{1,0:T(8,128)(2,1)S(1)}, u32[]{:S(2)}, u32[]{:S(2)}) collective-permute-start(bf16[32,2048]{1,0:T(8,128)(2,1)} %get-tuple-element.18), channel_id=1, source_target_pairs={{0,32},{1,33},{2,34},{3,35},{4,36},{5,37},{6,38},{7,39},{8,40},{9,... | collective-permute-start | bytes 393224 | tf_op jit(solution)/shard_map/ppermute | solution.py:146
  124.2 11.2 %collective-permute-start.13 = (bf16[32,2048]{1,0:T(8,128)(2,1)}, bf16[32,2048]{1,0:T(8,128)(2,1)S(1)}, u32[]{:S(2)}, u32[]{:S(2)}) collective-permute-start(bf16[32,2048]{1,0:T(8,128)(2,1)} %get-tuple-element.20), channel_id=1, source_target_pairs={{0,64},{1,65},{2,66},{3,67},{4,68},{5,69},{6,70},{7,71},{8,72},{9,... | collective-permute-start | bytes 393224 | tf_op jit(solution)/shard_map/ppermute | solution.py:146
  130.4 5.9 %collective-permute-start.14 = (bf16[32,2048]{1,0:T(8,128)(2,1)}, bf16[32,2048]{1,0:T(8,128)(2,1)S(1)}, u32[]{:S(2)}, u32[]{:S(2)}) collective-permute-start(bf16[32,2048]{1,0:T(8,128)(2,1)} %get-tuple-element.19), channel_id=1, source_target_pairs={{0,96},{1,97},{2,98},{3,99},{4,100},{5,101},{6,102},{7,103},{8,104... | collective-permute-start | bytes 393224 | tf_op jit(solution)/shard_map/ppermute | solution.py:146
  136.5 11.4 %collective-permute-start.15 = (bf16[8,8192]{1,0:T(8,128)(2,1)S(1)}, bf16[8,8192]{1,0:T(8,128)(2,1)S(1)}, u32[]{:S(2)}, u32[]{:S(2)}) collective-permute-start(bf16[8,8192]{1,0:T(8,128)(2,1)S(1)} %get-tuple-element.15), channel_id=1, source_target_pairs={{0,128},{1,129},{2,130},{3,131},{4,132},{5,133},{6,134},{7,135},{8... | collective-permute-start | bytes 393224 | tf_op jit(solution)/shard_map/ppermute | solution.py:146
  139.0 9.4 %collective-permute-start.16 = (bf16[8,8192]{1,0:T(8,128)(2,1)S(1)}, bf16[8,8192]{1,0:T(8,128)(2,1)S(1)}, u32[]{:S(2)}, u32[]{:S(2)}) collective-permute-start(bf16[8,8192]{1,0:T(8,128)(2,1)S(1)} %get-tuple-element.17), channel_id=1, source_target_pairs={{0,256},{1,257},{2,258},{3,259},{4,263},{5,260},{6,261},{7,262},{8... | collective-permute-start | bytes 393224 | tf_op jit(solution)/shard_map/ppermute | solution.py:146
  144.8 5.7 %collective-permute-start.17 = (bf16[8,8192]{1,0:T(8,128)(2,1)S(1)}, bf16[8,8192]{1,0:T(8,128)(2,1)S(1)}, u32[]{:S(2)}, u32[]{:S(2)}) collective-permute-start(bf16[8,8192]{1,0:T(8,128)(2,1)S(1)} %get-tuple-element.16), channel_id=1, source_target_pairs={{0,387},{1,384},{2,385},{3,386},{4,391},{5,388},{6,389},{7,390},{8... | collective-permute-start | bytes 393224 | tf_op jit(solution)/shard_map/ppermute | solution.py:146
  150.6 16.3 %collective-permute-start.18 = (bf16[8,8192]{1,0:T(8,128)(2,1)S(1)}, bf16[8,8192]{1,0:T(8,128)(2,1)S(1)}, u32[]{:S(2)}, u32[]{:S(2)}) collective-permute-start(bf16[8,8192]{1,0:T(8,128)(2,1)S(1)} %fusion.9), channel_id=1, source_target_pairs={{0,2},{1,3},{2,0},{3,1},{4,6},{5,7},{6,4},{7,5},{8,10},{9,11},{10,... | collective-permute-start | bytes 393224 | tf_op jit(solution)/shard_map/ppermute | solution.py:146
  157.6 11.6 %collective-permute-start.19 = (bf16[8,8192]{1,0:T(8,128)(2,1)S(1)}, bf16[8,8192]{1,0:T(8,128)(2,1)S(1)}, u32[]{:S(2)}, u32[]{:S(2)}) collective-permute-start(bf16[8,8192]{1,0:T(8,128)(2,1)S(1)} %fusion.9), channel_id=1, source_target_pairs={{0,1},{1,2},{2,3},{3,0},{4,5},{5,6},{6,7},{7,4},{8,9},{9,10},{10,1... | collective-permute-start | bytes 393224 | tf_op jit(solution)/shard_map/ppermute | solution.py:146
  162.9 22.7 %collective-permute-start.20 = (bf16[8,8192]{1,0:T(8,128)(2,1)S(1)}, bf16[8,8192]{1,0:T(8,128)(2,1)S(1)}, u32[]{:S(2)}, u32[]{:S(2)}) collective-permute-start(bf16[8,8192]{1,0:T(8,128)(2,1)S(1)} %fusion.9), channel_id=1, source_target_pairs={{0,3},{1,0},{2,1},{3,2},{4,7},{5,4},{6,5},{7,6},{8,11},{9,8},{10,9... | collective-permute-start | bytes 393224 | tf_op jit(solution)/shard_map/ppermute | solution.py:146
Sparse Core Ops, SparseCore 0:
  10.2 63.0 all-gather.3
  148.0 43.0 reduce-scatter.1

commit v6 on v5

--- a/solution.py
+++ b/solution.py
@@ -22,47 +22,48 @@
 CHUNKS = 8
 
 
-def layer_kernel(
-    image_hbm,
-    weight_hbm,
-    query_hbm,
-    cot_hbm,
-    low_ref,
-    up_ref,
-    valid_ref,
-    live_ref,
-    kv_grad_ref,
-    back_ref,
-    own_ref,
-    *rest,
-):
-    *away_refs, image_ref, weight_ref, query_ref, cot_ref, sems = rest
+def layer_kernel(*refs):
+    pieces, refs = refs[: 2 * SIDE], refs[2 * SIDE :]
+    weight_hbm, query_hbm, cot_hbm, head_ref, low_ref, up_ref, valid_ref, live_ref, *refs = refs
+    kv_grad_ref, back_ref, own_ref, *rest = refs
+    *away_refs, quarter_ref, others_ref, weight_ref, query_ref, cot_ref, sems = rest
     columns = weight_ref.shape[1] // 2
     local_kv = columns // HD
     group = query_ref.shape[1] // HD // local_kv
     block = own_ref.shape[0]
     share = weight_ref.shape[0] // CHUNKS
 
+    first = quarter_ref.shape[1] // share
+
     def chunk(c):
         return pl.ds(c * share, share)
 
-    image_copy = pltpu.make_async_copy(image_hbm, image_ref, sems.at[CHUNKS])
-    query_copy = pltpu.make_async_copy(query_hbm, query_ref, sems.at[CHUNKS + 1])
-    cot_copy = pltpu.make_async_copy(cot_hbm, cot_ref, sems.at[CHUNKS + 2])
+    def turned(c):
+        return pl.ds(pl.multiple_of((head_ref[0] * first + c) % CHUNKS * share, share), share)
+
+    query_copy = pltpu.make_async_copy(query_hbm, query_ref, sems.at[CHUNKS])
+    cot_copy = pltpu.make_async_copy(cot_hbm, cot_ref, sems.at[CHUNKS + 1])
+    image_copies = []
+    for i, piece in enumerate(pieces):
+        target = (quarter_ref if i < SIDE else others_ref).at[pl.ds(i % SIDE * block, block)]
+        image_copies.append(pltpu.make_async_copy(piece, target, sems.at[CHUNKS + 2 + i]))
     weight_copies = [
-        pltpu.make_async_copy(weight_hbm.at[chunk(c)], weight_ref.at[chunk(c)], sems.at[c]) for c in range(CHUNKS)
+        pltpu.make_async_copy(weight_hbm.at[turned(c)], weight_ref.at[turned(c)], sems.at[c]) for c in range(CHUNKS)
     ]
-    image_copy.start()
+    for copy in image_copies:
+        copy.start()
     for copy in weight_copies:
         copy.start()
     query_copy.start()
     cot_copy.start()
 
     key_value = adapter_scale * jnp.dot(low_ref[...], up_ref[...], preferred_element_type=f32)
-    image_copy.wait()
+    for copy in image_copies:
+        copy.wait()
     for c, copy in enumerate(weight_copies):
         copy.wait()
-        key_value += jnp.dot(image_ref[:, chunk(c)], weight_ref[chunk(c), :], preferred_element_type=f32)
+        image = quarter_ref[:, chunk(c)] if c < first else others_ref[:, chunk(c - first)]
+        key_value += jnp.dot(image, weight_ref[turned(c), :], preferred_element_type=f32)
     key_value = key_value.astype(bf16)
     query_copy.wait()
     cot_copy.wait()
@@ -100,8 +101,8 @@
             ref[:, chunk(c)] = total[(i + 1) * block : (i + 2) * block].astype(bf16)
 
 
-def layer(image, weight, low, up, query, cot, valid, live):
-    rows, width = image.shape
+def layer(quarter, others, weight, head, low, up, query, cot, valid, live):
+    rows, width = SIDE * quarter[0].shape[0], weight.shape[0]
     columns = weight.shape[1]
     rank = low.shape[1]
     block = rows // SIDE
@@ -109,7 +110,7 @@
     inside_vmem = pl.BlockSpec(memory_space=pltpu.VMEM)
     return pl.pallas_call(
         layer_kernel,
-        in_specs=[outside] * 4 + [inside_vmem] * 4,
+        in_specs=[outside] * (2 * SIDE + 3) + [pl.BlockSpec(memory_space=pltpu.SMEM)] + [inside_vmem] * 4,
         out_specs=[inside_vmem] * (2 + SIDE),
         out_shape=[
             jax.ShapeDtypeStruct((rows, columns), bf16),
@@ -118,14 +119,15 @@
         ]
         + [jax.ShapeDtypeStruct((block, width), bf16)] * (SIDE - 1),
         scratch_shapes=[
-            pltpu.VMEM(image.shape, bf16),
+            pltpu.VMEM((rows, quarter[0].shape[1]), bf16),
+            pltpu.VMEM((rows, others[0].shape[1]), bf16),
             pltpu.VMEM(weight.shape, bf16),
             pltpu.VMEM(query.shape, bf16),
             pltpu.VMEM(cot.shape, bf16),
-            pltpu.SemaphoreType.DMA((CHUNKS + 3,)),
+            pltpu.SemaphoreType.DMA((CHUNKS + 2 + 2 * SIDE,)),
         ],
         name="layer",
-    )(image, weight, query, cot, low, up, valid, live)
+    )(*quarter, *others, weight, query, cot, head, low, up, valid, live)
 
 
 def make_body(mesh):
@@ -170,22 +172,18 @@
         down = adapter_down_weight[0]
         fourth = down.shape[0]
 
-        line = [shift(own, dz=-1), shift(own, dz=2, opposite=True), shift(own, dz=1)]
-        others = jnp.concatenate(line, axis=0)
-        image = jnp.concatenate(
-            [
-                own,
-                *line,
-                shift(own, dx=-1),
-                shift(others, dx=-1),
-                shift(own, dx=2, opposite=True),
-                shift(others, dx=2, opposite=True),
-                shift(own, dx=1),
-                shift(others, dx=1),
-            ],
-            axis=0,
-        )
-        rows = image.shape[0]
+        line = jnp.concatenate([own, shift(own, dz=-1), shift(own, dz=2, opposite=True), shift(own, dz=1)], axis=0)
+
+        def quarter_of(k):
+            return lax.dynamic_slice_in_dim(line, (parallel_index + k) % heads * fourth, fourth, 1)
+
+        def over_line(v):
+            return [v, shift(v, dx=-1), shift(v, dx=2, opposite=True), shift(v, dx=1)]
+
+        quarter = over_line(quarter_of(0))
+        image_fourth = jnp.concatenate(quarter, axis=0)
+        image_others = over_line(jnp.concatenate([quarter_of(k) for k in range(1, heads)], axis=1))
+        rows = image_fourth.shape[0]
         offset = jnp.arange(rows, dtype=jnp.int32)
         x_off, z_off, tok = offset // (runs * tokens), (offset // tokens) % runs, offset % tokens
         position = (
@@ -194,7 +192,6 @@
 
         local_weight = frozen_key_value[0].reshape(-1, CORES * columns)
         weight = lax.all_gather(local_weight, "dp", axis=0, tiled=True)
-        image_fourth = lax.dynamic_slice_in_dim(image, parallel_index * fourth, fourth, 1)
         low = jnp.dot(image_fourth, down, preferred_element_type=f32)
         low = lax.all_gather(low, "mp", axis=0)
         low = jnp.sum(low, axis=0).astype(bf16)
@@ -208,8 +205,10 @@
         valid = jnp.broadcast_to(valid[:, None], (rows, text_rows))
         live = jnp.broadcast_to(live[None, :], (8, text_rows))
         kv_grad, back, stay, next_x, far_x, prior_x = layer(
-            image,
+            quarter,
+            image_others,
             weight,
+            parallel_index.astype(jnp.int32)[None],
             low,
             up_both,
             queries[0, 0],

time: 217 us -> 208 us (0.959)
  waiting for transfers between devices: 44.8 us -> 29.1 us
  blocking collectives: 46.8 us -> 54.4 us
    ppermute x21, waiting for transfers between devices: 40 us -> 27.6 us  [shift(): return lax.ppermute(v, AXES, pairs)]
    all_gather x1, blocking collectives: 15.1 us -> 21.1 us  [body(): back = lax.all_gather(back, 'mp', axis=0)]
    reduce_scatter x1, waiting for transfers between devices: 4.77 us -> 0.01 us  [body(): both = lax.psum_scatter(both, 'dp', scatter_dimension=0, tiled=True)]
  transfers between devices with their start and end apart: 23 -> 23, of which waited for: 9 -> 8; matrix products, arithmetic and copies ran while one was open for 4% -> 3% of each run, Pallas kernels for 0% -> 0%
where the time goes in v6:
time: 208 us; the launch traced here: 207 us
  starting transfers between devices  79.6 us (38%)
  blocking collectives  54.4 us (26%)
  waiting for transfers between devices  29.1 us (14%)
  between operations  16 us (8%)
  Pallas kernels  13.1 us (6%)
  other arithmetic  7.02 us (3%)
  local copies, waits for them, and re-layouts  6.2 us (3%)
    ppermute x21, starting transfers between devices, shift(): return lax.ppermute(v, AXES, pairs)  79.5 us
    ppermute x21, waiting for transfers between devices, shift(): return lax.ppermute(v, AXES, pairs)  27.6 us
    all_gather x1, blocking collectives, body(): back = lax.all_gather(back, 'mp', axis=0)  21.1 us
    all_gather x1, blocking collectives, body(): low = lax.all_gather(low, 'mp', axis=0)  18 us
    all_gather x1, blocking collectives, body(): both = lax.all_gather(both, 'dp', axis=0, tiled=True)  15.4 us
    pallas_call x1, Pallas kernels, layer(): pl.pallas_call(layer_kernel, in_specs=[outside] * (2 * SIDE + 3) + [pl.Bl...  13.1 us
  transfers between devices with their start and end apart: 23, of which 8 were waited for; matrix products, arithmetic and copies ran while one was open for 3% of the time, Pallas kernels for 0%

profile of v6, /device:TPU:1, one launch (start us, length us, event | category | flops | bytes accessed | tf_op | source)
XLA Modules:
  0.0 206.7 jit_solution(2360056411094291798)
XLA Ops:
  7.2 2.5 %copy.11 = bf16[128,8,2,256]{3,1,2,0:T(8,128)(2,1)} copy(bf16[128,8,2,256]{3,2,1,0:T(2,128)(2,1)} %bitcast.35) | data formatting | bytes 2097152
  9.8 11.9 %collective-permute-start = (bf16[8,8192]{1,0:T(8,128)(2,1)S(1)}, bf16[8,8192]{1,0:T(8,128)(2,1)S(1)}, u32[]{:S(2)}, u32[]{:S(2)}) collective-permute-start(bf16[8,8192]{1,0:T(8,128)(2,1)S(1)} %bitcast.39), channel_id=1, source_target_pairs={{0,387},{1,384},{2,385},{3,386},{4,391},{5,388},{6,389},{7,390},{8... | collective-permute-start | bytes 393224 | tf_op jit(solution)/shard_map/ppermute | solution.py:148
  21.8 3.1 %collective-permute-start.1 = (bf16[8,8192]{1,0:T(8,128)(2,1)S(1)}, bf16[8,8192]{1,0:T(8,128)(2,1)S(1)}, u32[]{:S(2)}, u32[]{:S(2)}) collective-permute-start(bf16[8,8192]{1,0:T(8,128)(2,1)S(1)} %bitcast.40), channel_id=1, source_target_pairs={{0,256},{1,257},{2,258},{3,259},{4,263},{5,260},{6,261},{7,262},{8... | collective-permute-start | bytes 393224 | tf_op jit(solution)/shard_map/ppermute | solution.py:148
  24.9 2.6 %collective-permute-start.2 = (bf16[8,8192]{1,0:T(8,128)(2,1)S(1)}, bf16[8,8192]{1,0:T(8,128)(2,1)S(1)}, u32[]{:S(2)}, u32[]{:S(2)}) collective-permute-start(bf16[8,8192]{1,0:T(8,128)(2,1)S(1)} %bitcast.41), channel_id=1, source_target_pairs={{0,128},{1,129},{2,130},{3,131},{4,132},{5,133},{6,134},{7,135},{8... | collective-permute-start | bytes 393224 | tf_op jit(solution)/shard_map/ppermute | solution.py:148
  29.6 4.5 %collective-permute-done.2 = bf16[8,8192]{1,0:T(8,128)(2,1)S(1)} collective-permute-done((bf16[8,8192]{1,0:T(8,128)(2,1)S(1)}, bf16[8,8192]{1,0:T(8,128)(2,1)S(1)}, u32[]{:S(2)}, u32[]{:S(2)}) %collective-permute-start.2) | collective-permute-done | bytes 131104 | tf_op jit(solution)/shard_map/ppermute | solution.py:148
  34.2 4.4 %collective-permute-start.3 = (bf16[32,2048]{1,0:T(8,128)(2,1)S(1)}, bf16[32,2048]{1,0:T(8,128)(2,1)S(1)}, u32[]{:S(2)}, u32[]{:S(2)}) collective-permute-start(bf16[32,2048]{1,0:T(8,128)(2,1)S(1)} %get-tuple-element.24.refs_0_), channel_id=1, source_target_pairs={{0,96},{1,97},{2,98},{3,99},{4,100},{5,101},{6,102},{7,103},{8,104... | collective-permute-start | bytes 393224 | tf_op jit(solution)/shard_map/ppermute | solution.py:148
  38.6 2.4 %collective-permute-start.4 = (bf16[32,2048]{1,0:T(8,128)(2,1)S(1)}, bf16[32,2048]{1,0:T(8,128)(2,1)S(1)}, u32[]{:S(2)}, u32[]{:S(2)}) collective-permute-start(bf16[32,2048]{1,0:T(8,128)(2,1)S(1)} %get-tuple-element.24.refs_0_), channel_id=1, source_target_pairs={{0,64},{1,65},{2,66},{3,67},{4,68},{5,69},{6,70},{7,71},{8,72},{9,... | collective-permute-start | bytes 393224 | tf_op jit(solution)/shard_map/ppermute | solution.py:148
  41.1 2.5 %collective-permute-start.5 = (bf16[32,2048]{1,0:T(8,128)(2,1)S(1)}, bf16[32,2048]{1,0:T(8,128)(2,1)S(1)}, u32[]{:S(2)}, u32[]{:S(2)}) collective-permute-start(bf16[32,2048]{1,0:T(8,128)(2,1)S(1)} %get-tuple-element.24.refs_0_), channel_id=1, source_target_pairs={{0,32},{1,33},{2,34},{3,35},{4,36},{5,37},{6,38},{7,39},{8,40},{9,... | collective-permute-start | bytes 393224 | tf_op jit(solution)/shard_map/ppermute | solution.py:148
  43.6 4.0 %collective-permute-start.6 = (bf16[32,6144]{1,0:T(8,128)(2,1)S(1)}, bf16[32,6144]{1,0:T(8,128)(2,1)S(1)}, u32[]{:S(2)}, u32[]{:S(2)}) collective-permute-start(bf16[32,6144]{1,0:T(8,128)(2,1)S(1)} %pad_maximum_fusion.3.refs_4_), channel_id=1, source_target_pairs={{0,96},{1,97},{2,98},{3,99},{4,100},{5,101},{6,102},{7,103},{8,104... | collective-permute-start | bytes 1179656 | tf_op jit(solution)/shard_map/ppermute | solution.py:148
  47.6 3.1 %collective-permute-start.7 = (bf16[32,6144]{1,0:T(8,128)(2,1)S(1)}, bf16[32,6144]{1,0:T(8,128)(2,1)S(1)}, u32[]{:S(2)}, u32[]{:S(2)}) collective-permute-start(bf16[32,6144]{1,0:T(8,128)(2,1)S(1)} %pad_maximum_fusion.3.refs_4_), channel_id=1, source_target_pairs={{0,64},{1,65},{2,66},{3,67},{4,68},{5,69},{6,70},{7,71},{8,72},{9,... | collective-permute-start | bytes 1179656 | tf_op jit(solution)/shard_map/ppermute | solution.py:148
  50.8 1.9 collective-permute-start.8
  53.1 18.0 %all-gather = f32[512,128]{1,0:T(8,128)S(1)} all-gather(f32[128,128]{1,0:T(8,128)S(1)} %fusion.2), channel_id=2, replica_groups=mesh['segment'=16,'dp'=8,'mp'=4] {'mp'}, dimensions={0}, use_global_device_ids=true | all-gather | bytes 327680 | tf_op jit(solution)/shard_map/all_gather | solution.py:196
  74.5 13.1 %layer.1 = (bf16[128,512]{1,0:T(8,128)(2,1)}, bf16[128,128]{1,0:T(8,128)(2,1)}, f32[32,8192]{1,0:T(8,128)}, bf16[32,8192]{1,0:T(8,128)(2,1)}, bf16[32,8192]{1,0:T(8,128)(2,1)}, /*index=5*/bf16[32,8192]{1,0:T(8,128)(2,1)}) custom-call(bf16[32,2048]{1,0:T(8,128)(2,1)} %copy-done.2, bf16[32,2048]{1,0:T(8,128)(2,1)} %copy-done.8, bf16[32,2048]{1,0:T(8,128)(2,1)} %copy-done.10, ...), custom_call_target="tpu_custom_call" | custom-call | tf_op jit(solution)/shard_map/layer/pallas_call | solution.py:111
  87.6 4.6 %collective-permute-start.10 = (bf16[32,8192]{1,0:T(8,128)(2,1)}, bf16[32,8192]{1,0:T(8,128)(2,1)S(1)}, u32[]{:S(2)}, u32[]{:S(2)}) collective-permute-start(bf16[32,8192]{1,0:T(8,128)(2,1)} %get-tuple-element.13), channel_id=1, source_target_pairs={{0,64},{1,65},{2,66},{3,67},{4,68},{5,69},{6,70},{7,71},{8,72},{9,... | collective-permute-start | bytes 1572872 | tf_op jit(solution)/shard_map/ppermute | solution.py:148
  92.2 2.8 %collective-permute-start.11 = (bf16[32,8192]{1,0:T(8,128)(2,1)}, bf16[32,8192]{1,0:T(8,128)(2,1)}, u32[]{:S(2)}, u32[]{:S(2)}) collective-permute-start(bf16[32,8192]{1,0:T(8,128)(2,1)} %get-tuple-element.14), channel_id=1, source_target_pairs={{0,96},{1,97},{2,98},{3,99},{4,100},{5,101},{6,102},{7,103},{8,104... | collective-permute-start | bytes 1572872 | tf_op jit(solution)/shard_map/ppermute | solution.py:148
  95.0 2.5 %collective-permute-start.9 = (bf16[32,8192]{1,0:T(8,128)(2,1)}, bf16[32,8192]{1,0:T(8,128)(2,1)}, u32[]{:S(2)}, u32[]{:S(2)}) collective-permute-start(bf16[32,8192]{1,0:T(8,128)(2,1)} %get-tuple-element.12), channel_id=1, source_target_pairs={{0,32},{1,33},{2,34},{3,35},{4,36},{5,37},{6,38},{7,39},{8,40},{9,... | collective-permute-start | bytes 1572872 | tf_op jit(solution)/shard_map/ppermute | solution.py:148
  97.5 21.1 %all-gather.1 = bf16[512,128]{1,0:T(8,128)(2,1)S(1)} all-gather(bf16[128,128]{1,0:T(8,128)(2,1)} %get-tuple-element.9), channel_id=3, replica_groups=mesh['segment'=16,'dp'=8,'mp'=4] {'mp'}, dimensions={0}, use_global_device_ids=true | all-gather | bytes 163840 | tf_op jit(solution)/shard_map/all_gather | solution.py:227
  119.7 2.1 collective-permute-start.12
  121.8 5.0 %collective-permute-start.13 = (bf16[32,2048]{1,0:T(8,128)(2,1)}, bf16[32,2048]{1,0:T(8,128)(2,1)}, u32[]{:S(2)}, u32[]{:S(2)}) collective-permute-start(bf16[32,2048]{1,0:T(8,128)(2,1)} %get-tuple-element.20), channel_id=1, source_target_pairs={{0,64},{1,65},{2,66},{3,67},{4,68},{5,69},{6,70},{7,71},{8,72},{9,... | collective-permute-start | bytes 393224 | tf_op jit(solution)/shard_map/ppermute | solution.py:148
  127.7 1.9 collective-permute-start.14
  131.4 3.1 %collective-permute-done.14 = bf16[32,2048]{1,0:T(8,128)(2,1)S(1)} collective-permute-done((bf16[32,2048]{1,0:T(8,128)(2,1)}, bf16[32,2048]{1,0:T(8,128)(2,1)S(1)}, u32[]{:S(2)}, u32[]{:S(2)}) %collective-permute-start.14) | collective-permute-done | bytes 131104 | tf_op jit(solution)/shard_map/ppermute | solution.py:148
  135.6 2.0 collective-permute-start.15
  137.7 3.1 %collective-permute-start.16 = (bf16[8,8192]{1,0:T(8,128)(2,1)S(1)}, bf16[8,8192]{1,0:T(8,128)(2,1)S(1)}, u32[]{:S(2)}, u32[]{:S(2)}) collective-permute-start(bf16[8,8192]{1,0:T(8,128)(2,1)S(1)} %get-tuple-element.17), channel_id=1, source_target_pairs={{0,256},{1,257},{2,258},{3,259},{4,263},{5,260},{6,261},{7,262},{8... | collective-permute-start | bytes 393224 | tf_op jit(solution)/shard_map/ppermute | solution.py:148
  140.8 3.2 %collective-permute-start.17 = (bf16[8,8192]{1,0:T(8,128)(2,1)S(1)}, bf16[8,8192]{1,0:T(8,128)(2,1)S(1)}, u32[]{:S(2)}, u32[]{:S(2)}) collective-permute-start(bf16[8,8192]{1,0:T(8,128)(2,1)S(1)} %get-tuple-element.16), channel_id=1, source_target_pairs={{0,387},{1,384},{2,385},{3,386},{4,391},{5,388},{6,389},{7,390},{8... | collective-permute-start | bytes 393224 | tf_op jit(solution)/shard_map/ppermute | solution.py:148
  145.5 2.6 %collective-permute-done.17 = bf16[8,8192]{1,0:T(8,128)(2,1)S(1)} collective-permute-done((bf16[8,8192]{1,0:T(8,128)(2,1)S(1)}, bf16[8,8192]{1,0:T(8,128)(2,1)S(1)}, u32[]{:S(2)}, u32[]{:S(2)}) %collective-permute-start.17) | collective-permute-done | bytes 131104 | tf_op jit(solution)/shard_map/ppermute | solution.py:148
  148.2 7.0 %collective-permute-start.18 = (bf16[8,8192]{1,0:T(8,128)(2,1)S(1)}, bf16[8,8192]{1,0:T(8,128)(2,1)S(1)}, u32[]{:S(2)}, u32[]{:S(2)}) collective-permute-start(bf16[8,8192]{1,0:T(8,128)(2,1)S(1)} %fusion.6), channel_id=1, source_target_pairs={{0,2},{1,3},{2,0},{3,1},{4,6},{5,7},{6,4},{7,5},{8,10},{9,11},{10,... | collective-permute-start | bytes 393224 | tf_op jit(solution)/shard_map/ppermute | solution.py:148
  155.2 3.1 %collective-permute-start.19 = (bf16[8,8192]{1,0:T(8,128)(2,1)S(1)}, bf16[8,8192]{1,0:T(8,128)(2,1)S(1)}, u32[]{:S(2)}, u32[]{:S(2)}) collective-permute-start(bf16[8,8192]{1,0:T(8,128)(2,1)S(1)} %fusion.6), channel_id=1, source_target_pairs={{0,1},{1,2},{2,3},{3,0},{4,5},{5,6},{6,7},{7,4},{8,9},{9,10},{10,1... | collective-permute-start | bytes 393224 | tf_op jit(solution)/shard_map/ppermute | solution.py:148
  158.2 6.1 %collective-permute-start.20 = (bf16[8,8192]{1,0:T(8,128)(2,1)S(1)}, bf16[8,8192]{1,0:T(8,128)(2,1)S(1)}, u32[]{:S(2)}, u32[]{:S(2)}) collective-permute-start(bf16[8,8192]{1,0:T(8,128)(2,1)S(1)} %fusion.6), channel_id=1, source_target_pairs={{0,3},{1,0},{2,1},{3,2},{4,7},{5,4},{6,5},{7,6},{8,11},{9,8},{10,9... | collective-permute-start | bytes 393224 | tf_op jit(solution)/shard_map/ppermute | solution.py:148
  164.4 11.7 %collective-permute-done.18 = bf16[8,8192]{1,0:T(8,128)(2,1)S(1)} collective-permute-done((bf16[8,8192]{1,0:T(8,128)(2,1)S(1)}, bf16[8,8192]{1,0:T(8,128)(2,1)S(1)}, u32[]{:S(2)}, u32[]{:S(2)}) %collective-permute-start.18) | collective-permute-done | bytes 131104 | tf_op jit(solution)/shard_map/ppermute | solution.py:148
  176.0 2.6 %collective-permute-done.19 = bf16[8,8192]{1,0:T(8,128)(2,1)S(1)} collective-permute-done((bf16[8,8192]{1,0:T(8,128)(2,1)S(1)}, bf16[8,8192]{1,0:T(8,128)(2,1)S(1)}, u32[]{:S(2)}, u32[]{:S(2)}) %collective-permute-start.19) | collective-permute-done | bytes 131104 | tf_op jit(solution)/shard_map/ppermute | solution.py:148
  178.6 2.7 %collective-permute-done.20 = bf16[8,8192]{1,0:T(8,128)(2,1)S(1)} collective-permute-done((bf16[8,8192]{1,0:T(8,128)(2,1)S(1)}, bf16[8,8192]{1,0:T(8,128)(2,1)S(1)}, u32[]{:S(2)}, u32[]{:S(2)}) %collective-permute-start.20) | collective-permute-done | bytes 131104 | tf_op jit(solution)/shard_map/ppermute | solution.py:148
  183.0 15.4 %all_gather.23 = bf16[2304,128]{1,0:T(8,128)(2,1)S(1)} all-gather(bf16[288,128]{1,0:T(8,128)(2,1)S(1)} %convert_element_type.71), channel_id=1, replica_groups=mesh['segment'=16,'dp'=8,'mp'=4] {'dp'}, dimensions={0}, use_global_device_ids=true | all-gather | bytes 663552 | tf_op jit(solution)/shard_map/all_gather | solution.py:260
  (85 shorter events, 14.0 us)
Async XLA Ops:
  7.2 45.6 %copy-start = (bf16[1,2048,128]{2,1,0:T(8,128)(2,1)S(1)}, bf16[1,2048,128]{2,1,0:T(8,128)(2,1)}, u32[]{:S(2)}) copy-start(bf16[1,2048,128]{2,1,0:T(8,128)(2,1)} %param.10) | copy-start | bytes 1572868
  7.2 66.0 %all-gather.4.cloned.1.call-start = ((), (), s32[]{:S(2)}) async-start(), calls=%async_computation.1 | async-start | bytes 9437184 | tf_op jit(solution)/shard_map/all_gather | solution.py:194
  7.2 20.9 %copy-start.16 = (bf16[1,2,64,256]{3,2,1,0:T(8,128)(2,1)S(1)}, bf16[1,2,64,256]{3,2,1,0:T(8,128)(2,1)}, u32[]{:S(2)}) copy-start(bf16[1,2,64,256]{3,2,1,0:T(8,128)(2,1)} %param.11) | copy-start | bytes 196612
  9.8 172.3 %reduce-scatter.2.cloned.1.call-start = ((), (), s32[]{:S(2)}) async-start(), calls=%async_computation.2 | async-start | bytes 1327104 | tf_op jit(solution)/shard_map/reduce_scatter | solution.py:249
  9.8 19.8 %collective-permute-start = (bf16[8,8192]{1,0:T(8,128)(2,1)S(1)}, bf16[8,8192]{1,0:T(8,128)(2,1)S(1)}, u32[]{:S(2)}, u32[]{:S(2)}) collective-permute-start(bf16[8,8192]{1,0:T(8,128)(2,1)S(1)} %bitcast.39), channel_id=1, source_target_pairs={{0,387},{1,384},{2,385},{3,386},{4,391},{5,388},{6,389},{7,390},{8... | collective-permute-start | bytes 393224 | tf_op jit(solution)/shard_map/ppermute | solution.py:148
  21.8 7.8 %collective-permute-start.1 = (bf16[8,8192]{1,0:T(8,128)(2,1)S(1)}, bf16[8,8192]{1,0:T(8,128)(2,1)S(1)}, u32[]{:S(2)}, u32[]{:S(2)}) collective-permute-start(bf16[8,8192]{1,0:T(8,128)(2,1)S(1)} %bitcast.40), channel_id=1, source_target_pairs={{0,256},{1,257},{2,258},{3,259},{4,263},{5,260},{6,261},{7,262},{8... | collective-permute-start | bytes 393224 | tf_op jit(solution)/shard_map/ppermute | solution.py:148
  24.9 9.3 %collective-permute-start.2 = (bf16[8,8192]{1,0:T(8,128)(2,1)S(1)}, bf16[8,8192]{1,0:T(8,128)(2,1)S(1)}, u32[]{:S(2)}, u32[]{:S(2)}) collective-permute-start(bf16[8,8192]{1,0:T(8,128)(2,1)S(1)} %bitcast.41), channel_id=1, source_target_pairs={{0,128},{1,129},{2,130},{3,131},{4,132},{5,133},{6,134},{7,135},{8... | collective-permute-start | bytes 393224 | tf_op jit(solution)/shard_map/ppermute | solution.py:148
  34.2 18.9 %copy-start.2 = (bf16[32,2048]{1,0:T(8,128)(2,1)}, bf16[32,2048]{1,0:T(8,128)(2,1)S(1)}, u32[]{:S(2)}) copy-start(bf16[32,2048]{1,0:T(8,128)(2,1)S(1)} %get-tuple-element.24.refs_0_) | copy-start | bytes 393220
  34.2 16.5 %collective-permute-start.3 = (bf16[32,2048]{1,0:T(8,128)(2,1)S(1)}, bf16[32,2048]{1,0:T(8,128)(2,1)S(1)}, u32[]{:S(2)}, u32[]{:S(2)}) collective-permute-start(bf16[32,2048]{1,0:T(8,128)(2,1)S(1)} %get-tuple-element.24.refs_0_), channel_id=1, source_target_pairs={{0,96},{1,97},{2,98},{3,99},{4,100},{5,101},{6,102},{7,103},{8,104... | collective-permute-start | bytes 393224 | tf_op jit(solution)/shard_map/ppermute | solution.py:148
  38.6 14.1 %collective-permute-start.4 = (bf16[32,2048]{1,0:T(8,128)(2,1)S(1)}, bf16[32,2048]{1,0:T(8,128)(2,1)S(1)}, u32[]{:S(2)}, u32[]{:S(2)}) collective-permute-start(bf16[32,2048]{1,0:T(8,128)(2,1)S(1)} %get-tuple-element.24.refs_0_), channel_id=1, source_target_pairs={{0,64},{1,65},{2,66},{3,67},{4,68},{5,69},{6,70},{7,71},{8,72},{9,... | collective-permute-start | bytes 393224 | tf_op jit(solution)/shard_map/ppermute | solution.py:148
  41.1 11.7 %collective-permute-start.5 = (bf16[32,2048]{1,0:T(8,128)(2,1)S(1)}, bf16[32,2048]{1,0:T(8,128)(2,1)S(1)}, u32[]{:S(2)}, u32[]{:S(2)}) collective-permute-start(bf16[32,2048]{1,0:T(8,128)(2,1)S(1)} %get-tuple-element.24.refs_0_), channel_id=1, source_target_pairs={{0,32},{1,33},{2,34},{3,35},{4,36},{5,37},{6,38},{7,39},{8,40},{9,... | collective-permute-start | bytes 393224 | tf_op jit(solution)/shard_map/ppermute | solution.py:148
  43.6 27.5 %copy-start.1 = (bf16[32,6144]{1,0:T(8,128)(2,1)}, bf16[32,6144]{1,0:T(8,128)(2,1)S(1)}, u32[]{:S(2)}) copy-start(bf16[32,6144]{1,0:T(8,128)(2,1)S(1)} %pad_maximum_fusion.3.refs_4_) | copy-start | bytes 1179652
  43.6 28.1 %collective-permute-start.6 = (bf16[32,6144]{1,0:T(8,128)(2,1)S(1)}, bf16[32,6144]{1,0:T(8,128)(2,1)S(1)}, u32[]{:S(2)}, u32[]{:S(2)}) collective-permute-start(bf16[32,6144]{1,0:T(8,128)(2,1)S(1)} %pad_maximum_fusion.3.refs_4_), channel_id=1, source_target_pairs={{0,96},{1,97},{2,98},{3,99},{4,100},{5,101},{6,102},{7,103},{8,104... | collective-permute-start | bytes 1179656 | tf_op jit(solution)/shard_map/ppermute | solution.py:148
  47.6 24.1 %collective-permute-start.7 = (bf16[32,6144]{1,0:T(8,128)(2,1)S(1)}, bf16[32,6144]{1,0:T(8,128)(2,1)S(1)}, u32[]{:S(2)}, u32[]{:S(2)}) collective-permute-start(bf16[32,6144]{1,0:T(8,128)(2,1)S(1)} %pad_maximum_fusion.3.refs_4_), channel_id=1, source_target_pairs={{0,64},{1,65},{2,66},{3,67},{4,68},{5,69},{6,70},{7,71},{8,72},{9,... | collective-permute-start | bytes 1179656 | tf_op jit(solution)/shard_map/ppermute | solution.py:148
  50.8 20.3 %copy-start.8 = (bf16[32,2048]{1,0:T(8,128)(2,1)}, bf16[32,2048]{1,0:T(8,128)(2,1)S(1)}, u32[]{:S(2)}) copy-start(bf16[32,2048]{1,0:T(8,128)(2,1)S(1)} %collective-permute-done.3.refs_1_) | copy-start | bytes 393220
  50.8 20.9 %collective-permute-start.8 = (bf16[32,6144]{1,0:T(8,128)(2,1)S(1)}, bf16[32,6144]{1,0:T(8,128)(2,1)S(1)}, u32[]{:S(2)}, u32[]{:S(2)}) collective-permute-start(bf16[32,6144]{1,0:T(8,128)(2,1)S(1)} %pad_maximum_fusion.3.refs_4_), channel_id=1, source_target_pairs={{0,32},{1,33},{2,34},{3,35},{4,36},{5,37},{6,38},{7,39},{8,40},{9,... | collective-permute-start | bytes 1179656 | tf_op jit(solution)/shard_map/ppermute | solution.py:148
  52.8 18.3 %copy-start.10 = (bf16[32,2048]{1,0:T(8,128)(2,1)}, bf16[32,2048]{1,0:T(8,128)(2,1)S(1)}, u32[]{:S(2)}) copy-start(bf16[32,2048]{1,0:T(8,128)(2,1)S(1)} %collective-permute-done.4.refs_2_) | copy-start | bytes 393220
  52.8 18.3 %copy-start.12 = (bf16[32,2048]{1,0:T(8,128)(2,1)}, bf16[32,2048]{1,0:T(8,128)(2,1)S(1)}, u32[]{:S(2)}) copy-start(bf16[32,2048]{1,0:T(8,128)(2,1)S(1)} %collective-permute-done.5.refs_3_) | copy-start | bytes 393220
  87.6 40.1 %collective-permute-start.10 = (bf16[32,8192]{1,0:T(8,128)(2,1)}, bf16[32,8192]{1,0:T(8,128)(2,1)S(1)}, u32[]{:S(2)}, u32[]{:S(2)}) collective-permute-start(bf16[32,8192]{1,0:T(8,128)(2,1)} %get-tuple-element.13), channel_id=1, source_target_pairs={{0,64},{1,65},{2,66},{3,67},{4,68},{5,69},{6,70},{7,71},{8,72},{9,... | collective-permute-start | bytes 1572872 | tf_op jit(solution)/shard_map/ppermute | solution.py:148
  92.2 37.4 %collective-permute-start.11 = (bf16[32,8192]{1,0:T(8,128)(2,1)}, bf16[32,8192]{1,0:T(8,128)(2,1)}, u32[]{:S(2)}, u32[]{:S(2)}) collective-permute-start(bf16[32,8192]{1,0:T(8,128)(2,1)} %get-tuple-element.14), channel_id=1, source_target_pairs={{0,96},{1,97},{2,98},{3,99},{4,100},{5,101},{6,102},{7,103},{8,104... | collective-permute-start | bytes 1572872 | tf_op jit(solution)/shard_map/ppermute | solution.py:148
  95.0 34.6 %collective-permute-start.9 = (bf16[32,8192]{1,0:T(8,128)(2,1)}, bf16[32,8192]{1,0:T(8,128)(2,1)}, u32[]{:S(2)}, u32[]{:S(2)}) collective-permute-start(bf16[32,8192]{1,0:T(8,128)(2,1)} %get-tuple-element.12), channel_id=1, source_target_pairs={{0,32},{1,33},{2,34},{3,35},{4,36},{5,37},{6,38},{7,39},{8,40},{9,... | collective-permute-start | bytes 1572872 | tf_op jit(solution)/shard_map/ppermute | solution.py:148
  118.9 8.4 %copy-start.3 = (bf16[32,2048]{1,0:T(8,128)(2,1)S(1)}, bf16[32,2048]{1,0:T(8,128)(2,1)}, u32[]{:S(2)}) copy-start(bf16[32,2048]{1,0:T(8,128)(2,1)} %copy-done.2) | copy-start | bytes 393220
  119.0 8.4 %copy-start.9 = (bf16[32,2048]{1,0:T(8,128)(2,1)S(1)}, bf16[32,2048]{1,0:T(8,128)(2,1)}, u32[]{:S(2)}) copy-start(bf16[32,2048]{1,0:T(8,128)(2,1)} %copy-done.8) | copy-start | bytes 393220
  119.7 11.6 %collective-permute-start.12 = (bf16[32,2048]{1,0:T(8,128)(2,1)}, bf16[32,2048]{1,0:T(8,128)(2,1)S(1)}, u32[]{:S(2)}, u32[]{:S(2)}) collective-permute-start(bf16[32,2048]{1,0:T(8,128)(2,1)} %get-tuple-element.18), channel_id=1, source_target_pairs={{0,32},{1,33},{2,34},{3,35},{4,36},{5,37},{6,38},{7,39},{8,40},{9,... | collective-permute-start | bytes 393224 | tf_op jit(solution)/shard_map/ppermute | solution.py:148
  121.8 9.6 %collective-permute-start.13 = (bf16[32,2048]{1,0:T(8,128)(2,1)}, bf16[32,2048]{1,0:T(8,128)(2,1)}, u32[]{:S(2)}, u32[]{:S(2)}) collective-permute-start(bf16[32,2048]{1,0:T(8,128)(2,1)} %get-tuple-element.20), channel_id=1, source_target_pairs={{0,64},{1,65},{2,66},{3,67},{4,68},{5,69},{6,70},{7,71},{8,72},{9,... | collective-permute-start | bytes 393224 | tf_op jit(solution)/shard_map/ppermute | solution.py:148
  127.7 6.8 %collective-permute-start.14 = (bf16[32,2048]{1,0:T(8,128)(2,1)}, bf16[32,2048]{1,0:T(8,128)(2,1)S(1)}, u32[]{:S(2)}, u32[]{:S(2)}) collective-permute-start(bf16[32,2048]{1,0:T(8,128)(2,1)} %get-tuple-element.19), channel_id=1, source_target_pairs={{0,96},{1,97},{2,98},{3,99},{4,100},{5,101},{6,102},{7,103},{8,104... | collective-permute-start | bytes 393224 | tf_op jit(solution)/shard_map/ppermute | solution.py:148
  135.6 9.6 %collective-permute-start.15 = (bf16[8,8192]{1,0:T(8,128)(2,1)S(1)}, bf16[8,8192]{1,0:T(8,128)(2,1)S(1)}, u32[]{:S(2)}, u32[]{:S(2)}) collective-permute-start(bf16[8,8192]{1,0:T(8,128)(2,1)S(1)} %get-tuple-element.15), channel_id=1, source_target_pairs={{0,128},{1,129},{2,130},{3,131},{4,132},{5,133},{6,134},{7,135},{8... | collective-permute-start | bytes 393224 | tf_op jit(solution)/shard_map/ppermute | solution.py:148
  137.7 7.8 %collective-permute-start.16 = (bf16[8,8192]{1,0:T(8,128)(2,1)S(1)}, bf16[8,8192]{1,0:T(8,128)(2,1)S(1)}, u32[]{:S(2)}, u32[]{:S(2)}) collective-permute-start(bf16[8,8192]{1,0:T(8,128)(2,1)S(1)} %get-tuple-element.17), channel_id=1, source_target_pairs={{0,256},{1,257},{2,258},{3,259},{4,263},{5,260},{6,261},{7,262},{8... | collective-permute-start | bytes 393224 | tf_op jit(solution)/shard_map/ppermute | solution.py:148
  140.8 7.3 %collective-permute-start.17 = (bf16[8,8192]{1,0:T(8,128)(2,1)S(1)}, bf16[8,8192]{1,0:T(8,128)(2,1)S(1)}, u32[]{:S(2)}, u32[]{:S(2)}) collective-permute-start(bf16[8,8192]{1,0:T(8,128)(2,1)S(1)} %get-tuple-element.16), channel_id=1, source_target_pairs={{0,387},{1,384},{2,385},{3,386},{4,391},{5,388},{6,389},{7,390},{8... | collective-permute-start | bytes 393224 | tf_op jit(solution)/shard_map/ppermute | solution.py:148
  148.2 27.9 %collective-permute-start.18 = (bf16[8,8192]{1,0:T(8,128)(2,1)S(1)}, bf16[8,8192]{1,0:T(8,128)(2,1)S(1)}, u32[]{:S(2)}, u32[]{:S(2)}) collective-permute-start(bf16[8,8192]{1,0:T(8,128)(2,1)S(1)} %fusion.6), channel_id=1, source_target_pairs={{0,2},{1,3},{2,0},{3,1},{4,6},{5,7},{6,4},{7,5},{8,10},{9,11},{10,... | collective-permute-start | bytes 393224 | tf_op jit(solution)/shard_map/ppermute | solution.py:148
  155.2 23.5 %collective-permute-start.19 = (bf16[8,8192]{1,0:T(8,128)(2,1)S(1)}, bf16[8,8192]{1,0:T(8,128)(2,1)S(1)}, u32[]{:S(2)}, u32[]{:S(2)}) collective-permute-start(bf16[8,8192]{1,0:T(8,128)(2,1)S(1)} %fusion.6), channel_id=1, source_target_pairs={{0,1},{1,2},{2,3},{3,0},{4,5},{5,6},{6,7},{7,4},{8,9},{9,10},{10,1... | collective-permute-start | bytes 393224 | tf_op jit(solution)/shard_map/ppermute | solution.py:148
  158.2 23.1 %collective-permute-start.20 = (bf16[8,8192]{1,0:T(8,128)(2,1)S(1)}, bf16[8,8192]{1,0:T(8,128)(2,1)S(1)}, u32[]{:S(2)}, u32[]{:S(2)}) collective-permute-start(bf16[8,8192]{1,0:T(8,128)(2,1)S(1)} %fusion.6), channel_id=1, source_target_pairs={{0,3},{1,0},{2,1},{3,2},{4,7},{5,4},{6,5},{7,6},{8,11},{9,8},{10,9... | collective-permute-start | bytes 393224 | tf_op jit(solution)/shard_map/ppermute | solution.py:148
  (8 other events, 44.2 us)
Sparse Core Ops, SparseCore 0:
  10.1 63.0 all-gather.3
  145.3 36.6 reduce-scatter.1

commit v7 on v6

--- a/solution.py
+++ b/solution.py
@@ -25,8 +25,9 @@
 def layer_kernel(*refs):
     pieces, refs = refs[: 2 * SIDE], refs[2 * SIDE :]
     weight_hbm, query_hbm, cot_hbm, head_ref, low_ref, up_ref, valid_ref, live_ref, *refs = refs
-    kv_grad_ref, back_ref, own_ref, *rest = refs
-    *away_refs, quarter_ref, others_ref, weight_ref, query_ref, cot_ref, sems = rest
+    kv_grad_ref, back_ref, low_out_ref, *rest = refs
+    block_hbm, rest = rest[:SIDE], rest[SIDE:]
+    own_ref, *away_refs, quarter_ref, others_ref, weight_ref, query_ref, cot_ref, sems = rest
     columns = weight_ref.shape[1] // 2
     local_kv = columns // HD
     group = query_ref.shape[1] // HD // local_kv
@@ -57,7 +58,10 @@
     query_copy.start()
     cot_copy.start()
 
-    key_value = adapter_scale * jnp.dot(low_ref[...], up_ref[...], preferred_element_type=f32)
+    rows = low_out_ref.shape[0]
+    low = sum(low_ref[pl.ds(i * rows, rows), :] for i in range(low_ref.shape[0] // rows)).astype(bf16)
+    low_out_ref[...] = low
+    key_value = adapter_scale * jnp.dot(low, up_ref[...], preferred_element_type=f32)
     for copy in image_copies:
         copy.wait()
     for c, copy in enumerate(weight_copies):
@@ -94,11 +98,20 @@
     kv_grad = kv_grad_ref[...]
     back = adapter_scale * lax.dot_general(kv_grad, up_ref[...], contracted_columns, preferred_element_type=f32)
     back_ref[...] = back.astype(bf16)
+    out_copies = []
     for c in range(CHUNKS):
         total = lax.dot_general(kv_grad, weight_ref[chunk(c), :], contracted_columns, preferred_element_type=f32)
         own_ref[:, chunk(c)] = total[:block]
         for i, ref in enumerate(away_refs):
             ref[:, chunk(c)] = total[(i + 1) * block : (i + 2) * block].astype(bf16)
+        for i, (ref, target) in enumerate(zip((own_ref, *away_refs), block_hbm)):
+            copy = pltpu.make_async_copy(
+                ref.at[:, chunk(c)], target.at[:, chunk(c)], sems.at[CHUNKS + 2 + 2 * SIDE + c * SIDE + i]
+            )
+            copy.start()
+            out_copies.append(copy)
+    for copy in out_copies:
+        copy.wait()
 
 
 def layer(quarter, others, weight, head, low, up, query, cot, valid, live):
@@ -106,25 +119,27 @@
     columns = weight.shape[1]
     rank = low.shape[1]
     block = rows // SIDE
+    blocks = [(block, width, f32)] + [(block, width, bf16)] * (SIDE - 1)
     outside = pl.BlockSpec(memory_space=pl.ANY)
     inside_vmem = pl.BlockSpec(memory_space=pltpu.VMEM)
     return pl.pallas_call(
         layer_kernel,
         in_specs=[outside] * (2 * SIDE + 3) + [pl.BlockSpec(memory_space=pltpu.SMEM)] + [inside_vmem] * 4,
-        out_specs=[inside_vmem] * (2 + SIDE),
+        out_specs=[inside_vmem] * 3 + [outside] * SIDE,
         out_shape=[
             jax.ShapeDtypeStruct((rows, columns), bf16),
             jax.ShapeDtypeStruct((rows, rank), bf16),
-            jax.ShapeDtypeStruct((block, width), f32),
+            jax.ShapeDtypeStruct((rows, rank), bf16),
         ]
-        + [jax.ShapeDtypeStruct((block, width), bf16)] * (SIDE - 1),
-        scratch_shapes=[
+        + [jax.ShapeDtypeStruct(v[:2], v[2]) for v in blocks],
+        scratch_shapes=[pltpu.VMEM(v[:2], v[2]) for v in blocks]
+        + [
             pltpu.VMEM((rows, quarter[0].shape[1]), bf16),
             pltpu.VMEM((rows, others[0].shape[1]), bf16),
             pltpu.VMEM(weight.shape, bf16),
             pltpu.VMEM(query.shape, bf16),
             pltpu.VMEM(cot.shape, bf16),
-            pltpu.SemaphoreType.DMA((CHUNKS + 2 + 2 * SIDE,)),
+            pltpu.SemaphoreType.DMA((CHUNKS + 2 + 2 * SIDE + CHUNKS * SIDE,)),
         ],
         name="layer",
     )(*quarter, *others, weight, query, cot, head, low, up, valid, live)
@@ -193,8 +208,7 @@
         local_weight = frozen_key_value[0].reshape(-1, CORES * columns)
         weight = lax.all_gather(local_weight, "dp", axis=0, tiled=True)
         low = jnp.dot(image_fourth, down, preferred_element_type=f32)
-        low = lax.all_gather(low, "mp", axis=0)
-        low = jnp.sum(low, axis=0).astype(bf16)
+        low = lax.all_gather(low, "mp", axis=0, tiled=True)
         text_rows = queries.shape[2]
         none = jnp.zeros_like(up_key)
         up_both = jnp.concatenate(
@@ -204,7 +218,7 @@
         live = (jnp.arange(text_rows, dtype=jnp.int32) < text_token_length[0]).astype(f32)
         valid = jnp.broadcast_to(valid[:, None], (rows, text_rows))
         live = jnp.broadcast_to(live[None, :], (8, text_rows))
-        kv_grad, back, stay, next_x, far_x, prior_x = layer(
+        kv_grad, back, low, stay, next_x, far_x, prior_x = layer(
             quarter,
             image_others,
             weight,

time: 208 us -> 208 us (level)
  no operation moved by 1% of the time
where the time goes in v7:
time: 208 us; the launch traced here: 207 us
  starting transfers between devices  79.5 us (38%)
  blocking collectives  53.5 us (26%)
  waiting for transfers between devices  30.7 us (15%)
  between operations  16 us (8%)
  Pallas kernels  13.3 us (6%)
  other arithmetic  6.42 us (3%)
  local copies, waits for them, and re-layouts  6.21 us (3%)
    ppermute x21, starting transfers between devices, shift(): return lax.ppermute(v, AXES, pairs)  79.4 us
    ppermute x21, waiting for transfers between devices, shift(): return lax.ppermute(v, AXES, pairs)  29.1 us
    all_gather x1, blocking collectives, body(): back = lax.all_gather(back, 'mp', axis=0)  21.1 us
    all_gather x1, blocking collectives, body(): low = lax.all_gather(low, 'mp', axis=0, tiled=True)  18.5 us
    all_gather x1, blocking collectives, body(): both = lax.all_gather(both, 'dp', axis=0, tiled=True)  14 us
    pallas_call x1, Pallas kernels, layer(): pl.pallas_call(layer_kernel, in_specs=[outside] * (2 * SIDE + 3) + [pl.Bl...  13.3 us
  transfers between devices with their start and end apart: 23, of which 8 were waited for; matrix products, arithmetic and copies ran while one was open for 3% of the time, Pallas kernels for 0%

profile of v7, /device:TPU:1, one launch (start us, length us, event | category | flops | bytes accessed | tf_op | source)
XLA Modules:
  0.0 207.0 jit_solution(10660431848175264880)
XLA Ops:
  7.2 2.5 %copy.11 = bf16[128,8,2,256]{3,1,2,0:T(8,128)(2,1)} copy(bf16[128,8,2,256]{3,2,1,0:T(2,128)(2,1)} %bitcast.33) | data formatting | bytes 2097152
  9.8 11.9 %collective-permute-start = (bf16[8,8192]{1,0:T(8,128)(2,1)S(1)}, bf16[8,8192]{1,0:T(8,128)(2,1)S(1)}, u32[]{:S(2)}, u32[]{:S(2)}) collective-permute-start(bf16[8,8192]{1,0:T(8,128)(2,1)S(1)} %bitcast.37), channel_id=1, source_target_pairs={{0,387},{1,384},{2,385},{3,386},{4,391},{5,388},{6,389},{7,390},{8... | collective-permute-start | bytes 393224 | tf_op jit(solution)/shard_map/ppermute | solution.py:163
  21.8 3.1 %collective-permute-start.1 = (bf16[8,8192]{1,0:T(8,128)(2,1)S(1)}, bf16[8,8192]{1,0:T(8,128)(2,1)S(1)}, u32[]{:S(2)}, u32[]{:S(2)}) collective-permute-start(bf16[8,8192]{1,0:T(8,128)(2,1)S(1)} %bitcast.38), channel_id=1, source_target_pairs={{0,256},{1,257},{2,258},{3,259},{4,263},{5,260},{6,261},{7,262},{8... | collective-permute-start | bytes 393224 | tf_op jit(solution)/shard_map/ppermute | solution.py:163
  24.9 2.6 %collective-permute-start.2 = (bf16[8,8192]{1,0:T(8,128)(2,1)S(1)}, bf16[8,8192]{1,0:T(8,128)(2,1)S(1)}, u32[]{:S(2)}, u32[]{:S(2)}) collective-permute-start(bf16[8,8192]{1,0:T(8,128)(2,1)S(1)} %bitcast.39), channel_id=1, source_target_pairs={{0,128},{1,129},{2,130},{3,131},{4,132},{5,133},{6,134},{7,135},{8... | collective-permute-start | bytes 393224 | tf_op jit(solution)/shard_map/ppermute | solution.py:163
  29.6 4.5 %collective-permute-done.2 = bf16[8,8192]{1,0:T(8,128)(2,1)S(1)} collective-permute-done((bf16[8,8192]{1,0:T(8,128)(2,1)S(1)}, bf16[8,8192]{1,0:T(8,128)(2,1)S(1)}, u32[]{:S(2)}, u32[]{:S(2)}) %collective-permute-start.2) | collective-permute-done | bytes 131104 | tf_op jit(solution)/shard_map/ppermute | solution.py:163
  34.2 4.4 %collective-permute-start.3 = (bf16[32,2048]{1,0:T(8,128)(2,1)S(1)}, bf16[32,2048]{1,0:T(8,128)(2,1)S(1)}, u32[]{:S(2)}, u32[]{:S(2)}) collective-permute-start(bf16[32,2048]{1,0:T(8,128)(2,1)S(1)} %get-tuple-element.26.refs_0_), channel_id=1, source_target_pairs={{0,96},{1,97},{2,98},{3,99},{4,100},{5,101},{6,102},{7,103},{8,104... | collective-permute-start | bytes 393224 | tf_op jit(solution)/shard_map/ppermute | solution.py:163
  38.6 2.4 %collective-permute-start.4 = (bf16[32,2048]{1,0:T(8,128)(2,1)S(1)}, bf16[32,2048]{1,0:T(8,128)(2,1)S(1)}, u32[]{:S(2)}, u32[]{:S(2)}) collective-permute-start(bf16[32,2048]{1,0:T(8,128)(2,1)S(1)} %get-tuple-element.26.refs_0_), channel_id=1, source_target_pairs={{0,64},{1,65},{2,66},{3,67},{4,68},{5,69},{6,70},{7,71},{8,72},{9,... | collective-permute-start | bytes 393224 | tf_op jit(solution)/shard_map/ppermute | solution.py:163
  41.1 2.5 %collective-permute-start.5 = (bf16[32,2048]{1,0:T(8,128)(2,1)S(1)}, bf16[32,2048]{1,0:T(8,128)(2,1)S(1)}, u32[]{:S(2)}, u32[]{:S(2)}) collective-permute-start(bf16[32,2048]{1,0:T(8,128)(2,1)S(1)} %get-tuple-element.26.refs_0_), channel_id=1, source_target_pairs={{0,32},{1,33},{2,34},{3,35},{4,36},{5,37},{6,38},{7,39},{8,40},{9,... | collective-permute-start | bytes 393224 | tf_op jit(solution)/shard_map/ppermute | solution.py:163
  43.6 4.0 %collective-permute-start.6 = (bf16[32,6144]{1,0:T(8,128)(2,1)S(1)}, bf16[32,6144]{1,0:T(8,128)(2,1)S(1)}, u32[]{:S(2)}, u32[]{:S(2)}) collective-permute-start(bf16[32,6144]{1,0:T(8,128)(2,1)S(1)} %pad_maximum_fusion.3.refs_4_), channel_id=1, source_target_pairs={{0,96},{1,97},{2,98},{3,99},{4,100},{5,101},{6,102},{7,103},{8,104... | collective-permute-start | bytes 1179656 | tf_op jit(solution)/shard_map/ppermute | solution.py:163
  47.6 3.1 %collective-permute-start.7 = (bf16[32,6144]{1,0:T(8,128)(2,1)S(1)}, bf16[32,6144]{1,0:T(8,128)(2,1)S(1)}, u32[]{:S(2)}, u32[]{:S(2)}) collective-permute-start(bf16[32,6144]{1,0:T(8,128)(2,1)S(1)} %pad_maximum_fusion.3.refs_4_), channel_id=1, source_target_pairs={{0,64},{1,65},{2,66},{3,67},{4,68},{5,69},{6,70},{7,71},{8,72},{9,... | collective-permute-start | bytes 1179656 | tf_op jit(solution)/shard_map/ppermute | solution.py:163
  50.8 1.9 collective-permute-start.8
  53.1 18.5 %all_gather.16.refs_12_ = f32[512,128]{1,0:T(8,128)} all-gather(f32[128,128]{1,0:T(8,128)S(1)} %fusion.2), channel_id=1, replica_groups=mesh['segment'=16,'dp'=8,'mp'=4] {'mp'}, dimensions={0}, use_global_device_ids=true | all-gather | bytes 327680 | tf_op jit(solution)/shard_map/all_gather | solution.py:211
  74.5 13.3 %layer.1 = (bf16[128,512]{1,0:T(8,128)(2,1)}, bf16[128,128]{1,0:T(8,128)(2,1)}, bf16[128,128]{1,0:T(8,128)(2,1)}, f32[32,8192]{1,0:T(8,128)}, bf16[32,8192]{1,0:...) custom-call(bf16[32,2048]{1,0:T(8,128)(2,1)} %copy-done.2, bf16[32,2048]{1,0:T(8,128)(2,1)} %copy-done.7, ...), custom_call_target="tpu_custom_call" | custom-call | tf_op jit(solution)/shard_map/layer/pallas_call | solution.py:125
  87.9 4.6 %collective-permute-start.10 = (bf16[32,8192]{1,0:T(8,128)(2,1)}, bf16[32,8192]{1,0:T(8,128)(2,1)S(1)}, u32[]{:S(2)}, u32[]{:S(2)}) collective-permute-start(bf16[32,8192]{1,0:T(8,128)(2,1)} %get-tuple-element.15), channel_id=1, source_target_pairs={{0,64},{1,65},{2,66},{3,67},{4,68},{5,69},{6,70},{7,71},{8,72},{9,... | collective-permute-start | bytes 1572872 | tf_op jit(solution)/shard_map/ppermute | solution.py:163
  92.5 2.8 %collective-permute-start.11 = (bf16[32,8192]{1,0:T(8,128)(2,1)}, bf16[32,8192]{1,0:T(8,128)(2,1)}, u32[]{:S(2)}, u32[]{:S(2)}) collective-permute-start(bf16[32,8192]{1,0:T(8,128)(2,1)} %get-tuple-element.16), channel_id=1, source_target_pairs={{0,96},{1,97},{2,98},{3,99},{4,100},{5,101},{6,102},{7,103},{8,104... | collective-permute-start | bytes 1572872 | tf_op jit(solution)/shard_map/ppermute | solution.py:163
  95.3 2.5 %collective-permute-start.9 = (bf16[32,8192]{1,0:T(8,128)(2,1)}, bf16[32,8192]{1,0:T(8,128)(2,1)}, u32[]{:S(2)}, u32[]{:S(2)}) collective-permute-start(bf16[32,8192]{1,0:T(8,128)(2,1)} %get-tuple-element.14), channel_id=1, source_target_pairs={{0,32},{1,33},{2,34},{3,35},{4,36},{5,37},{6,38},{7,39},{8,40},{9,... | collective-permute-start | bytes 1572872 | tf_op jit(solution)/shard_map/ppermute | solution.py:163
  97.8 21.1 %all-gather = bf16[512,128]{1,0:T(8,128)(2,1)S(1)} all-gather(bf16[128,128]{1,0:T(8,128)(2,1)} %get-tuple-element.10), channel_id=2, replica_groups=mesh['segment'=16,'dp'=8,'mp'=4] {'mp'}, dimensions={0}, use_global_device_ids=true | all-gather | bytes 163840 | tf_op jit(solution)/shard_map/all_gather | solution.py:241
  120.0 2.2 %collective-permute-start.12 = (bf16[32,2048]{1,0:T(8,128)(2,1)}, bf16[32,2048]{1,0:T(8,128)(2,1)S(1)}, u32[]{:S(2)}, u32[]{:S(2)}) collective-permute-start(bf16[32,2048]{1,0:T(8,128)(2,1)} %get-tuple-element.20), channel_id=1, source_target_pairs={{0,32},{1,33},{2,34},{3,35},{4,36},{5,37},{6,38},{7,39},{8,40},{9,... | collective-permute-start | bytes 393224 | tf_op jit(solution)/shard_map/ppermute | solution.py:163
  122.2 4.8 %collective-permute-start.13 = (bf16[32,2048]{1,0:T(8,128)(2,1)}, bf16[32,2048]{1,0:T(8,128)(2,1)}, u32[]{:S(2)}, u32[]{:S(2)}) collective-permute-start(bf16[32,2048]{1,0:T(8,128)(2,1)} %get-tuple-element.22), channel_id=1, source_target_pairs={{0,64},{1,65},{2,66},{3,67},{4,68},{5,69},{6,70},{7,71},{8,72},{9,... | collective-permute-start | bytes 393224 | tf_op jit(solution)/shard_map/ppermute | solution.py:163
  127.9 1.9 collective-permute-start.14
  131.6 3.4 %collective-permute-done.14 = bf16[32,2048]{1,0:T(8,128)(2,1)S(1)} collective-permute-done((bf16[32,2048]{1,0:T(8,128)(2,1)}, bf16[32,2048]{1,0:T(8,128)(2,1)S(1)}, u32[]{:S(2)}, u32[]{:S(2)}) %collective-permute-start.14) | collective-permute-done | bytes 131104 | tf_op jit(solution)/shard_map/ppermute | solution.py:163
  136.0 1.9 collective-permute-start.15
  138.0 3.2 %collective-permute-start.16 = (bf16[8,8192]{1,0:T(8,128)(2,1)S(1)}, bf16[8,8192]{1,0:T(8,128)(2,1)S(1)}, u32[]{:S(2)}, u32[]{:S(2)}) collective-permute-start(bf16[8,8192]{1,0:T(8,128)(2,1)S(1)} %get-tuple-element.19), channel_id=1, source_target_pairs={{0,256},{1,257},{2,258},{3,259},{4,263},{5,260},{6,261},{7,262},{8... | collective-permute-start | bytes 393224 | tf_op jit(solution)/shard_map/ppermute | solution.py:163
  141.1 3.3 %collective-permute-start.17 = (bf16[8,8192]{1,0:T(8,128)(2,1)S(1)}, bf16[8,8192]{1,0:T(8,128)(2,1)S(1)}, u32[]{:S(2)}, u32[]{:S(2)}) collective-permute-start(bf16[8,8192]{1,0:T(8,128)(2,1)S(1)} %get-tuple-element.18), channel_id=1, source_target_pairs={{0,387},{1,384},{2,385},{3,386},{4,391},{5,388},{6,389},{7,390},{8... | collective-permute-start | bytes 393224 | tf_op jit(solution)/shard_map/ppermute | solution.py:163
  145.8 2.7 %collective-permute-done.17 = bf16[8,8192]{1,0:T(8,128)(2,1)S(1)} collective-permute-done((bf16[8,8192]{1,0:T(8,128)(2,1)S(1)}, bf16[8,8192]{1,0:T(8,128)(2,1)S(1)}, u32[]{:S(2)}, u32[]{:S(2)}) %collective-permute-start.17) | collective-permute-done | bytes 131104 | tf_op jit(solution)/shard_map/ppermute | solution.py:163
  148.6 7.0 %collective-permute-start.18 = (bf16[8,8192]{1,0:T(8,128)(2,1)S(1)}, bf16[8,8192]{1,0:T(8,128)(2,1)S(1)}, u32[]{:S(2)}, u32[]{:S(2)}) collective-permute-start(bf16[8,8192]{1,0:T(8,128)(2,1)S(1)} %fusion.6), channel_id=1, source_target_pairs={{0,2},{1,3},{2,0},{3,1},{4,6},{5,7},{6,4},{7,5},{8,10},{9,11},{10,... | collective-permute-start | bytes 393224 | tf_op jit(solution)/shard_map/ppermute | solution.py:163
  155.6 2.9 %collective-permute-start.19 = (bf16[8,8192]{1,0:T(8,128)(2,1)S(1)}, bf16[8,8192]{1,0:T(8,128)(2,1)S(1)}, u32[]{:S(2)}, u32[]{:S(2)}) collective-permute-start(bf16[8,8192]{1,0:T(8,128)(2,1)S(1)} %fusion.6), channel_id=1, source_target_pairs={{0,1},{1,2},{2,3},{3,0},{4,5},{5,6},{6,7},{7,4},{8,9},{9,10},{10,1... | collective-permute-start | bytes 393224 | tf_op jit(solution)/shard_map/ppermute | solution.py:163
  158.5 6.3 %collective-permute-start.20 = (bf16[8,8192]{1,0:T(8,128)(2,1)S(1)}, bf16[8,8192]{1,0:T(8,128)(2,1)S(1)}, u32[]{:S(2)}, u32[]{:S(2)}) collective-permute-start(bf16[8,8192]{1,0:T(8,128)(2,1)S(1)} %fusion.6), channel_id=1, source_target_pairs={{0,3},{1,0},{2,1},{3,2},{4,7},{5,4},{6,5},{7,6},{8,11},{9,8},{10,9... | collective-permute-start | bytes 393224 | tf_op jit(solution)/shard_map/ppermute | solution.py:163
  164.8 12.2 %collective-permute-done.18 = bf16[8,8192]{1,0:T(8,128)(2,1)S(1)} collective-permute-done((bf16[8,8192]{1,0:T(8,128)(2,1)S(1)}, bf16[8,8192]{1,0:T(8,128)(2,1)S(1)}, u32[]{:S(2)}, u32[]{:S(2)}) %collective-permute-start.18) | collective-permute-done | bytes 131104 | tf_op jit(solution)/shard_map/ppermute | solution.py:163
  177.0 2.5 %collective-permute-done.19 = bf16[8,8192]{1,0:T(8,128)(2,1)S(1)} collective-permute-done((bf16[8,8192]{1,0:T(8,128)(2,1)S(1)}, bf16[8,8192]{1,0:T(8,128)(2,1)S(1)}, u32[]{:S(2)}, u32[]{:S(2)}) %collective-permute-start.19) | collective-permute-done | bytes 131104 | tf_op jit(solution)/shard_map/ppermute | solution.py:163
  179.5 3.5 %collective-permute-done.20 = bf16[8,8192]{1,0:T(8,128)(2,1)S(1)} collective-permute-done((bf16[8,8192]{1,0:T(8,128)(2,1)S(1)}, bf16[8,8192]{1,0:T(8,128)(2,1)S(1)}, u32[]{:S(2)}, u32[]{:S(2)}) %collective-permute-start.20) | collective-permute-done | bytes 131104 | tf_op jit(solution)/shard_map/ppermute | solution.py:163
  184.8 14.0 %all_gather.19 = bf16[2304,128]{1,0:T(8,128)(2,1)S(1)} all-gather(bf16[288,128]{1,0:T(8,128)(2,1)S(1)} %convert_element_type.67), channel_id=1, replica_groups=mesh['segment'=16,'dp'=8,'mp'=4] {'dp'}, dimensions={0}, use_global_device_ids=true | all-gather | bytes 663552 | tf_op jit(solution)/shard_map/all_gather | solution.py:274
  (84 shorter events, 13.4 us)
Async XLA Ops:
  7.2 45.6 %copy-start = (bf16[1,2048,128]{2,1,0:T(8,128)(2,1)S(1)}, bf16[1,2048,128]{2,1,0:T(8,128)(2,1)}, u32[]{:S(2)}) copy-start(bf16[1,2048,128]{2,1,0:T(8,128)(2,1)} %param.10) | copy-start | bytes 1572868
  7.2 66.0 %all-gather.3.cloned.1.call-start = ((), (), s32[]{:S(2)}) async-start(), calls=%async_computation.1 | async-start | bytes 9437184 | tf_op jit(solution)/shard_map/all_gather | solution.py:209
  7.2 20.9 %copy-start.16 = (bf16[1,2,64,256]{3,2,1,0:T(8,128)(2,1)S(1)}, bf16[1,2,64,256]{3,2,1,0:T(8,128)(2,1)}, u32[]{:S(2)}) copy-start(bf16[1,2,64,256]{3,2,1,0:T(8,128)(2,1)} %param.11) | copy-start | bytes 196612
  9.8 174.1 %reduce-scatter.2.cloned.1.call-start = ((), (), s32[]{:S(2)}) async-start(), calls=%async_computation.2 | async-start | bytes 1327104 | tf_op jit(solution)/shard_map/reduce_scatter | solution.py:263
  9.8 19.8 %collective-permute-start = (bf16[8,8192]{1,0:T(8,128)(2,1)S(1)}, bf16[8,8192]{1,0:T(8,128)(2,1)S(1)}, u32[]{:S(2)}, u32[]{:S(2)}) collective-permute-start(bf16[8,8192]{1,0:T(8,128)(2,1)S(1)} %bitcast.37), channel_id=1, source_target_pairs={{0,387},{1,384},{2,385},{3,386},{4,391},{5,388},{6,389},{7,390},{8... | collective-permute-start | bytes 393224 | tf_op jit(solution)/shard_map/ppermute | solution.py:163
  21.8 7.8 %collective-permute-start.1 = (bf16[8,8192]{1,0:T(8,128)(2,1)S(1)}, bf16[8,8192]{1,0:T(8,128)(2,1)S(1)}, u32[]{:S(2)}, u32[]{:S(2)}) collective-permute-start(bf16[8,8192]{1,0:T(8,128)(2,1)S(1)} %bitcast.38), channel_id=1, source_target_pairs={{0,256},{1,257},{2,258},{3,259},{4,263},{5,260},{6,261},{7,262},{8... | collective-permute-start | bytes 393224 | tf_op jit(solution)/shard_map/ppermute | solution.py:163
  24.9 9.3 %collective-permute-start.2 = (bf16[8,8192]{1,0:T(8,128)(2,1)S(1)}, bf16[8,8192]{1,0:T(8,128)(2,1)S(1)}, u32[]{:S(2)}, u32[]{:S(2)}) collective-permute-start(bf16[8,8192]{1,0:T(8,128)(2,1)S(1)} %bitcast.39), channel_id=1, source_target_pairs={{0,128},{1,129},{2,130},{3,131},{4,132},{5,133},{6,134},{7,135},{8... | collective-permute-start | bytes 393224 | tf_op jit(solution)/shard_map/ppermute | solution.py:163
  34.2 18.9 %copy-start.2 = (bf16[32,2048]{1,0:T(8,128)(2,1)}, bf16[32,2048]{1,0:T(8,128)(2,1)S(1)}, u32[]{:S(2)}) copy-start(bf16[32,2048]{1,0:T(8,128)(2,1)S(1)} %get-tuple-element.26.refs_0_) | copy-start | bytes 393220
  34.2 16.5 %collective-permute-start.3 = (bf16[32,2048]{1,0:T(8,128)(2,1)S(1)}, bf16[32,2048]{1,0:T(8,128)(2,1)S(1)}, u32[]{:S(2)}, u32[]{:S(2)}) collective-permute-start(bf16[32,2048]{1,0:T(8,128)(2,1)S(1)} %get-tuple-element.26.refs_0_), channel_id=1, source_target_pairs={{0,96},{1,97},{2,98},{3,99},{4,100},{5,101},{6,102},{7,103},{8,104... | collective-permute-start | bytes 393224 | tf_op jit(solution)/shard_map/ppermute | solution.py:163
  38.6 14.1 %collective-permute-start.4 = (bf16[32,2048]{1,0:T(8,128)(2,1)S(1)}, bf16[32,2048]{1,0:T(8,128)(2,1)S(1)}, u32[]{:S(2)}, u32[]{:S(2)}) collective-permute-start(bf16[32,2048]{1,0:T(8,128)(2,1)S(1)} %get-tuple-element.26.refs_0_), channel_id=1, source_target_pairs={{0,64},{1,65},{2,66},{3,67},{4,68},{5,69},{6,70},{7,71},{8,72},{9,... | collective-permute-start | bytes 393224 | tf_op jit(solution)/shard_map/ppermute | solution.py:163
  41.1 11.7 %collective-permute-start.5 = (bf16[32,2048]{1,0:T(8,128)(2,1)S(1)}, bf16[32,2048]{1,0:T(8,128)(2,1)S(1)}, u32[]{:S(2)}, u32[]{:S(2)}) collective-permute-start(bf16[32,2048]{1,0:T(8,128)(2,1)S(1)} %get-tuple-element.26.refs_0_), channel_id=1, source_target_pairs={{0,32},{1,33},{2,34},{3,35},{4,36},{5,37},{6,38},{7,39},{8,40},{9,... | collective-permute-start | bytes 393224 | tf_op jit(solution)/shard_map/ppermute | solution.py:163
  43.6 28.0 %copy-start.1 = (bf16[32,6144]{1,0:T(8,128)(2,1)}, bf16[32,6144]{1,0:T(8,128)(2,1)S(1)}, u32[]{:S(2)}) copy-start(bf16[32,6144]{1,0:T(8,128)(2,1)S(1)} %pad_maximum_fusion.3.refs_4_) | copy-start | bytes 1179652
  43.6 28.0 %collective-permute-start.6 = (bf16[32,6144]{1,0:T(8,128)(2,1)S(1)}, bf16[32,6144]{1,0:T(8,128)(2,1)S(1)}, u32[]{:S(2)}, u32[]{:S(2)}) collective-permute-start(bf16[32,6144]{1,0:T(8,128)(2,1)S(1)} %pad_maximum_fusion.3.refs_4_), channel_id=1, source_target_pairs={{0,96},{1,97},{2,98},{3,99},{4,100},{5,101},{6,102},{7,103},{8,104... | collective-permute-start | bytes 1179656 | tf_op jit(solution)/shard_map/ppermute | solution.py:163
  47.6 24.0 %collective-permute-start.7 = (bf16[32,6144]{1,0:T(8,128)(2,1)S(1)}, bf16[32,6144]{1,0:T(8,128)(2,1)S(1)}, u32[]{:S(2)}, u32[]{:S(2)}) collective-permute-start(bf16[32,6144]{1,0:T(8,128)(2,1)S(1)} %pad_maximum_fusion.3.refs_4_), channel_id=1, source_target_pairs={{0,64},{1,65},{2,66},{3,67},{4,68},{5,69},{6,70},{7,71},{8,72},{9,... | collective-permute-start | bytes 1179656 | tf_op jit(solution)/shard_map/ppermute | solution.py:163
  50.8 20.8 %copy-start.7 = (bf16[32,2048]{1,0:T(8,128)(2,1)}, bf16[32,2048]{1,0:T(8,128)(2,1)S(1)}, u32[]{:S(2)}) copy-start(bf16[32,2048]{1,0:T(8,128)(2,1)S(1)} %collective-permute-done.3.refs_1_) | copy-start | bytes 393220
  50.8 20.9 %collective-permute-start.8 = (bf16[32,6144]{1,0:T(8,128)(2,1)S(1)}, bf16[32,6144]{1,0:T(8,128)(2,1)S(1)}, u32[]{:S(2)}, u32[]{:S(2)}) collective-permute-start(bf16[32,6144]{1,0:T(8,128)(2,1)S(1)} %pad_maximum_fusion.3.refs_4_), channel_id=1, source_target_pairs={{0,32},{1,33},{2,34},{3,35},{4,36},{5,37},{6,38},{7,39},{8,40},{9,... | collective-permute-start | bytes 1179656 | tf_op jit(solution)/shard_map/ppermute | solution.py:163
  52.8 18.9 %copy-start.9 = (bf16[32,2048]{1,0:T(8,128)(2,1)}, bf16[32,2048]{1,0:T(8,128)(2,1)S(1)}, u32[]{:S(2)}) copy-start(bf16[32,2048]{1,0:T(8,128)(2,1)S(1)} %collective-permute-done.4.refs_2_) | copy-start | bytes 393220
  52.8 18.8 %copy-start.11 = (bf16[32,2048]{1,0:T(8,128)(2,1)}, bf16[32,2048]{1,0:T(8,128)(2,1)S(1)}, u32[]{:S(2)}) copy-start(bf16[32,2048]{1,0:T(8,128)(2,1)S(1)} %collective-permute-done.5.refs_3_) | copy-start | bytes 393220
  87.9 40.0 %collective-permute-start.10 = (bf16[32,8192]{1,0:T(8,128)(2,1)}, bf16[32,8192]{1,0:T(8,128)(2,1)S(1)}, u32[]{:S(2)}, u32[]{:S(2)}) collective-permute-start(bf16[32,8192]{1,0:T(8,128)(2,1)} %get-tuple-element.15), channel_id=1, source_target_pairs={{0,64},{1,65},{2,66},{3,67},{4,68},{5,69},{6,70},{7,71},{8,72},{9,... | collective-permute-start | bytes 1572872 | tf_op jit(solution)/shard_map/ppermute | solution.py:163
  92.5 37.3 %collective-permute-start.11 = (bf16[32,8192]{1,0:T(8,128)(2,1)}, bf16[32,8192]{1,0:T(8,128)(2,1)}, u32[]{:S(2)}, u32[]{:S(2)}) collective-permute-start(bf16[32,8192]{1,0:T(8,128)(2,1)} %get-tuple-element.16), channel_id=1, source_target_pairs={{0,96},{1,97},{2,98},{3,99},{4,100},{5,101},{6,102},{7,103},{8,104... | collective-permute-start | bytes 1572872 | tf_op jit(solution)/shard_map/ppermute | solution.py:163
  95.3 34.5 %collective-permute-start.9 = (bf16[32,8192]{1,0:T(8,128)(2,1)}, bf16[32,8192]{1,0:T(8,128)(2,1)}, u32[]{:S(2)}, u32[]{:S(2)}) collective-permute-start(bf16[32,8192]{1,0:T(8,128)(2,1)} %get-tuple-element.14), channel_id=1, source_target_pairs={{0,32},{1,33},{2,34},{3,35},{4,36},{5,37},{6,38},{7,39},{8,40},{9,... | collective-permute-start | bytes 1572872 | tf_op jit(solution)/shard_map/ppermute | solution.py:163
  119.2 8.3 %copy-start.3 = (bf16[32,2048]{1,0:T(8,128)(2,1)S(1)}, bf16[32,2048]{1,0:T(8,128)(2,1)}, u32[]{:S(2)}) copy-start(bf16[32,2048]{1,0:T(8,128)(2,1)} %copy-done.2) | copy-start | bytes 393220
  119.2 8.3 %copy-start.8 = (bf16[32,2048]{1,0:T(8,128)(2,1)S(1)}, bf16[32,2048]{1,0:T(8,128)(2,1)}, u32[]{:S(2)}) copy-start(bf16[32,2048]{1,0:T(8,128)(2,1)} %copy-done.7) | copy-start | bytes 393220
  120.0 11.5 %collective-permute-start.12 = (bf16[32,2048]{1,0:T(8,128)(2,1)}, bf16[32,2048]{1,0:T(8,128)(2,1)S(1)}, u32[]{:S(2)}, u32[]{:S(2)}) collective-permute-start(bf16[32,2048]{1,0:T(8,128)(2,1)} %get-tuple-element.20), channel_id=1, source_target_pairs={{0,32},{1,33},{2,34},{3,35},{4,36},{5,37},{6,38},{7,39},{8,40},{9,... | collective-permute-start | bytes 393224 | tf_op jit(solution)/shard_map/ppermute | solution.py:163
  122.2 9.4 %collective-permute-start.13 = (bf16[32,2048]{1,0:T(8,128)(2,1)}, bf16[32,2048]{1,0:T(8,128)(2,1)}, u32[]{:S(2)}, u32[]{:S(2)}) collective-permute-start(bf16[32,2048]{1,0:T(8,128)(2,1)} %get-tuple-element.22), channel_id=1, source_target_pairs={{0,64},{1,65},{2,66},{3,67},{4,68},{5,69},{6,70},{7,71},{8,72},{9,... | collective-permute-start | bytes 393224 | tf_op jit(solution)/shard_map/ppermute | solution.py:163
  127.9 7.1 %collective-permute-start.14 = (bf16[32,2048]{1,0:T(8,128)(2,1)}, bf16[32,2048]{1,0:T(8,128)(2,1)S(1)}, u32[]{:S(2)}, u32[]{:S(2)}) collective-permute-start(bf16[32,2048]{1,0:T(8,128)(2,1)} %get-tuple-element.21), channel_id=1, source_target_pairs={{0,96},{1,97},{2,98},{3,99},{4,100},{5,101},{6,102},{7,103},{8,104... | collective-permute-start | bytes 393224 | tf_op jit(solution)/shard_map/ppermute | solution.py:163
  136.0 9.6 %collective-permute-start.15 = (bf16[8,8192]{1,0:T(8,128)(2,1)S(1)}, bf16[8,8192]{1,0:T(8,128)(2,1)S(1)}, u32[]{:S(2)}, u32[]{:S(2)}) collective-permute-start(bf16[8,8192]{1,0:T(8,128)(2,1)S(1)} %get-tuple-element.17), channel_id=1, source_target_pairs={{0,128},{1,129},{2,130},{3,131},{4,132},{5,133},{6,134},{7,135},{8... | collective-permute-start | bytes 393224 | tf_op jit(solution)/shard_map/ppermute | solution.py:163
  138.0 7.8 %collective-permute-start.16 = (bf16[8,8192]{1,0:T(8,128)(2,1)S(1)}, bf16[8,8192]{1,0:T(8,128)(2,1)S(1)}, u32[]{:S(2)}, u32[]{:S(2)}) collective-permute-start(bf16[8,8192]{1,0:T(8,128)(2,1)S(1)} %get-tuple-element.19), channel_id=1, source_target_pairs={{0,256},{1,257},{2,258},{3,259},{4,263},{5,260},{6,261},{7,262},{8... | collective-permute-start | bytes 393224 | tf_op jit(solution)/shard_map/ppermute | solution.py:163
  141.1 7.4 %collective-permute-start.17 = (bf16[8,8192]{1,0:T(8,128)(2,1)S(1)}, bf16[8,8192]{1,0:T(8,128)(2,1)S(1)}, u32[]{:S(2)}, u32[]{:S(2)}) collective-permute-start(bf16[8,8192]{1,0:T(8,128)(2,1)S(1)} %get-tuple-element.18), channel_id=1, source_target_pairs={{0,387},{1,384},{2,385},{3,386},{4,391},{5,388},{6,389},{7,390},{8... | collective-permute-start | bytes 393224 | tf_op jit(solution)/shard_map/ppermute | solution.py:163
  148.6 28.4 %collective-permute-start.18 = (bf16[8,8192]{1,0:T(8,128)(2,1)S(1)}, bf16[8,8192]{1,0:T(8,128)(2,1)S(1)}, u32[]{:S(2)}, u32[]{:S(2)}) collective-permute-start(bf16[8,8192]{1,0:T(8,128)(2,1)S(1)} %fusion.6), channel_id=1, source_target_pairs={{0,2},{1,3},{2,0},{3,1},{4,6},{5,7},{6,4},{7,5},{8,10},{9,11},{10,... | collective-permute-start | bytes 393224 | tf_op jit(solution)/shard_map/ppermute | solution.py:163
  155.6 23.9 %collective-permute-start.19 = (bf16[8,8192]{1,0:T(8,128)(2,1)S(1)}, bf16[8,8192]{1,0:T(8,128)(2,1)S(1)}, u32[]{:S(2)}, u32[]{:S(2)}) collective-permute-start(bf16[8,8192]{1,0:T(8,128)(2,1)S(1)} %fusion.6), channel_id=1, source_target_pairs={{0,1},{1,2},{2,3},{3,0},{4,5},{5,6},{6,7},{7,4},{8,9},{9,10},{10,1... | collective-permute-start | bytes 393224 | tf_op jit(solution)/shard_map/ppermute | solution.py:163
  158.5 24.5 %collective-permute-start.20 = (bf16[8,8192]{1,0:T(8,128)(2,1)S(1)}, bf16[8,8192]{1,0:T(8,128)(2,1)S(1)}, u32[]{:S(2)}, u32[]{:S(2)}) collective-permute-start(bf16[8,8192]{1,0:T(8,128)(2,1)S(1)} %fusion.6), channel_id=1, source_target_pairs={{0,3},{1,0},{2,1},{3,2},{4,7},{5,4},{6,5},{7,6},{8,11},{9,8},{10,9... | collective-permute-start | bytes 393224 | tf_op jit(solution)/shard_map/ppermute | solution.py:163
  (8 other events, 43.9 us)
Sparse Core Ops, SparseCore 0:
  10.1 63.0 all-gather.2
  145.7 36.5 reduce-scatter.1

commit v8 on v7

--- a/solution.py
+++ b/solution.py
@@ -101,7 +101,7 @@
     out_copies = []
     for c in range(CHUNKS):
         total = lax.dot_general(kv_grad, weight_ref[chunk(c), :], contracted_columns, preferred_element_type=f32)
-        own_ref[:, chunk(c)] = total[:block]
+        own_ref[:, chunk(c)] = total[:block].astype(bf16)
         for i, ref in enumerate(away_refs):
             ref[:, chunk(c)] = total[(i + 1) * block : (i + 2) * block].astype(bf16)
         for i, (ref, target) in enumerate(zip((own_ref, *away_refs), block_hbm)):
@@ -119,7 +119,7 @@
     columns = weight.shape[1]
     rank = low.shape[1]
     block = rows // SIDE
-    blocks = [(block, width, f32)] + [(block, width, bf16)] * (SIDE - 1)
+    blocks = [(block, width, bf16)] * SIDE
     outside = pl.BlockSpec(memory_space=pl.ANY)
     inside_vmem = pl.BlockSpec(memory_space=pltpu.VMEM)
     return pl.pallas_call(
@@ -232,7 +232,7 @@
         )
 
         image_grad = (
-            stay
+            stay.astype(f32)
             + shift(next_x, dx=1).astype(f32)
             + shift(far_x, dx=2, opposite=True).astype(f32)
             + shift(prior_x, dx=-1).astype(f32)

time: 208 us -> 208 us (level)
  no operation moved by 1% of the time
where the time goes in v8:
time: 208 us; the launch traced here: 207 us
  starting transfers between devices  79.6 us (38%)
  blocking collectives  53.3 us (26%)
  waiting for transfers between devices  31 us (15%)
  between operations  16 us (8%)
  Pallas kernels  13.3 us (6%)
  other arithmetic  6.28 us (3%)
  local copies, waits for them, and re-layouts  6.24 us (3%)
    ppermute x21, starting transfers between devices, shift(): return lax.ppermute(v, AXES, pairs)  79.5 us
    ppermute x21, waiting for transfers between devices, shift(): return lax.ppermute(v, AXES, pairs)  29.4 us
    all_gather x1, blocking collectives, body(): back = lax.all_gather(back, 'mp', axis=0)  21 us
    all_gather x1, blocking collectives, body(): low = lax.all_gather(low, 'mp', axis=0, tiled=True)  18.5 us
    all_gather x1, blocking collectives, body(): both = lax.all_gather(both, 'dp', axis=0, tiled=True)  13.8 us
    pallas_call x1, Pallas kernels, layer(): pl.pallas_call(layer_kernel, in_specs=[outside] * (2 * SIDE + 3) + [pl.Bl...  13.3 us
  transfers between devices with their start and end apart: 23, of which 8 were waited for; matrix products, arithmetic and copies ran while one was open for 3% of the time, Pallas kernels for 0%

profile of v8, /device:TPU:1, one launch (start us, length us, event | category | flops | bytes accessed | tf_op | source)
XLA Modules:
  0.0 207.1 jit_solution(4355421334185500502)
XLA Ops:
  7.2 2.5 %copy.11 = bf16[128,8,2,256]{3,1,2,0:T(8,128)(2,1)} copy(bf16[128,8,2,256]{3,2,1,0:T(2,128)(2,1)} %bitcast.33) | data formatting | bytes 2097152
  9.8 11.9 %collective-permute-start = (bf16[8,8192]{1,0:T(8,128)(2,1)S(1)}, bf16[8,8192]{1,0:T(8,128)(2,1)S(1)}, u32[]{:S(2)}, u32[]{:S(2)}) collective-permute-start(bf16[8,8192]{1,0:T(8,128)(2,1)S(1)} %bitcast.37), channel_id=1, source_target_pairs={{0,387},{1,384},{2,385},{3,386},{4,391},{5,388},{6,389},{7,390},{8... | collective-permute-start | bytes 393224 | tf_op jit(solution)/shard_map/ppermute | solution.py:163
  21.8 3.1 %collective-permute-start.1 = (bf16[8,8192]{1,0:T(8,128)(2,1)S(1)}, bf16[8,8192]{1,0:T(8,128)(2,1)S(1)}, u32[]{:S(2)}, u32[]{:S(2)}) collective-permute-start(bf16[8,8192]{1,0:T(8,128)(2,1)S(1)} %bitcast.38), channel_id=1, source_target_pairs={{0,256},{1,257},{2,258},{3,259},{4,263},{5,260},{6,261},{7,262},{8... | collective-permute-start | bytes 393224 | tf_op jit(solution)/shard_map/ppermute | solution.py:163
  24.9 2.6 %collective-permute-start.2 = (bf16[8,8192]{1,0:T(8,128)(2,1)S(1)}, bf16[8,8192]{1,0:T(8,128)(2,1)S(1)}, u32[]{:S(2)}, u32[]{:S(2)}) collective-permute-start(bf16[8,8192]{1,0:T(8,128)(2,1)S(1)} %bitcast.39), channel_id=1, source_target_pairs={{0,128},{1,129},{2,130},{3,131},{4,132},{5,133},{6,134},{7,135},{8... | collective-permute-start | bytes 393224 | tf_op jit(solution)/shard_map/ppermute | solution.py:163
  29.6 4.5 %collective-permute-done.2 = bf16[8,8192]{1,0:T(8,128)(2,1)S(1)} collective-permute-done((bf16[8,8192]{1,0:T(8,128)(2,1)S(1)}, bf16[8,8192]{1,0:T(8,128)(2,1)S(1)}, u32[]{:S(2)}, u32[]{:S(2)}) %collective-permute-start.2) | collective-permute-done | bytes 131104 | tf_op jit(solution)/shard_map/ppermute | solution.py:163
  34.2 4.4 %collective-permute-start.3 = (bf16[32,2048]{1,0:T(8,128)(2,1)S(1)}, bf16[32,2048]{1,0:T(8,128)(2,1)S(1)}, u32[]{:S(2)}, u32[]{:S(2)}) collective-permute-start(bf16[32,2048]{1,0:T(8,128)(2,1)S(1)} %get-tuple-element.26.refs_0_), channel_id=1, source_target_pairs={{0,96},{1,97},{2,98},{3,99},{4,100},{5,101},{6,102},{7,103},{8,104... | collective-permute-start | bytes 393224 | tf_op jit(solution)/shard_map/ppermute | solution.py:163
  38.6 2.4 %collective-permute-start.4 = (bf16[32,2048]{1,0:T(8,128)(2,1)S(1)}, bf16[32,2048]{1,0:T(8,128)(2,1)S(1)}, u32[]{:S(2)}, u32[]{:S(2)}) collective-permute-start(bf16[32,2048]{1,0:T(8,128)(2,1)S(1)} %get-tuple-element.26.refs_0_), channel_id=1, source_target_pairs={{0,64},{1,65},{2,66},{3,67},{4,68},{5,69},{6,70},{7,71},{8,72},{9,... | collective-permute-start | bytes 393224 | tf_op jit(solution)/shard_map/ppermute | solution.py:163
  41.1 2.5 %collective-permute-start.5 = (bf16[32,2048]{1,0:T(8,128)(2,1)S(1)}, bf16[32,2048]{1,0:T(8,128)(2,1)S(1)}, u32[]{:S(2)}, u32[]{:S(2)}) collective-permute-start(bf16[32,2048]{1,0:T(8,128)(2,1)S(1)} %get-tuple-element.26.refs_0_), channel_id=1, source_target_pairs={{0,32},{1,33},{2,34},{3,35},{4,36},{5,37},{6,38},{7,39},{8,40},{9,... | collective-permute-start | bytes 393224 | tf_op jit(solution)/shard_map/ppermute | solution.py:163
  43.6 4.0 %collective-permute-start.6 = (bf16[32,6144]{1,0:T(8,128)(2,1)S(1)}, bf16[32,6144]{1,0:T(8,128)(2,1)S(1)}, u32[]{:S(2)}, u32[]{:S(2)}) collective-permute-start(bf16[32,6144]{1,0:T(8,128)(2,1)S(1)} %pad_maximum_fusion.3.refs_4_), channel_id=1, source_target_pairs={{0,96},{1,97},{2,98},{3,99},{4,100},{5,101},{6,102},{7,103},{8,104... | collective-permute-start | bytes 1179656 | tf_op jit(solution)/shard_map/ppermute | solution.py:163
  47.6 3.1 %collective-permute-start.7 = (bf16[32,6144]{1,0:T(8,128)(2,1)S(1)}, bf16[32,6144]{1,0:T(8,128)(2,1)S(1)}, u32[]{:S(2)}, u32[]{:S(2)}) collective-permute-start(bf16[32,6144]{1,0:T(8,128)(2,1)S(1)} %pad_maximum_fusion.3.refs_4_), channel_id=1, source_target_pairs={{0,64},{1,65},{2,66},{3,67},{4,68},{5,69},{6,70},{7,71},{8,72},{9,... | collective-permute-start | bytes 1179656 | tf_op jit(solution)/shard_map/ppermute | solution.py:163
  50.8 1.9 collective-permute-start.8
  53.1 18.5 %all_gather.16.refs_12_ = f32[512,128]{1,0:T(8,128)} all-gather(f32[128,128]{1,0:T(8,128)S(1)} %fusion.2), channel_id=1, replica_groups=mesh['segment'=16,'dp'=8,'mp'=4] {'mp'}, dimensions={0}, use_global_device_ids=true | all-gather | bytes 327680 | tf_op jit(solution)/shard_map/all_gather | solution.py:211
  74.5 13.3 %layer.1 = (bf16[128,512]{1,0:T(8,128)(2,1)}, bf16[128,128]{1,0:T(8,128)(2,1)}, bf16[128,128]{1,0:T(8,128)(2,1)}, bf16[32,8192]{1,0:T(8,128)(2,1)}, bf16[32,8192...) custom-call(bf16[32,2048]{1,0:T(8,128)(2,1)} %copy-done.2, bf16[32,2048]{1,0:T(8,128)(2,1)} %copy-done.8, ...), custom_call_target="tpu_custom_call" | custom-call | tf_op jit(solution)/shard_map/layer/pallas_call | solution.py:125
  87.9 4.6 %collective-permute-start.10 = (bf16[32,8192]{1,0:T(8,128)(2,1)}, bf16[32,8192]{1,0:T(8,128)(2,1)}, u32[]{:S(2)}, u32[]{:S(2)}) collective-permute-start(bf16[32,8192]{1,0:T(8,128)(2,1)} %get-tuple-element.15), channel_id=1, source_target_pairs={{0,64},{1,65},{2,66},{3,67},{4,68},{5,69},{6,70},{7,71},{8,72},{9,... | collective-permute-start | bytes 1572872 | tf_op jit(solution)/shard_map/ppermute | solution.py:163
  92.5 2.8 %collective-permute-start.11 = (bf16[32,8192]{1,0:T(8,128)(2,1)}, bf16[32,8192]{1,0:T(8,128)(2,1)}, u32[]{:S(2)}, u32[]{:S(2)}) collective-permute-start(bf16[32,8192]{1,0:T(8,128)(2,1)} %get-tuple-element.16), channel_id=1, source_target_pairs={{0,96},{1,97},{2,98},{3,99},{4,100},{5,101},{6,102},{7,103},{8,104... | collective-permute-start | bytes 1572872 | tf_op jit(solution)/shard_map/ppermute | solution.py:163
  95.3 2.5 %collective-permute-start.9 = (bf16[32,8192]{1,0:T(8,128)(2,1)}, bf16[32,8192]{1,0:T(8,128)(2,1)}, u32[]{:S(2)}, u32[]{:S(2)}) collective-permute-start(bf16[32,8192]{1,0:T(8,128)(2,1)} %get-tuple-element.14), channel_id=1, source_target_pairs={{0,32},{1,33},{2,34},{3,35},{4,36},{5,37},{6,38},{7,39},{8,40},{9,... | collective-permute-start | bytes 1572872 | tf_op jit(solution)/shard_map/ppermute | solution.py:163
  97.8 21.0 %all-gather = bf16[512,128]{1,0:T(8,128)(2,1)S(1)} all-gather(bf16[128,128]{1,0:T(8,128)(2,1)} %get-tuple-element.10), channel_id=2, replica_groups=mesh['segment'=16,'dp'=8,'mp'=4] {'mp'}, dimensions={0}, use_global_device_ids=true | all-gather | bytes 163840 | tf_op jit(solution)/shard_map/all_gather | solution.py:241
  120.0 2.1 %collective-permute-start.12 = (bf16[32,2048]{1,0:T(8,128)(2,1)}, bf16[32,2048]{1,0:T(8,128)(2,1)S(1)}, u32[]{:S(2)}, u32[]{:S(2)}) collective-permute-start(bf16[32,2048]{1,0:T(8,128)(2,1)} %get-tuple-element.20), channel_id=1, source_target_pairs={{0,32},{1,33},{2,34},{3,35},{4,36},{5,37},{6,38},{7,39},{8,40},{9,... | collective-permute-start | bytes 393224 | tf_op jit(solution)/shard_map/ppermute | solution.py:163
  122.1 5.0 %collective-permute-start.13 = (bf16[32,2048]{1,0:T(8,128)(2,1)}, bf16[32,2048]{1,0:T(8,128)(2,1)}, u32[]{:S(2)}, u32[]{:S(2)}) collective-permute-start(bf16[32,2048]{1,0:T(8,128)(2,1)} %get-tuple-element.22), channel_id=1, source_target_pairs={{0,64},{1,65},{2,66},{3,67},{4,68},{5,69},{6,70},{7,71},{8,72},{9,... | collective-permute-start | bytes 393224 | tf_op jit(solution)/shard_map/ppermute | solution.py:163
  128.0 1.9 collective-permute-start.14
  131.6 3.4 %collective-permute-done.14 = bf16[32,2048]{1,0:T(8,128)(2,1)S(1)} collective-permute-done((bf16[32,2048]{1,0:T(8,128)(2,1)}, bf16[32,2048]{1,0:T(8,128)(2,1)S(1)}, u32[]{:S(2)}, u32[]{:S(2)}) %collective-permute-start.14) | collective-permute-done | bytes 131104 | tf_op jit(solution)/shard_map/ppermute | solution.py:163
  136.0 1.9 collective-permute-start.15
  138.0 3.2 %collective-permute-start.16 = (bf16[8,8192]{1,0:T(8,128)(2,1)S(1)}, bf16[8,8192]{1,0:T(8,128)(2,1)S(1)}, u32[]{:S(2)}, u32[]{:S(2)}) collective-permute-start(bf16[8,8192]{1,0:T(8,128)(2,1)S(1)} %get-tuple-element.19), channel_id=1, source_target_pairs={{0,256},{1,257},{2,258},{3,259},{4,263},{5,260},{6,261},{7,262},{8... | collective-permute-start | bytes 393224 | tf_op jit(solution)/shard_map/ppermute | solution.py:163
  141.1 3.3 %collective-permute-start.17 = (bf16[8,8192]{1,0:T(8,128)(2,1)S(1)}, bf16[8,8192]{1,0:T(8,128)(2,1)S(1)}, u32[]{:S(2)}, u32[]{:S(2)}) collective-permute-start(bf16[8,8192]{1,0:T(8,128)(2,1)S(1)} %get-tuple-element.18), channel_id=1, source_target_pairs={{0,387},{1,384},{2,385},{3,386},{4,391},{5,388},{6,389},{7,390},{8... | collective-permute-start | bytes 393224 | tf_op jit(solution)/shard_map/ppermute | solution.py:163
  145.7 2.8 %collective-permute-done.17 = bf16[8,8192]{1,0:T(8,128)(2,1)S(1)} collective-permute-done((bf16[8,8192]{1,0:T(8,128)(2,1)S(1)}, bf16[8,8192]{1,0:T(8,128)(2,1)S(1)}, u32[]{:S(2)}, u32[]{:S(2)}) %collective-permute-start.17) | collective-permute-done | bytes 131104 | tf_op jit(solution)/shard_map/ppermute | solution.py:163
  148.6 7.0 %collective-permute-start.18 = (bf16[8,8192]{1,0:T(8,128)(2,1)S(1)}, bf16[8,8192]{1,0:T(8,128)(2,1)S(1)}, u32[]{:S(2)}, u32[]{:S(2)}) collective-permute-start(bf16[8,8192]{1,0:T(8,128)(2,1)S(1)} %fusion.6), channel_id=1, source_target_pairs={{0,2},{1,3},{2,0},{3,1},{4,6},{5,7},{6,4},{7,5},{8,10},{9,11},{10,... | collective-permute-start | bytes 393224 | tf_op jit(solution)/shard_map/ppermute | solution.py:163
  155.6 2.9 %collective-permute-start.19 = (bf16[8,8192]{1,0:T(8,128)(2,1)S(1)}, bf16[8,8192]{1,0:T(8,128)(2,1)S(1)}, u32[]{:S(2)}, u32[]{:S(2)}) collective-permute-start(bf16[8,8192]{1,0:T(8,128)(2,1)S(1)} %fusion.6), channel_id=1, source_target_pairs={{0,1},{1,2},{2,3},{3,0},{4,5},{5,6},{6,7},{7,4},{8,9},{9,10},{10,1... | collective-permute-start | bytes 393224 | tf_op jit(solution)/shard_map/ppermute | solution.py:163
  158.5 6.3 %collective-permute-start.20 = (bf16[8,8192]{1,0:T(8,128)(2,1)S(1)}, bf16[8,8192]{1,0:T(8,128)(2,1)S(1)}, u32[]{:S(2)}, u32[]{:S(2)}) collective-permute-start(bf16[8,8192]{1,0:T(8,128)(2,1)S(1)} %fusion.6), channel_id=1, source_target_pairs={{0,3},{1,0},{2,1},{3,2},{4,7},{5,4},{6,5},{7,6},{8,11},{9,8},{10,9... | collective-permute-start | bytes 393224 | tf_op jit(solution)/shard_map/ppermute | solution.py:163
  164.8 12.2 %collective-permute-done.18 = bf16[8,8192]{1,0:T(8,128)(2,1)S(1)} collective-permute-done((bf16[8,8192]{1,0:T(8,128)(2,1)S(1)}, bf16[8,8192]{1,0:T(8,128)(2,1)S(1)}, u32[]{:S(2)}, u32[]{:S(2)}) %collective-permute-start.18) | collective-permute-done | bytes 131104 | tf_op jit(solution)/shard_map/ppermute | solution.py:163
  177.0 2.5 %collective-permute-done.19 = bf16[8,8192]{1,0:T(8,128)(2,1)S(1)} collective-permute-done((bf16[8,8192]{1,0:T(8,128)(2,1)S(1)}, bf16[8,8192]{1,0:T(8,128)(2,1)S(1)}, u32[]{:S(2)}, u32[]{:S(2)}) %collective-permute-start.19) | collective-permute-done | bytes 131104 | tf_op jit(solution)/shard_map/ppermute | solution.py:163
  179.5 3.8 %collective-permute-done.20 = bf16[8,8192]{1,0:T(8,128)(2,1)S(1)} collective-permute-done((bf16[8,8192]{1,0:T(8,128)(2,1)S(1)}, bf16[8,8192]{1,0:T(8,128)(2,1)S(1)}, u32[]{:S(2)}, u32[]{:S(2)}) %collective-permute-start.20) | collective-permute-done | bytes 131104 | tf_op jit(solution)/shard_map/ppermute | solution.py:163
  185.0 13.8 %all_gather.19 = bf16[2304,128]{1,0:T(8,128)(2,1)S(1)} all-gather(bf16[288,128]{1,0:T(8,128)(2,1)S(1)} %convert_element_type.70), channel_id=1, replica_groups=mesh['segment'=16,'dp'=8,'mp'=4] {'dp'}, dimensions={0}, use_global_device_ids=true | all-gather | bytes 663552 | tf_op jit(solution)/shard_map/all_gather | solution.py:274
  (86 shorter events, 13.2 us)
Async XLA Ops:
  7.2 45.6 %copy-start = (bf16[1,2048,128]{2,1,0:T(8,128)(2,1)S(1)}, bf16[1,2048,128]{2,1,0:T(8,128)(2,1)}, u32[]{:S(2)}) copy-start(bf16[1,2048,128]{2,1,0:T(8,128)(2,1)} %param.10) | copy-start | bytes 1572868
  7.2 66.0 %all-gather.3.cloned.1.call-start = ((), (), s32[]{:S(2)}) async-start(), calls=%async_computation.1 | async-start | bytes 9437184 | tf_op jit(solution)/shard_map/all_gather | solution.py:209
  7.2 20.9 %copy-start.17 = (bf16[1,2,64,256]{3,2,1,0:T(8,128)(2,1)S(1)}, bf16[1,2,64,256]{3,2,1,0:T(8,128)(2,1)}, u32[]{:S(2)}) copy-start(bf16[1,2,64,256]{3,2,1,0:T(8,128)(2,1)} %param.11) | copy-start | bytes 196612
  9.8 174.3 %reduce-scatter.2.cloned.1.call-start = ((), (), s32[]{:S(2)}) async-start(), calls=%async_computation.2 | async-start | bytes 1327104 | tf_op jit(solution)/shard_map/reduce_scatter | solution.py:263
  9.8 19.8 %collective-permute-start = (bf16[8,8192]{1,0:T(8,128)(2,1)S(1)}, bf16[8,8192]{1,0:T(8,128)(2,1)S(1)}, u32[]{:S(2)}, u32[]{:S(2)}) collective-permute-start(bf16[8,8192]{1,0:T(8,128)(2,1)S(1)} %bitcast.37), channel_id=1, source_target_pairs={{0,387},{1,384},{2,385},{3,386},{4,391},{5,388},{6,389},{7,390},{8... | collective-permute-start | bytes 393224 | tf_op jit(solution)/shard_map/ppermute | solution.py:163
  21.8 7.8 %collective-permute-start.1 = (bf16[8,8192]{1,0:T(8,128)(2,1)S(1)}, bf16[8,8192]{1,0:T(8,128)(2,1)S(1)}, u32[]{:S(2)}, u32[]{:S(2)}) collective-permute-start(bf16[8,8192]{1,0:T(8,128)(2,1)S(1)} %bitcast.38), channel_id=1, source_target_pairs={{0,256},{1,257},{2,258},{3,259},{4,263},{5,260},{6,261},{7,262},{8... | collective-permute-start | bytes 393224 | tf_op jit(solution)/shard_map/ppermute | solution.py:163
  24.9 9.3 %collective-permute-start.2 = (bf16[8,8192]{1,0:T(8,128)(2,1)S(1)}, bf16[8,8192]{1,0:T(8,128)(2,1)S(1)}, u32[]{:S(2)}, u32[]{:S(2)}) collective-permute-start(bf16[8,8192]{1,0:T(8,128)(2,1)S(1)} %bitcast.39), channel_id=1, source_target_pairs={{0,128},{1,129},{2,130},{3,131},{4,132},{5,133},{6,134},{7,135},{8... | collective-permute-start | bytes 393224 | tf_op jit(solution)/shard_map/ppermute | solution.py:163
  34.2 18.9 %copy-start.2 = (bf16[32,2048]{1,0:T(8,128)(2,1)}, bf16[32,2048]{1,0:T(8,128)(2,1)S(1)}, u32[]{:S(2)}) copy-start(bf16[32,2048]{1,0:T(8,128)(2,1)S(1)} %get-tuple-element.26.refs_0_) | copy-start | bytes 393220
  34.2 16.5 %collective-permute-start.3 = (bf16[32,2048]{1,0:T(8,128)(2,1)S(1)}, bf16[32,2048]{1,0:T(8,128)(2,1)S(1)}, u32[]{:S(2)}, u32[]{:S(2)}) collective-permute-start(bf16[32,2048]{1,0:T(8,128)(2,1)S(1)} %get-tuple-element.26.refs_0_), channel_id=1, source_target_pairs={{0,96},{1,97},{2,98},{3,99},{4,100},{5,101},{6,102},{7,103},{8,104... | collective-permute-start | bytes 393224 | tf_op jit(solution)/shard_map/ppermute | solution.py:163
  38.6 14.1 %collective-permute-start.4 = (bf16[32,2048]{1,0:T(8,128)(2,1)S(1)}, bf16[32,2048]{1,0:T(8,128)(2,1)S(1)}, u32[]{:S(2)}, u32[]{:S(2)}) collective-permute-start(bf16[32,2048]{1,0:T(8,128)(2,1)S(1)} %get-tuple-element.26.refs_0_), channel_id=1, source_target_pairs={{0,64},{1,65},{2,66},{3,67},{4,68},{5,69},{6,70},{7,71},{8,72},{9,... | collective-permute-start | bytes 393224 | tf_op jit(solution)/shard_map/ppermute | solution.py:163
  41.1 11.7 %collective-permute-start.5 = (bf16[32,2048]{1,0:T(8,128)(2,1)S(1)}, bf16[32,2048]{1,0:T(8,128)(2,1)S(1)}, u32[]{:S(2)}, u32[]{:S(2)}) collective-permute-start(bf16[32,2048]{1,0:T(8,128)(2,1)S(1)} %get-tuple-element.26.refs_0_), channel_id=1, source_target_pairs={{0,32},{1,33},{2,34},{3,35},{4,36},{5,37},{6,38},{7,39},{8,40},{9,... | collective-permute-start | bytes 393224 | tf_op jit(solution)/shard_map/ppermute | solution.py:163
  43.6 28.0 %copy-start.1 = (bf16[32,6144]{1,0:T(8,128)(2,1)}, bf16[32,6144]{1,0:T(8,128)(2,1)S(1)}, u32[]{:S(2)}) copy-start(bf16[32,6144]{1,0:T(8,128)(2,1)S(1)} %pad_maximum_fusion.3.refs_4_) | copy-start | bytes 1179652
  43.6 28.0 %collective-permute-start.6 = (bf16[32,6144]{1,0:T(8,128)(2,1)S(1)}, bf16[32,6144]{1,0:T(8,128)(2,1)S(1)}, u32[]{:S(2)}, u32[]{:S(2)}) collective-permute-start(bf16[32,6144]{1,0:T(8,128)(2,1)S(1)} %pad_maximum_fusion.3.refs_4_), channel_id=1, source_target_pairs={{0,96},{1,97},{2,98},{3,99},{4,100},{5,101},{6,102},{7,103},{8,104... | collective-permute-start | bytes 1179656 | tf_op jit(solution)/shard_map/ppermute | solution.py:163
  47.6 24.0 %collective-permute-start.7 = (bf16[32,6144]{1,0:T(8,128)(2,1)S(1)}, bf16[32,6144]{1,0:T(8,128)(2,1)S(1)}, u32[]{:S(2)}, u32[]{:S(2)}) collective-permute-start(bf16[32,6144]{1,0:T(8,128)(2,1)S(1)} %pad_maximum_fusion.3.refs_4_), channel_id=1, source_target_pairs={{0,64},{1,65},{2,66},{3,67},{4,68},{5,69},{6,70},{7,71},{8,72},{9,... | collective-permute-start | bytes 1179656 | tf_op jit(solution)/shard_map/ppermute | solution.py:163
  50.8 20.8 %copy-start.8 = (bf16[32,2048]{1,0:T(8,128)(2,1)}, bf16[32,2048]{1,0:T(8,128)(2,1)S(1)}, u32[]{:S(2)}) copy-start(bf16[32,2048]{1,0:T(8,128)(2,1)S(1)} %collective-permute-done.3.refs_1_) | copy-start | bytes 393220
  50.8 20.9 %collective-permute-start.8 = (bf16[32,6144]{1,0:T(8,128)(2,1)S(1)}, bf16[32,6144]{1,0:T(8,128)(2,1)S(1)}, u32[]{:S(2)}, u32[]{:S(2)}) collective-permute-start(bf16[32,6144]{1,0:T(8,128)(2,1)S(1)} %pad_maximum_fusion.3.refs_4_), channel_id=1, source_target_pairs={{0,32},{1,33},{2,34},{3,35},{4,36},{5,37},{6,38},{7,39},{8,40},{9,... | collective-permute-start | bytes 1179656 | tf_op jit(solution)/shard_map/ppermute | solution.py:163
  52.8 18.9 %copy-start.10 = (bf16[32,2048]{1,0:T(8,128)(2,1)}, bf16[32,2048]{1,0:T(8,128)(2,1)S(1)}, u32[]{:S(2)}) copy-start(bf16[32,2048]{1,0:T(8,128)(2,1)S(1)} %collective-permute-done.4.refs_2_) | copy-start | bytes 393220
  52.8 18.8 %copy-start.12 = (bf16[32,2048]{1,0:T(8,128)(2,1)}, bf16[32,2048]{1,0:T(8,128)(2,1)S(1)}, u32[]{:S(2)}) copy-start(bf16[32,2048]{1,0:T(8,128)(2,1)S(1)} %collective-permute-done.5.refs_3_) | copy-start | bytes 393220
  87.9 40.1 %collective-permute-start.10 = (bf16[32,8192]{1,0:T(8,128)(2,1)}, bf16[32,8192]{1,0:T(8,128)(2,1)}, u32[]{:S(2)}, u32[]{:S(2)}) collective-permute-start(bf16[32,8192]{1,0:T(8,128)(2,1)} %get-tuple-element.15), channel_id=1, source_target_pairs={{0,64},{1,65},{2,66},{3,67},{4,68},{5,69},{6,70},{7,71},{8,72},{9,... | collective-permute-start | bytes 1572872 | tf_op jit(solution)/shard_map/ppermute | solution.py:163
  92.5 37.4 %collective-permute-start.11 = (bf16[32,8192]{1,0:T(8,128)(2,1)}, bf16[32,8192]{1,0:T(8,128)(2,1)}, u32[]{:S(2)}, u32[]{:S(2)}) collective-permute-start(bf16[32,8192]{1,0:T(8,128)(2,1)} %get-tuple-element.16), channel_id=1, source_target_pairs={{0,96},{1,97},{2,98},{3,99},{4,100},{5,101},{6,102},{7,103},{8,104... | collective-permute-start | bytes 1572872 | tf_op jit(solution)/shard_map/ppermute | solution.py:163
  95.3 34.7 %collective-permute-start.9 = (bf16[32,8192]{1,0:T(8,128)(2,1)}, bf16[32,8192]{1,0:T(8,128)(2,1)}, u32[]{:S(2)}, u32[]{:S(2)}) collective-permute-start(bf16[32,8192]{1,0:T(8,128)(2,1)} %get-tuple-element.14), channel_id=1, source_target_pairs={{0,32},{1,33},{2,34},{3,35},{4,36},{5,37},{6,38},{7,39},{8,40},{9,... | collective-permute-start | bytes 1572872 | tf_op jit(solution)/shard_map/ppermute | solution.py:163
  119.2 8.4 %copy-start.3 = (bf16[32,2048]{1,0:T(8,128)(2,1)S(1)}, bf16[32,2048]{1,0:T(8,128)(2,1)}, u32[]{:S(2)}) copy-start(bf16[32,2048]{1,0:T(8,128)(2,1)} %copy-done.2) | copy-start | bytes 393220
  119.2 8.4 %copy-start.9 = (bf16[32,2048]{1,0:T(8,128)(2,1)S(1)}, bf16[32,2048]{1,0:T(8,128)(2,1)}, u32[]{:S(2)}) copy-start(bf16[32,2048]{1,0:T(8,128)(2,1)} %copy-done.8) | copy-start | bytes 393220
  120.0 11.6 %collective-permute-start.12 = (bf16[32,2048]{1,0:T(8,128)(2,1)}, bf16[32,2048]{1,0:T(8,128)(2,1)S(1)}, u32[]{:S(2)}, u32[]{:S(2)}) collective-permute-start(bf16[32,2048]{1,0:T(8,128)(2,1)} %get-tuple-element.20), channel_id=1, source_target_pairs={{0,32},{1,33},{2,34},{3,35},{4,36},{5,37},{6,38},{7,39},{8,40},{9,... | collective-permute-start | bytes 393224 | tf_op jit(solution)/shard_map/ppermute | solution.py:163
  122.1 9.5 %collective-permute-start.13 = (bf16[32,2048]{1,0:T(8,128)(2,1)}, bf16[32,2048]{1,0:T(8,128)(2,1)}, u32[]{:S(2)}, u32[]{:S(2)}) collective-permute-start(bf16[32,2048]{1,0:T(8,128)(2,1)} %get-tuple-element.22), channel_id=1, source_target_pairs={{0,64},{1,65},{2,66},{3,67},{4,68},{5,69},{6,70},{7,71},{8,72},{9,... | collective-permute-start | bytes 393224 | tf_op jit(solution)/shard_map/ppermute | solution.py:163
  128.0 6.9 %collective-permute-start.14 = (bf16[32,2048]{1,0:T(8,128)(2,1)}, bf16[32,2048]{1,0:T(8,128)(2,1)S(1)}, u32[]{:S(2)}, u32[]{:S(2)}) collective-permute-start(bf16[32,2048]{1,0:T(8,128)(2,1)} %get-tuple-element.21), channel_id=1, source_target_pairs={{0,96},{1,97},{2,98},{3,99},{4,100},{5,101},{6,102},{7,103},{8,104... | collective-permute-start | bytes 393224 | tf_op jit(solution)/shard_map/ppermute | solution.py:163
  136.0 9.6 %collective-permute-start.15 = (bf16[8,8192]{1,0:T(8,128)(2,1)S(1)}, bf16[8,8192]{1,0:T(8,128)(2,1)S(1)}, u32[]{:S(2)}, u32[]{:S(2)}) collective-permute-start(bf16[8,8192]{1,0:T(8,128)(2,1)S(1)} %get-tuple-element.17), channel_id=1, source_target_pairs={{0,128},{1,129},{2,130},{3,131},{4,132},{5,133},{6,134},{7,135},{8... | collective-permute-start | bytes 393224 | tf_op jit(solution)/shard_map/ppermute | solution.py:163
  138.0 7.8 %collective-permute-start.16 = (bf16[8,8192]{1,0:T(8,128)(2,1)S(1)}, bf16[8,8192]{1,0:T(8,128)(2,1)S(1)}, u32[]{:S(2)}, u32[]{:S(2)}) collective-permute-start(bf16[8,8192]{1,0:T(8,128)(2,1)S(1)} %get-tuple-element.19), channel_id=1, source_target_pairs={{0,256},{1,257},{2,258},{3,259},{4,263},{5,260},{6,261},{7,262},{8... | collective-permute-start | bytes 393224 | tf_op jit(solution)/shard_map/ppermute | solution.py:163
  141.1 7.4 %collective-permute-start.17 = (bf16[8,8192]{1,0:T(8,128)(2,1)S(1)}, bf16[8,8192]{1,0:T(8,128)(2,1)S(1)}, u32[]{:S(2)}, u32[]{:S(2)}) collective-permute-start(bf16[8,8192]{1,0:T(8,128)(2,1)S(1)} %get-tuple-element.18), channel_id=1, source_target_pairs={{0,387},{1,384},{2,385},{3,386},{4,391},{5,388},{6,389},{7,390},{8... | collective-permute-start | bytes 393224 | tf_op jit(solution)/shard_map/ppermute | solution.py:163
  148.6 28.4 %collective-permute-start.18 = (bf16[8,8192]{1,0:T(8,128)(2,1)S(1)}, bf16[8,8192]{1,0:T(8,128)(2,1)S(1)}, u32[]{:S(2)}, u32[]{:S(2)}) collective-permute-start(bf16[8,8192]{1,0:T(8,128)(2,1)S(1)} %fusion.6), channel_id=1, source_target_pairs={{0,2},{1,3},{2,0},{3,1},{4,6},{5,7},{6,4},{7,5},{8,10},{9,11},{10,... | collective-permute-start | bytes 393224 | tf_op jit(solution)/shard_map/ppermute | solution.py:163
  155.6 23.9 %collective-permute-start.19 = (bf16[8,8192]{1,0:T(8,128)(2,1)S(1)}, bf16[8,8192]{1,0:T(8,128)(2,1)S(1)}, u32[]{:S(2)}, u32[]{:S(2)}) collective-permute-start(bf16[8,8192]{1,0:T(8,128)(2,1)S(1)} %fusion.6), channel_id=1, source_target_pairs={{0,1},{1,2},{2,3},{3,0},{4,5},{5,6},{6,7},{7,4},{8,9},{9,10},{10,1... | collective-permute-start | bytes 393224 | tf_op jit(solution)/shard_map/ppermute | solution.py:163
  158.5 24.9 %collective-permute-start.20 = (bf16[8,8192]{1,0:T(8,128)(2,1)S(1)}, bf16[8,8192]{1,0:T(8,128)(2,1)S(1)}, u32[]{:S(2)}, u32[]{:S(2)}) collective-permute-start(bf16[8,8192]{1,0:T(8,128)(2,1)S(1)} %fusion.6), channel_id=1, source_target_pairs={{0,3},{1,0},{2,1},{3,2},{4,7},{5,4},{6,5},{7,6},{8,11},{9,8},{10,9... | collective-permute-start | bytes 393224 | tf_op jit(solution)/shard_map/ppermute | solution.py:163
  (9 other events, 47.0 us)
Sparse Core Ops, SparseCore 0:
  10.1 63.0 all-gather.2
  145.7 36.5 reduce-scatter.1
